TPU v7x, 32 devices: a whole 2x2x4 slice. The times are simulated.
32 devices in a mesh: tok: 4 (over y, x), col: 8 (over z, core).
Axes of the slice: x: 2, y: 2, z: 4, core: 2. Of those that a mesh axis runs over, the one named last changes fastest.
Arguments:
- activations: bfloat16 [8192, 8192], P('tok', 'col'), may hold values from -60 to 60, as said below
- weight: bfloat16 [8192, 8192], P('tok', 'col'), may hold values from -6 to 6
- keep_mask: int32 [8192, 8192], P('tok', 'col'), may hold values from 0 to 1
Outputs:
- new_weight: bfloat16 [8192, 8192], P('tok', 'col')
Inputs may be any that keep to these rules, and one draw needn't show every extreme that they name: activations of calibration tokens.
All inputs are finite; a program needn't handle non-finite values.
Results may differ from a plain program's by a relative error of at most 0.00115.
Values may be sent and summed in bfloat16 or wider, within the bound.
No kernel may reach another device: no remote copies, remote signals or barrier semaphores. Data moves between devices by JAX's collectives and lax.ppermute only.
A program may use at most 128 MiB of HBM per device.

v0:
```python
import jax
import jax.numpy as jnp
from jax import lax
from jax.sharding import PartitionSpec as P

B = 1024
ITERS = 4


def per_device(activations, weight, keep_mask):
    highest = lax.Precision.HIGHEST
    n_col = lax.axis_size("col")
    n_tok = lax.axis_size("tok")
    tok_rows = activations.shape[0]
    panel_width = B // n_col
    total_count = tok_rows * n_tok
    partial_panel = lax.dot_general(
        activations,
        lax.all_gather(activations[:, :panel_width], "col", axis=1, tiled=True),
        (((0,), (0,)), ((), ())),
        preferred_element_type=jnp.float32,
    )
    block_part = lax.psum(partial_panel[:panel_width], "tok") / total_count
    diagonal_block = lax.all_gather(block_part, "col", axis=0, tiled=True)
    identity = jnp.eye(B, dtype=jnp.float32)
    damping = 0.01 * jnp.mean(jnp.diagonal(diagonal_block))
    damped = diagonal_block + damping * identity
    frobenius = jnp.sqrt(jnp.sum(damped * damped))
    col_index = lax.axis_index("col")
    row_ids = col_index * panel_width + lax.iota(jnp.int32, panel_width)
    iterate = (row_ids[:, None] == lax.iota(jnp.int32, B)[None, :]).astype(jnp.float32) / frobenius
    for sweep in range(ITERS):
        if sweep == 0:
            whole = identity / frobenius
        else:
            whole = lax.all_gather(iterate.astype(jnp.bfloat16), "col", axis=0, tiled=True).astype(
                iterate.dtype
            )
        product = jnp.dot(iterate, damped, precision=highest)
        iterate = 2.0 * iterate - jnp.dot(product, whole, precision=highest)
    inverse = lax.all_gather(iterate, "col", axis=0, tiled=True)
    remainder = lax.psum(partial_panel[panel_width:], "tok") / total_count
    hessian_panel = jnp.concatenate([block_part, remainder], axis=0)
    pruned = jnp.where(
        keep_mask[:, :panel_width] == 0, weight[:, :panel_width], jnp.zeros((), jnp.bfloat16)
    )
    pruned_panel = lax.all_gather(pruned, "col", axis=1, tiled=True).astype(jnp.float32)
    factor_rows = jnp.dot(pruned_panel, inverse, precision=highest)
    correction = lax.dot_general(
        factor_rows, hessian_panel, (((1,), (1,)), ((), ())), precision=highest
    )
    kept = keep_mask.astype(jnp.float32)
    return (kept * (weight.astype(jnp.float32) - correction)).astype(jnp.bfloat16)


def solution(mesh):
    return jax.shard_map(
        per_device,
        mesh=mesh,
        in_specs=(P("tok", "col"), P("tok", "col"), P("tok", "col")),
        out_specs=P("tok", "col"),
        check_vma=False,
    )
```

profile of v0, /device:TPU:0, one launch (start us, length us, event | category | flops | bytes accessed | tf_op | source)
XLA Modules:
  0.0 493.3 jit_solution(1033233946870937970)
XLA Ops:
  8.5 51.0 %all-gather.10.cloned.1.call-done = bf16[2048,1024]{1,0:T(8,128)(2,1)} async-done(((bf16[2048,128]{1,0:T(8,128)(2,1)}), bf16[2048,1024]{1,0:T(8,128)(2,1)}) %all-gather.10.cloned.1.call-update) | async-done | bytes 4194320 | tf_op jit(solution)/shard_map/all_gather | solution.py:19
  59.5 7.6 %fusion.31 = f32[1024,1024]{1,0:T(8,128)S(1)} fusion(bf16[2048,1024]{1,0:T(8,128)(2,1)} %param.3, bf16[2048,1024]{1,0:T(8,128)(2,1)} %all-gather.10.cloned.1.call-done), kind=kOutput, calls=%fused_computation.42 | convolution fusion | flops 4294967296 | bytes 12582912 | tf_op jit(solution)/shard_map/dot_general | solution.py:17
  67.9 2.3 slice.23
  70.3 101.9 %all-reduce.3.cloned.1.call-done = (f32[128,1024]{1,0:T(8,128)}, f32[896,1024]{1,0:T(8,128)}) async-done(((f32[128,1024]{1,0:T(8,128)}, f32[896,1024]{1,0:T(8,128)}), (f32[128,1024]{1,0:T(8,128)}, f32[896,1024]{1,0:T(8,128)})) %all-reduce.3.cloned.1.call-update) | async-done | bytes 4194320 | tf_op jit(solution)/shard_map/psum | solution.py:23
  174.2 46.9 %all-gather.12.cloned.1.call-done = f32[1024,1024]{1,0:T(8,128)} async-done(((f32[128,1024]{1,0:T(8,128)}), f32[1024,1024]{1,0:T(8,128)}) %all-gather.12.cloned.1.call-update) | async-done | bytes 4194320 | tf_op jit(solution)/shard_map/all_gather | solution.py:24
  221.2 17.1 %gather_fusion = f32[1024]{0:T(1024)S(1)} fusion(f32[1024,1024]{1,0:T(8,128)} %all-gather.12.cloned.1.call-done, s32[1024]{0:T(1024)S(1)} %bitcast.16), kind=kCustom, calls=%fused_computation | custom fusion | bytes 16384 | tf_op jit(solution)/shard_map/jit(diagonal)/cond/branch_0_fun/gather | solution.py:26
  239.5 3.9 multiply_reduce_fusion
  244.0 4.7 fusion.16
  248.8 2.5 fusion.28
  251.3 4.7 fusion.15
  256.0 23.4 %all-gather.14.cloned.1.call-done = bf16[1024,1024]{1,0:T(8,128)(2,1)} async-done(((bf16[128,1024]{1,0:T(8,128)(2,1)}), bf16[1024,1024]{1,0:T(8,128)(2,1)}) %all-gather.14.cloned.1.call-update) | async-done | bytes 2097168 | tf_op jit(solution)/shard_map/all_gather | solution.py:36
  279.4 3.3 fusion.29
  283.0 4.7 fusion.14
  287.7 23.8 %all-gather.16.cloned.1.call-done = bf16[1024,1024]{1,0:T(8,128)(2,1)} async-done(((bf16[128,1024]{1,0:T(8,128)(2,1)}), bf16[1024,1024]{1,0:T(8,128)(2,1)}) %all-gather.16.cloned.1.call-update) | async-done | bytes 2097168 | tf_op jit(solution)/shard_map/all_gather | solution.py:36
  311.5 3.3 fusion.30
  314.9 2.3 fusion.17
  317.3 4.7 fusion.13
  322.0 21.6 %all-gather.18.cloned.1.call-done = bf16[1024,1024]{1,0:T(8,128)(2,1)} async-done(((bf16[128,1024]{1,0:T(8,128)(2,1)}), bf16[1024,1024]{1,0:T(8,128)(2,1)}) %all-gather.18.cloned.1.call-update) | async-done | bytes 2097168 | tf_op jit(solution)/shard_map/all_gather | solution.py:36
  343.6 3.4 convolution_subtract_fusion
  347.0 4.6 broadcast_multiply_fusion
  351.6 40.8 %all-gather.8.cloned.1.call-done = bf16[2048,1024]{1,0:T(8,128)(2,1)} async-done(((bf16[2048,128]{1,0:T(8,128)(2,1)}), bf16[2048,1024]{1,0:T(8,128)(2,1)}) %all-gather.8.cloned.1.call-update) | async-done | bytes 4194320 | tf_op jit(solution)/shard_map/all_gather | solution.py:47
  392.4 46.7 %all-gather.20.cloned.1.call-done = f32[1024,1024]{1,0:T(8,128)} async-done(((f32[128,1024]{1,0:T(8,128)}), f32[1024,1024]{1,0:T(8,128)}) %all-gather.20.cloned.1.call-update) | async-done | bytes 4194320 | tf_op jit(solution)/shard_map/all_gather | solution.py:41
  439.1 16.8 %fusion.32 = f32[2048,1024]{1,0:T(8,128)S(1)} fusion(bf16[2048,1024]{1,0:T(8,128)(2,1)} %all-gather.8.cloned.1.call-done, f32[1024,1024]{1,0:T(8,128)} %all-gather.20.cloned.1.call-done), kind=kOutput, calls=%fused_computation.43 | convolution fusion | flops 25769803776 | bytes 16777216 | tf_op jit(solution)/shard_map/dot_general | solution.py:48
  455.9 30.5 %multiply_convert_fusion = bf16[2048,1024]{1,0:T(8,128)(2,1)} fusion(bf16[2048,1024]{1,0:T(8,128)(2,1)S(1)} %copy-done.2, s32[2048,1024]{1,0:T(8,128)} %param.5, f32[2048,1024]{1,0:T(8,128)S(1)} %fusion.32, f32[896,1024]{1,0:T(8,128)S(1)} %copy-done, f32[128,1024]{1,0:T(8,128)S(1)} %copy-done.1), kind=kOutput, calls=%fused_computation.1 | convolution fusion | flops 25781338112 | bytes 29360128 | tf_op jit(solution)/shard_map/dot_general | solution.py:49
  (28 shorter events, 5.9 us)
Async XLA Ops:
  6.5 53.0 %all-gather.10.cloned.1.call-start = ((), (), s32[]{:S(2)}) async-start(), calls=%async_computation.1 | async-start | bytes 4718592 | tf_op jit(solution)/shard_map/all_gather | solution.py:19
  8.4 163.8 %all-reduce.3.cloned.1.call-start = ((), (), s32[]{:S(2)}) async-start(), calls=%async_computation.7 | async-start | bytes 8388608 | tf_op jit(solution)/shard_map/psum | solution.py:23
  70.2 150.9 %all-gather.12.cloned.1.call-start = ((), (), s32[]{:S(2)}) async-start(), calls=%async_computation.2 | async-start | bytes 4718592 | tf_op jit(solution)/shard_map/all_gather | solution.py:24
  174.1 105.3 %all-gather.14.cloned.1.call-start = ((), (), s32[]{:S(2)}) async-start(), calls=%async_computation.3 | async-start | bytes 2359296 | tf_op jit(solution)/shard_map/all_gather | solution.py:36
  251.3 60.2 %all-gather.16.cloned.1.call-start = ((), (), s32[]{:S(2)}) async-start(), calls=%async_computation.4 | async-start | bytes 2359296 | tf_op jit(solution)/shard_map/all_gather | solution.py:36
  282.8 60.8 %all-gather.18.cloned.1.call-start = ((), (), s32[]{:S(2)}) async-start(), calls=%async_computation.5 | async-start | bytes 2359296 | tf_op jit(solution)/shard_map/all_gather | solution.py:36
  314.9 77.5 %all-gather.8.cloned.1.call-start = ((), (), s32[]{:S(2)}) async-start(), calls=%async_computation | async-start | bytes 4718592 | tf_op jit(solution)/shard_map/all_gather | solution.py:47
  317.2 121.8 %all-gather.20.cloned.1.call-start = ((), (), s32[]{:S(2)}) async-start(), calls=%async_computation.6 | async-start | bytes 4718592 | tf_op jit(solution)/shard_map/all_gather | solution.py:41
  351.6 104.3 %copy-start.1 = (f32[128,1024]{1,0:T(8,128)S(1)}, f32[128,1024]{1,0:T(8,128)}, u32[]{:S(2)}) copy-start(f32[128,1024]{1,0:T(8,128)} %broadcast_multiply_fusion.1) | copy-start | bytes 1572868
  439.1 16.8 %copy-start = (f32[896,1024]{1,0:T(8,128)S(1)}, f32[896,1024]{1,0:T(8,128)}, u32[]{:S(2)}) copy-start(f32[896,1024]{1,0:T(8,128)} %broadcast_multiply_fusion) | copy-start | bytes 11010052
  439.1 16.8 %copy-start.2 = (bf16[2048,1024]{1,0:T(8,128)(2,1)S(1)}, bf16[2048,1024]{1,0:T(8,128)(2,1)}, u32[]{:S(2)}) copy-start(bf16[2048,1024]{1,0:T(8,128)(2,1)} %param.4) | copy-start | bytes 12582916
Sparse Core Ops, SparseCore 0:
  8.9 50.5 all-gather.9
  70.3 101.8 all-reduce.2
  174.3 46.8 all-gather.11
  251.4 27.9 all-gather.13
  282.9 28.6 all-gather.15
  315.0 28.5 all-gather.17
  345.2 47.2 all-gather.7
  394.0 45.0 all-gather.19
where the time goes:
time: 494 us; the launch traced here: 493 us
  waiting for transfers between devices  356 us (72%)
  matrix products  86.3 us (17%)
  local copies, waits for them, and re-layouts  22.1 us (4%)
  between operations  14.9 us (3%)
  other arithmetic  13.3 us (3%)
    psum x1, waiting for transfers between devices, per_device(): block_part = lax.psum(partial_panel[:panel_width], 'tok') / total_count  102 us
    all_gather x3, waiting for transfers between devices, per_device(): lax.all_gather(iterate.astype(jnp.bfloat16), 'col', axis=0, tiled=True)  68.8 us
    all_gather x1, waiting for transfers between devices, per_device(): lax.all_gather(activations[:, :panel_width], 'col', axis=1, tiled=True)  51 us
    all_gather x1, waiting for transfers between devices, per_device(): diagonal_block = lax.all_gather(block_part, 'col', axis=0, tiled=True)  46.9 us
    all_gather x1, waiting for transfers between devices, per_device(): inverse = lax.all_gather(iterate, 'col', axis=0, tiled=True)  46.7 us
    all_gather x1, waiting for transfers between devices, per_device(): lax.all_gather(pruned, 'col', axis=1, tiled=True).astype(jnp.float32)  40.8 us
    dot_general x1, matrix products, per_device(): lax.dot_general(factor_rows, hessian_panel, (((1,), (1,)), ((), ())), pre...  30.5 us
    dot_general x4, matrix products, per_device(): product = jnp.dot(iterate, damped, precision=highest)  18.8 us
  transfers between devices with their start and end apart: 8, of which 8 were waited for; matrix products, arithmetic and copies ran while one was open for 5% of the time, Pallas kernels for 0%

commit v1 on v0

v1 whole, which is shorter than its diff:
```python
import functools

import jax
import jax.numpy as jnp
from jax import lax
from jax.experimental import pallas as pl
from jax.experimental.pallas import tpu as pltpu
from jax.sharding import PartitionSpec as P

B = 1024
ITERS = 4
BF16 = jnp.bfloat16
F32 = jnp.float32
VMEM_LIMIT = 60 << 20


def shift_chip(x, n_col, step):
    return lax.ppermute(x, "col", [(i, (i + 2 * step) % n_col) for i in range(n_col)])


def swap_core(x, n_col):
    return lax.ppermute(x, "col", [(i, i ^ 1) for i in range(n_col)])


def swap_tok(x, n_tok, bit):
    return lax.ppermute(x, "tok", [(i, i ^ bit) for i in range(n_tok)])


def gather_chips(x, n_col):
    chips = n_col // 2
    steps = [1] + list(range(2, chips - 1)) + ([chips - 1] if chips > 2 else [])
    return [x] + [shift_chip(x, n_col, s) for s in steps[: chips - 1]]


def sum_tok(parts, n_tok):
    bits = [1 << k for k in range(n_tok.bit_length() - 1)]
    half = len(bits) // 2
    orders = (bits, bits[half:] + bits[:half])
    parts = list(parts)
    for k in range(len(bits)):
        got = [swap_tok(p, n_tok, order[k]) for p, order in zip(parts, orders)]
        parts = [(p.astype(F32) + g.astype(F32)).astype(BF16) for p, g in zip(parts, got)]
    return parts


def scatter_tok(parts, n_tok):
    index = lax.axis_index("tok")
    count = n_tok.bit_length() - 1
    bits = list(range(count))
    half = count // 2
    orders = (bits, bits[half:] + bits[:half])
    rows = parts[0].shape[0] // n_tok
    parts = [p.reshape((2,) * count + (rows, p.shape[1])) for p in parts]
    for k in range(count):
        sent, kept = [], []
        for p, order in zip(parts, orders):
            axis = count - 1 - order[k]
            mine = (index >> order[k]) & 1
            sent.append(lax.dynamic_slice_in_dim(p, 1 - mine, 1, axis))
            kept.append(lax.dynamic_slice_in_dim(p, mine, 1, axis))
        got = [swap_tok(s, n_tok, 1 << order[k]) for s, order in zip(sent, orders)]
        parts = [a + b for a, b in zip(kept, got)]
    return [p.reshape(rows, p.shape[-1]) for p in parts]


def gather_tok(x, n_tok):
    if n_tok != 4:
        items = [x]
        bit = 1
        while bit < n_tok:
            items = items + [swap_tok(v, n_tok, bit) for v in items]
            bit *= 2
        return items
    half = x.shape[0] // 2
    over_x, over_y = swap_tok(x, n_tok, 1), swap_tok(x, n_tok, 2)
    upper = swap_tok(over_x[:half], n_tok, 2)
    lower = swap_tok(over_y[half:], n_tok, 1)
    return [x, over_x, over_y, jnp.concatenate([upper, lower], axis=0)]


def inverse_kernel(own_ref, other_ref, v_hi_ref, v_lo_ref, scale_ref, q, v, qa, qb, vb):
    size = q.shape[0]
    half = size // 2
    tile = min(256, half)
    n_tiles = size // tile

    q[:half, :] = own_ref[...].astype(F32)
    q[half:, :half] = other_ref[:, half:].astype(F32)
    q[half:, half:] = other_ref[:, :half].astype(F32)

    def rows_of(i):
        return pl.ds(pl.multiple_of(i * tile, tile), tile)

    def eye(i):
        r = lax.broadcasted_iota(jnp.int32, (tile, size), 0) + i * tile
        return r == lax.broadcasted_iota(jnp.int32, (tile, size), 1)

    def measure(i, carry):
        squares, trace = carry
        x = q[rows_of(i), :]
        squares += jnp.sum(x * x)
        trace += jnp.sum(jnp.where(eye(i), x, 0.0))
        return squares, trace

    squares, trace = lax.fori_loop(0, n_tiles, measure, (F32(0.0), F32(0.0)))
    damping = 0.01 * trace / size
    total = squares + 2.0 * damping * trace + size * damping * damping
    scale = lax.rsqrt(jnp.full((8, 128), total, F32))
    scale_ref[...] = scale
    scale = scale[0:1, 0:1]

    def begin(i, carry):
        x = (q[rows_of(i), :] + jnp.where(eye(i), damping, 0.0)) * scale
        q[rows_of(i), :] = x
        v[rows_of(i), :] = x
        qa[rows_of(i), :] = x.astype(BF16)
        vb[rows_of(i), :] = x.astype(BF16)
        return carry

    lax.fori_loop(0, n_tiles, begin, 0)

    def first(i, carry):
        x = 2.0 * q[rows_of(i), :] - jnp.dot(qa[rows_of(i), :], qa[...], preferred_element_type=F32)
        q[rows_of(i), :] = x
        qb[rows_of(i), :] = x.astype(BF16)
        return carry

    lax.fori_loop(0, n_tiles, first, 0)
    old, new = qb, qa
    weight = 2.0
    for step in range(1, ITERS):
        last = step == ITERS - 1

        def sweep(i, carry, old=old, new=new, weight=weight, last=last):
            rows = rows_of(i)
            qs = q[rows, :]
            vs = 2.0 * v[rows, :] + weight * qs - jnp.dot(vb[rows, :], old[...], preferred_element_type=F32)
            if last:
                hi = vs.astype(BF16)
                v_hi_ref[rows, :] = hi
                v_lo_ref[rows, :] = (vs - hi.astype(F32)).astype(BF16)
            else:
                v[rows, :] = vs
                qn = 2.0 * qs - jnp.dot(old[rows, :], old[...], preferred_element_type=F32)
                q[rows, :] = qn
                new[rows, :] = qn.astype(BF16)
                vb[rows, :] = vs.astype(BF16)
            return carry

        lax.fori_loop(0, n_tiles, sweep, 0)
        old, new = new, old
        weight *= 2.0


def inverse(own, other):
    size = B
    return pl.pallas_call(
        inverse_kernel,
        out_shape=[
            jax.ShapeDtypeStruct((size, size), BF16),
            jax.ShapeDtypeStruct((size, size), BF16),
            jax.ShapeDtypeStruct((8, 128), F32),
        ],
        in_specs=[pl.BlockSpec(memory_space=pltpu.VMEM)] * 2,
        out_specs=[pl.BlockSpec(memory_space=pltpu.VMEM)] * 3,
        scratch_shapes=[
            pltpu.VMEM((size, size), F32),
            pltpu.VMEM((size, size), F32),
            pltpu.VMEM((size, size), BF16),
            pltpu.VMEM((size, size), BF16),
            pltpu.VMEM((size, size), BF16),
        ],
        compiler_params=pltpu.CompilerParams(vmem_limit_bytes=VMEM_LIMIT),
        cost_estimate=pl.CostEstimate(flops=12 * size**3, bytes_accessed=8 * size**2, transcendentals=0),
        name="inverse",
    )(own, other)


def rows_kernel(h_ref, v_hi_ref, v_lo_ref, scale_ref, out_ref):
    h = h_ref[...]
    hi = h.astype(BF16)
    lo = (h - hi.astype(F32)).astype(BF16)
    product = jnp.dot(hi, v_hi_ref[...], preferred_element_type=F32)
    product += jnp.dot(lo, v_hi_ref[...], preferred_element_type=F32)
    product += jnp.dot(hi, v_lo_ref[...], preferred_element_type=F32)
    out_ref[...] = (scale_ref[0:1, 0:1] * (2.0**ITERS * h - product)).astype(BF16)


def solve_rows(h, v_hi, v_lo, scale):
    return pl.pallas_call(
        rows_kernel,
        out_shape=jax.ShapeDtypeStruct(h.shape, BF16),
        in_specs=[pl.BlockSpec(memory_space=pltpu.VMEM)] * 4,
        out_specs=pl.BlockSpec(memory_space=pltpu.VMEM),
        compiler_params=pltpu.CompilerParams(vmem_limit_bytes=VMEM_LIMIT),
        cost_estimate=pl.CostEstimate(
            flops=6 * h.shape[0] * B * B, bytes_accessed=4 * B * B, transcendentals=0
        ),
        name="solve_rows",
    )(h, v_hi, v_lo, scale)


def update_kernel(index_ref, weight_ref, mask_ref, pruned_ref, *rest):
    *pieces, out_ref = rest
    width = out_ref.shape[1] // len(pieces)
    for m, piece in enumerate(pieces):
        if len(pieces) > 1:
            place = jnp.bitwise_xor(index_ref[0], m)
            columns = pl.ds(pl.multiple_of(place * width, width), width)
        else:
            columns = slice(None)
        fix = lax.dot_general(
            pruned_ref[...], piece[...], (((1,), (1,)), ((), ())), preferred_element_type=F32
        )
        kept = weight_ref[:, columns].astype(F32) - fix
        out_ref[:, columns] = (mask_ref[:, columns].astype(F32) * kept).astype(BF16)


def update(weight, mask, pruned, pieces):
    rows, columns = weight.shape
    tile = min(256, rows)
    index = lax.axis_index("tok").astype(jnp.int32)
    if pieces[0].shape[0] % 128:
        order = jnp.arange(len(pieces), dtype=jnp.int32) ^ index
        pieces = [jnp.take(jnp.stack(pieces), order, axis=0).reshape(columns, -1)]
    index = index.reshape(1)
    block = pl.BlockSpec((tile, columns), lambda i, *_: (i, 0))
    return pl.pallas_call(
        update_kernel,
        out_shape=jax.ShapeDtypeStruct((rows, columns), BF16),
        grid_spec=pltpu.PrefetchScalarGridSpec(
            num_scalar_prefetch=1,
            grid=(rows // tile,),
            in_specs=[block, block, pl.BlockSpec((tile, pruned.shape[1]), lambda i, *_: (i, 0))]
            + [pl.BlockSpec(memory_space=pltpu.VMEM)] * len(pieces),
            out_specs=block,
        ),
        compiler_params=pltpu.CompilerParams(vmem_limit_bytes=VMEM_LIMIT),
        cost_estimate=pl.CostEstimate(
            flops=2 * rows * columns * B, bytes_accessed=10 * rows * columns, transcendentals=0
        ),
        name="update",
    )(index, weight, mask, pruned, *pieces)


def per_device(activations, weight, keep_mask):
    n_col = lax.axis_size("col")
    n_tok = lax.axis_size("tok")
    panel_width = B // n_col

    mine = jnp.concatenate(gather_chips(activations[:, :panel_width], n_col), axis=1)
    theirs = swap_core(mine, n_col)
    contract = functools.partial(
        lax.dot_general, dimension_numbers=(((0,), (0,)), ((), ())), preferred_element_type=F32
    )
    block_parts = sum_tok([contract(mine, x).astype(BF16) for x in (mine, theirs)], n_tok)
    own_rows = jnp.concatenate(block_parts, axis=1)
    other_rows = swap_core(own_rows, n_col)
    v_hi, v_lo, scale = inverse(own_rows, other_rows)

    panel_parts = scatter_tok([contract(activations, x) for x in (mine, theirs)], n_tok)
    solved = solve_rows(jnp.concatenate(panel_parts, axis=1), v_hi, v_lo, scale)
    pieces = gather_tok(solved, n_tok)

    pruned = jnp.where(keep_mask[:, :panel_width] == 0, weight[:, :panel_width], jnp.zeros((), BF16))
    pruned_mine = jnp.concatenate(gather_chips(pruned, n_col), axis=1)
    pruned_panel = jnp.concatenate([pruned_mine, swap_core(pruned_mine, n_col)], axis=1)
    return update(weight, keep_mask, pruned_panel, pieces)


def solution(mesh):
    return jax.shard_map(
        per_device,
        mesh=mesh,
        in_specs=(P("tok", "col"), P("tok", "col"), P("tok", "col")),
        out_specs=P("tok", "col"),
        check_vma=False,
    )
```

time: 494 us -> 205 us (0.41)
  waiting for transfers between devices: 356 us -> 94 us
  matrix products: 86.3 us -> 13.1 us
  Pallas kernels: 0 us -> 41.3 us
  starting transfers between devices: 0.48 us -> 27.2 us
  between operations: 14.9 us -> 0.2 us
  local copies, waits for them, and re-layouts: 22.1 us -> 16.4 us
    all_gather x7 -> x0, waiting for transfers between devices: 254 us -> none  [the longest x3 68.8 us: per_device(): lax.all_gather(iterate.astype(jnp.bfloat16), 'col', axis=0, tiled=True)]
    psum x1 -> x0, waiting for transfers between devices: 102 us -> none  [per_device(): block_part = lax.psum(partial_panel[:panel_width], 'tok') / total_count]
    ppermute x0 -> x21, waiting for transfers between devices: none -> 94 us  [the longest x12 50.2 us: swap_tok(): return lax.ppermute(x, 'tok', [(i, i ^ bit) for i in range(n_tok)])]
    dot_general x11 -> x4, matrix products: 86.3 us -> 13.1 us  [the longest x2 8.92 us: per_device(): contract(activations, x)]
    pallas_call x0 -> x3, Pallas kernels: none -> 41.3 us  [the longest x1 22.9 us: inverse(): pl.pallas_call(inverse_kernel, out_shape=[jax.ShapeDtypeStruct((size, siz...]
    ppermute x0 -> x21, starting transfers between devices: none -> 27.2 us  [the longest x12 16.1 us: swap_tok(): return lax.ppermute(x, 'tok', [(i, i ^ bit) for i in range(n_tok)])]
    gather x1 -> x0, local copies, waits for them, and re-layouts: 17.1 us -> none  [per_device(): damping = 0.01 * jnp.mean(jnp.diagonal(diagonal_block))]
    div x2 -> x0, other arithmetic: 6.49 us -> none  [the longest x1 4.58 us: per_device(): remainder = lax.psum(partial_panel[panel_width:], 'tok') / total_count]
  transfers between devices with their start and end apart: 8 -> 21, of which waited for: 8 -> 11; matrix products, arithmetic and copies ran while one was open for 5% -> 19% of each run, Pallas kernels for 0% -> 14%
where the time goes in v1:
time: 205 us; the launch traced here: 204 us
  waiting for transfers between devices  94 us (46%)
  Pallas kernels  41.3 us (20%)
  starting transfers between devices  27.2 us (13%)
  local copies, waits for them, and re-layouts  16.4 us (8%)
  matrix products  13.1 us (6%)
  other arithmetic  11.9 us (6%)
    ppermute x12, waiting for transfers between devices, swap_tok(): return lax.ppermute(x, 'tok', [(i, i ^ bit) for i in range(n_tok)])  50.2 us
    ppermute x6, waiting for transfers between devices, shift_chip(): lax.ppermute(x, 'col', [(i, (i + 2 * step) % n_col) for i in range(n_col)])  43.8 us
    pallas_call x1, Pallas kernels, inverse(): pl.pallas_call(inverse_kernel, out_shape=[jax.ShapeDtypeStruct((size, siz...  22.9 us
    ppermute x12, starting transfers between devices, swap_tok(): return lax.ppermute(x, 'tok', [(i, i ^ bit) for i in range(n_tok)])  16.1 us
    pallas_call x1, Pallas kernels, update(): pl.pallas_call(update_kernel, out_shape=jax.ShapeDtypeStruct((rows, colum...  13.2 us
    ppermute x6, starting transfers between devices, shift_chip(): lax.ppermute(x, 'col', [(i, (i + 2 * step) % n_col) for i in range(n_col)])  10.7 us
    dot_general x2, matrix products, per_device(): contract(activations, x)  8.92 us
    pallas_call x1, Pallas kernels, solve_rows(): pl.pallas_call(rows_kernel, out_shape=jax.ShapeDtypeStruct(h.shape, BF16)...  5.21 us
  transfers between devices with their start and end apart: 21, of which 11 were waited for; matrix products, arithmetic and copies ran while one was open for 19% of the time, Pallas kernels for 14%

profile of v1, /device:TPU:0, one launch (start us, length us, event | category | flops | bytes accessed | tf_op | source)
XLA Modules:
  0.0 204.1 jit_solution(6162272340583832082)
XLA Ops:
  1.1 5.1 %collective-permute-start.6 = (bf16[2048,128]{1,0:T(8,128)(2,1)S(1)}, bf16[2048,128]{1,0:T(8,128)(2,1)S(1)}, u32[]{:S(2)}, u32[]{:S(2)}) collective-permute-start(bf16[2048,128]{1,0:T(8,128)(2,1)S(1)} %slice.17), channel_id=1, source_target_pairs={{0,6},{1,7},{2,0},{3,1},{4,2},{5,3},{6,4},{7,5},{8,14},{9,15},{10,... | collective-permute-start | bytes 1572872 | tf_op jit(solution)/shard_map/ppermute | solution.py:18
  7.2 11.3 %collective-permute-done.6 = bf16[2048,128]{1,0:T(8,128)(2,1)S(1)} collective-permute-done((bf16[2048,128]{1,0:T(8,128)(2,1)S(1)}, bf16[2048,128]{1,0:T(8,128)(2,1)S(1)}, u32[]{:S(2)}, u32[]{:S(2)}) %collective-permute-start.6) | collective-permute-done | bytes 524320 | tf_op jit(solution)/shard_map/ppermute | solution.py:18
  18.6 32.4 %collective-permute-done.5 = bf16[2048,128]{1,0:T(8,128)(2,1)S(1)} collective-permute-done((bf16[2048,128]{1,0:T(8,128)(2,1)S(1)}, bf16[2048,128]{1,0:T(8,128)(2,1)S(1)}, u32[]{:S(2)}, u32[]{:S(2)}) %collective-permute-start.5) | collective-permute-done | bytes 524320 | tf_op jit(solution)/shard_map/ppermute | solution.py:18
  51.3 2.6 %constant_dynamic-update-slice_fusion.4 = (bf16[2048,1024]{1,0:T(8,128)(2,1)}, bf16[2048,128]{1,0:T(8,128)(2,1)}) fusion(bf16[2048,1024]{1,0:T(8,128)(2,1)} %weight_ref.1, s32[2048,1024]{1,0:T(8,128)} %mask_ref.1), kind=kLoop, calls=%fused_computation.23 | loop fusion | flops 524287 | bytes 2621440
  53.9 2.8 %collective-permute-start.1 = (bf16[2048,128]{1,0:T(8,128)(2,1)}, bf16[2048,128]{1,0:T(8,128)(2,1)}, u32[]{:S(2)}, u32[]{:S(2)}) collective-permute-start(bf16[2048,128]{1,0:T(8,128)(2,1)} %get-tuple-element.12), channel_id=1, source_target_pairs={{0,4},{1,5},{2,6},{3,7},{4,0},{5,1},{6,2},{7,3},{8,12},{9,13},{10,... | collective-permute-start | bytes 1572872 | tf_op jit(solution)/shard_map/ppermute | solution.py:18
  59.5 3.7 %convolution_bitcast_fusion.1 = f32[1024,512]{0,1:T(8,128)} fusion(bf16[2048,512]{1,0:T(8,128)(2,1)S(1)} %pad_maximum_fusion.1, bf16[2048,1024]{1,0:T(8,128)(2,1)S(1)} %copy-done.4), kind=kOutput, calls=%fused_computation.3 | convolution fusion | flops 2147483648 | bytes 8388608 | tf_op jit(solution)/shard_map/dot_general | solution.py:261
  63.2 3.0 %copy.4 = f32[1024,512]{1,0:T(8,128)} copy(f32[1024,512]{0,1:T(8,128)} %convolution_bitcast_fusion.1) | data formatting | bytes 4194304 | tf_op jit(solution)/shard_map/dot_general | solution.py:261
  66.2 2.3 %constant_dynamic-slice_fusion.3 = f32[2,1,256,512]{3,2,1,0:T(8,128)} fusion(f32[2,2,256,512]{3,2,1,0:T(8,128)} %bitcast.21, s32[]{:T(128)S(6)} %select_n.22), kind=kLoop, calls=%fused_computation.27 | loop fusion | bytes 2097156 | tf_op jit(solution)/shard_map/dynamic_slice | solution.py:59
  69.3 3.6 %collective-permute-done.12 = bf16[512,512]{1,0:T(8,128)(2,1)} collective-permute-done((bf16[512,512]{1,0:T(8,128)(2,1)S(1)}, bf16[512,512]{1,0:T(8,128)(2,1)}, u32[]{:S(2)}, u32[]{:S(2)}) %collective-permute-start.12) | collective-permute-done | bytes 524320 | tf_op jit(solution)/shard_map/ppermute | solution.py:26
  75.7 2.9 %convolution_convert_fusion = bf16[512,512]{1,0:T(8,128)(2,1)S(1)} fusion(bf16[2048,512]{1,0:T(8,128)(2,1)S(1)} %pad_maximum_fusion.1, bf16[2048,512]{1,0:T(8,128)(2,1)} %collective-permute-done.9), kind=kOutput, calls=%fused_computation.4 | convolution fusion | flops 1074003968 | bytes 4718592 | tf_op jit(solution)/shard_map/dot_general | solution.py:256
  79.5 5.3 %convolution_bitcast_fusion = f32[1024,512]{0,1:T(8,128)} fusion(bf16[2048,512]{1,0:T(8,128)(2,1)} %collective-permute-done.9, bf16[2048,1024]{1,0:T(8,128)(2,1)S(1)} %copy-done.5), kind=kOutput, calls=%fused_computation.2 | convolution fusion | flops 2147483648 | bytes 8388608 | tf_op jit(solution)/shard_map/dot_general | solution.py:261
  84.7 1.9 copy.5
  86.7 11.2 %collective-permute-done.14 = bf16[512,512]{1,0:T(8,128)(2,1)} collective-permute-done((bf16[512,512]{1,0:T(8,128)(2,1)S(1)}, bf16[512,512]{1,0:T(8,128)(2,1)}, u32[]{:S(2)}, u32[]{:S(2)}) %collective-permute-start.14) | collective-permute-done | bytes 524320 | tf_op jit(solution)/shard_map/ppermute | solution.py:26
  106.7 5.3 %collective-permute-done.15 = bf16[512,512]{1,0:T(8,128)(2,1)S(1)} collective-permute-done((bf16[512,512]{1,0:T(8,128)(2,1)S(1)}, bf16[512,512]{1,0:T(8,128)(2,1)S(1)}, u32[]{:S(2)}, u32[]{:S(2)}) %collective-permute-start.15) | collective-permute-done | bytes 524320 | tf_op jit(solution)/shard_map/ppermute | solution.py:26
  112.8 11.2 %collective-permute-done.10 = f32[1,2,256,512]{3,2,1,0:T(8,128)S(1)} collective-permute-done((f32[1,2,256,512]{3,2,1,0:T(8,128)S(1)}, f32[1,2,256,512]{3,2,1,0:T(8,128)S(1)}, u32[]{:S(2)}, u32[]{:S(2)}) %collective-permute-start.10) | collective-permute-done | bytes 1048608 | tf_op jit(solution)/shard_map/ppermute | solution.py:26
  127.7 4.3 %collective-permute-done.8 = f32[1,1,256,512]{3,2,1,0:T(8,128)S(1)} collective-permute-done((f32[1,1,256,512]{3,2,1,0:T(8,128)S(1)}, f32[1,1,256,512]{3,2,1,0:T(8,128)S(1)}, u32[]{:S(2)}, u32[]{:S(2)}) %collective-permute-start.8) | collective-permute-done | bytes 524320 | tf_op jit(solution)/shard_map/ppermute | solution.py:26
  132.1 6.6 %collective-permute-done.11 = f32[1,1,256,512]{3,2,1,0:T(8,128)S(1)} collective-permute-done((f32[1,1,256,512]{3,2,1,0:T(8,128)S(1)}, f32[1,1,256,512]{3,2,1,0:T(8,128)S(1)}, u32[]{:S(2)}, u32[]{:S(2)}) %collective-permute-start.11) | collective-permute-done | bytes 524320 | tf_op jit(solution)/shard_map/ppermute | solution.py:26
  139.8 22.9 %inverse.1 = (bf16[1024,1024]{1,0:T(8,128)(2,1)}, bf16[1024,1024]{1,0:T(8,128)(2,1)}, f32[8,128]{1,0:T(8,128)}) custom-call(bf16[512,1024]{1,0:T(8,128)(2,1)} %copy-done.3, bf16[512,1024]{1,0:T(8,128)(2,1)} %collective-permute-done.16.other_ref), custom_call_target="tpu_custom_call" | custom-call | flops 12884901888 | bytes 8388608 | tf_op jit(solution)/shard_map/inverse/pallas_call | solution.py:157
  162.7 5.2 %solve_rows.1.rest_0_ = bf16[256,1024]{1,0:T(8,128)(2,1)} custom-call(f32[256,1024]{1,0:T(8,128)} %pad_maximum_fusion.2.h_ref, bf16[1024,1024]{1,0:T(8,128)(2,1)} %get-tuple-element.8.v_hi_ref, bf16[1024,1024]{1,0:T(8,128)(2,1)} %get-tuple-element.9.v_lo_ref, f32[8,128]{1,0:T(8,128)} %get-tuple-element.10.scale_ref), custom_call_target="tpu_custom_call" | custom-call | flops 1610612736 | bytes 4194304 | tf_op jit(solution)/shard_map/solve_rows/pallas_call | solution.py:190
  171.8 2.0 constant_dynamic-update-slice_fusion.2
  173.8 1.9 constant_dynamic-update-slice_fusion.1
  175.7 5.9 %collective-permute-done.18.rest_2_ = bf16[256,1024]{1,0:T(8,128)(2,1)S(1)} collective-permute-done((bf16[256,1024]{1,0:T(8,128)(2,1)}, bf16[256,1024]{1,0:T(8,128)(2,1)S(1)}, u32[]{:S(2)}, u32[]{:S(2)}) %collective-permute-start.18) | collective-permute-done | bytes 524320 | tf_op jit(solution)/shard_map/ppermute | solution.py:26
  184.8 3.1 %constant_dynamic-update-slice_fusion.pruned_ref = bf16[2048,1024]{1,0:T(8,128)(2,1)} fusion(bf16[2048,1024]{1,0:T(8,128)(2,1)} %constant_dynamic-update-slice_fusion.1, bf16[2048,512]{1,0:T(8,128)(2,1)} %collective-permute-done.3), kind=kLoop, calls=%fused_computation.19 | loop fusion | bytes 4194304 | tf_op jit(solution)/shard_map/concatenate | solution.py:267
  190.9 13.2 %update.1 = bf16[2048,1024]{1,0:T(8,128)(2,1)} custom-call(s32[1]{0:T(128)} %bitcast.index_ref, bf16[2048,1024]{1,0:T(8,128)(2,1)} %weight_ref.1, s32[2048,1024]{1,0:T(8,128)} %mask_ref.1, bf16[2048,1024]{1,0:T(8,128)(2,1)} %constant_dynamic-update-slice_fusion.pruned_ref, bf16[256,1024]{1,0:T(8,128)(2,1)} %solve_rows.1.rest_0_, ...), custom_call_target="tpu_custom_call" | custom-call | flops 4294967296 | bytes 20971520 | tf_op jit(solution)/shard_map/update/pallas_call | solution.py:228
  (64 shorter events, 34.2 us)
Async XLA Ops:
  1.1 17.5 %collective-permute-start.6 = (bf16[2048,128]{1,0:T(8,128)(2,1)S(1)}, bf16[2048,128]{1,0:T(8,128)(2,1)S(1)}, u32[]{:S(2)}, u32[]{:S(2)}) collective-permute-start(bf16[2048,128]{1,0:T(8,128)(2,1)S(1)} %slice.17), channel_id=1, source_target_pairs={{0,6},{1,7},{2,0},{3,1},{4,2},{5,3},{6,4},{7,5},{8,14},{9,15},{10,... | collective-permute-start | bytes 1572872 | tf_op jit(solution)/shard_map/ppermute | solution.py:18
  6.2 44.8 %collective-permute-start.5 = (bf16[2048,128]{1,0:T(8,128)(2,1)S(1)}, bf16[2048,128]{1,0:T(8,128)(2,1)S(1)}, u32[]{:S(2)}, u32[]{:S(2)}) collective-permute-start(bf16[2048,128]{1,0:T(8,128)(2,1)S(1)} %slice.17), channel_id=1, source_target_pairs={{0,4},{1,5},{2,6},{3,7},{4,0},{5,1},{6,2},{7,3},{8,12},{9,13},{10,... | collective-permute-start | bytes 1572872 | tf_op jit(solution)/shard_map/ppermute | solution.py:18
  6.2 44.8 %collective-permute-start.4 = (bf16[2048,128]{1,0:T(8,128)(2,1)S(1)}, bf16[2048,128]{1,0:T(8,128)(2,1)S(1)}, u32[]{:S(2)}, u32[]{:S(2)}) collective-permute-start(bf16[2048,128]{1,0:T(8,128)(2,1)S(1)} %slice.17), channel_id=1, source_target_pairs={{0,2},{1,3},{2,4},{3,5},{4,6},{5,7},{6,0},{7,1},{8,10},{9,11},{10,... | collective-permute-start | bytes 1572872 | tf_op jit(solution)/shard_map/ppermute | solution.py:18
  51.2 24.5 %collective-permute-start.9 = (bf16[2048,512]{1,0:T(8,128)(2,1)S(1)}, bf16[2048,512]{1,0:T(8,128)(2,1)}, u32[]{:S(2)}, u32[]{:S(2)}) collective-permute-start(bf16[2048,512]{1,0:T(8,128)(2,1)S(1)} %pad_maximum_fusion.1), channel_id=1, source_target_pairs={{0,1},{1,0},{2,3},{3,2},{4,5},{5,4},{6,7},{7,6},{8,9},{9,8},{10,11... | collective-permute-start | bytes 6291464 | tf_op jit(solution)/shard_map/ppermute | solution.py:22
  53.9 70.4 %collective-permute-start.2 = (bf16[2048,128]{1,0:T(8,128)(2,1)}, bf16[2048,128]{1,0:T(8,128)(2,1)}, u32[]{:S(2)}, u32[]{:S(2)}) collective-permute-start(bf16[2048,128]{1,0:T(8,128)(2,1)} %get-tuple-element.12), channel_id=1, source_target_pairs={{0,6},{1,7},{2,0},{3,1},{4,2},{5,3},{6,4},{7,5},{8,14},{9,15},{10,... | collective-permute-start | bytes 1572872 | tf_op jit(solution)/shard_map/ppermute | solution.py:18
  53.9 72.0 %collective-permute-start.1 = (bf16[2048,128]{1,0:T(8,128)(2,1)}, bf16[2048,128]{1,0:T(8,128)(2,1)}, u32[]{:S(2)}, u32[]{:S(2)}) collective-permute-start(bf16[2048,128]{1,0:T(8,128)(2,1)} %get-tuple-element.12), channel_id=1, source_target_pairs={{0,4},{1,5},{2,6},{3,7},{4,0},{5,1},{6,2},{7,3},{8,12},{9,13},{10,... | collective-permute-start | bytes 1572872 | tf_op jit(solution)/shard_map/ppermute | solution.py:18
  58.0 15.0 %collective-permute-start.12 = (bf16[512,512]{1,0:T(8,128)(2,1)S(1)}, bf16[512,512]{1,0:T(8,128)(2,1)}, u32[]{:S(2)}, u32[]{:S(2)}) collective-permute-start(bf16[512,512]{1,0:T(8,128)(2,1)S(1)} %convolution_convert_fusion.1), channel_id=1, source_target_pairs={{0,8},{8,0},{16,24},{24,16},{1,9},{9,1},{17,25},{25,17},{2,10},{10... | collective-permute-start | bytes 1572872 | tf_op jit(solution)/shard_map/ppermute | solution.py:26
  68.5 32.2 %collective-permute-start.7 = (f32[2,1,256,512]{3,2,1,0:T(8,128)}, f32[2,1,256,512]{3,2,1,0:T(8,128)}, u32[]{:S(2)}, u32[]{:S(2)}) collective-permute-start(f32[2,1,256,512]{3,2,1,0:T(8,128)} %constant_dynamic-slice_fusion.3), channel_id=1, source_target_pairs={{0,8},{8,0},{16,24},{24,16},{1,9},{9,1},{17,25},{25,17},{2,10},{10... | collective-permute-start | bytes 3145736 | tf_op jit(solution)/shard_map/ppermute | solution.py:26
  74.1 29.6 %collective-permute-start.13 = (bf16[512,512]{1,0:T(8,128)(2,1)S(1)}, bf16[512,512]{1,0:T(8,128)(2,1)}, u32[]{:S(2)}, u32[]{:S(2)}) collective-permute-start(bf16[512,512]{1,0:T(8,128)(2,1)S(1)} %add_convert_fusion.3), channel_id=1, source_target_pairs={{0,16},{8,24},{16,0},{24,8},{1,17},{9,25},{17,1},{25,9},{2,18},{10... | collective-permute-start | bytes 1572872 | tf_op jit(solution)/shard_map/ppermute | solution.py:26
  78.6 19.4 %collective-permute-start.14 = (bf16[512,512]{1,0:T(8,128)(2,1)S(1)}, bf16[512,512]{1,0:T(8,128)(2,1)}, u32[]{:S(2)}, u32[]{:S(2)}) collective-permute-start(bf16[512,512]{1,0:T(8,128)(2,1)S(1)} %convolution_convert_fusion), channel_id=1, source_target_pairs={{0,16},{8,24},{16,0},{24,8},{1,17},{9,25},{17,1},{25,9},{2,18},{10... | collective-permute-start | bytes 1572872 | tf_op jit(solution)/shard_map/ppermute | solution.py:26
  86.6 15.6 %copy-start = (f32[1024,512]{1,0:T(8,128)S(1)}, f32[1024,512]{1,0:T(8,128)}, u32[]{:S(2)}) copy-start(f32[1024,512]{1,0:T(8,128)} %copy.4) | copy-start | bytes 6291460
  98.0 26.0 %collective-permute-start.10 = (f32[1,2,256,512]{3,2,1,0:T(8,128)S(1)}, f32[1,2,256,512]{3,2,1,0:T(8,128)S(1)}, u32[]{:S(2)}, u32[]{:S(2)}) collective-permute-start(f32[1,2,256,512]{3,2,1,0:T(8,128)S(1)} %constant_dynamic-slice_fusion.1), channel_id=1, source_target_pairs={{0,16},{8,24},{16,0},{24,8},{1,17},{9,25},{17,1},{25,9},{2,18},{10... | collective-permute-start | bytes 3145736 | tf_op jit(solution)/shard_map/ppermute | solution.py:26
  100.7 11.4 %collective-permute-start.15 = (bf16[512,512]{1,0:T(8,128)(2,1)S(1)}, bf16[512,512]{1,0:T(8,128)(2,1)S(1)}, u32[]{:S(2)}, u32[]{:S(2)}) collective-permute-start(bf16[512,512]{1,0:T(8,128)(2,1)S(1)} %add_convert_fusion.1), channel_id=1, source_target_pairs={{0,8},{8,0},{16,24},{24,16},{1,9},{9,1},{17,25},{25,17},{2,10},{10... | collective-permute-start | bytes 1572872 | tf_op jit(solution)/shard_map/ppermute | solution.py:26
  103.7 22.1 %collective-permute-start = (bf16[2048,128]{1,0:T(8,128)(2,1)}, bf16[2048,128]{1,0:T(8,128)(2,1)S(1)}, u32[]{:S(2)}, u32[]{:S(2)}) collective-permute-start(bf16[2048,128]{1,0:T(8,128)(2,1)} %get-tuple-element.12), channel_id=1, source_target_pairs={{0,2},{1,3},{2,4},{3,5},{4,6},{5,7},{6,0},{7,1},{8,10},{9,11},{10,... | collective-permute-start | bytes 1572872 | tf_op jit(solution)/shard_map/ppermute | solution.py:18
  112.1 20.0 %collective-permute-start.8 = (f32[1,1,256,512]{3,2,1,0:T(8,128)S(1)}, f32[1,1,256,512]{3,2,1,0:T(8,128)S(1)}, u32[]{:S(2)}, u32[]{:S(2)}) collective-permute-start(f32[1,1,256,512]{3,2,1,0:T(8,128)S(1)} %constant_dynamic-slice_fusion.2), channel_id=1, source_target_pairs={{0,16},{8,24},{16,0},{24,8},{1,17},{9,25},{17,1},{25,9},{2,18},{10... | collective-permute-start | bytes 1572872 | tf_op jit(solution)/shard_map/ppermute | solution.py:26
  112.8 11.5 %copy-start.3 = (bf16[512,1024]{1,0:T(8,128)(2,1)}, bf16[512,1024]{1,0:T(8,128)(2,1)S(1)}, u32[]{:S(2)}) copy-start(bf16[512,1024]{1,0:T(8,128)(2,1)S(1)} %pad_maximum_fusion.3.own_ref) | copy-start | bytes 3145732
  124.0 15.8 %collective-permute-start.16 = (bf16[512,1024]{1,0:T(8,128)(2,1)S(1)}, bf16[512,1024]{1,0:T(8,128)(2,1)}, u32[]{:S(2)}, u32[]{:S(2)}) collective-permute-start(bf16[512,1024]{1,0:T(8,128)(2,1)S(1)} %pad_maximum_fusion.3.own_ref), channel_id=1, source_target_pairs={{0,1},{1,0},{2,3},{3,2},{4,5},{5,4},{6,7},{7,6},{8,9},{9,8},{10,11... | collective-permute-start | bytes 3145736 | tf_op jit(solution)/shard_map/ppermute | solution.py:22
  124.3 14.4 %collective-permute-start.11 = (f32[1,1,256,512]{3,2,1,0:T(8,128)S(1)}, f32[1,1,256,512]{3,2,1,0:T(8,128)S(1)}, u32[]{:S(2)}, u32[]{:S(2)}) collective-permute-start(f32[1,1,256,512]{3,2,1,0:T(8,128)S(1)} %constant_dynamic-slice_fusion), channel_id=1, source_target_pairs={{0,8},{8,0},{16,24},{24,16},{1,9},{9,1},{17,25},{25,17},{2,10},{10... | collective-permute-start | bytes 1572872 | tf_op jit(solution)/shard_map/ppermute | solution.py:26
  127.4 57.3 %collective-permute-start.3 = (bf16[2048,512]{1,0:T(8,128)(2,1)S(1)}, bf16[2048,512]{1,0:T(8,128)(2,1)}, u32[]{:S(2)}, u32[]{:S(2)}) collective-permute-start(bf16[2048,512]{1,0:T(8,128)(2,1)S(1)} %pad_maximum_fusion), channel_id=1, source_target_pairs={{0,1},{1,0},{2,3},{3,2},{4,5},{5,4},{6,7},{7,6},{8,9},{9,8},{10,11... | collective-permute-start | bytes 6291464 | tf_op jit(solution)/shard_map/ppermute | solution.py:22
  167.9 13.7 %collective-permute-start.18 = (bf16[256,1024]{1,0:T(8,128)(2,1)}, bf16[256,1024]{1,0:T(8,128)(2,1)S(1)}, u32[]{:S(2)}, u32[]{:S(2)}) collective-permute-start(bf16[256,1024]{1,0:T(8,128)(2,1)} %solve_rows.1.rest_0_), channel_id=1, source_target_pairs={{0,16},{8,24},{16,0},{24,8},{1,17},{9,25},{17,1},{25,9},{2,18},{10... | collective-permute-start | bytes 1572872 | tf_op jit(solution)/shard_map/ppermute | solution.py:26
  169.4 13.8 %collective-permute-start.17 = (bf16[256,1024]{1,0:T(8,128)(2,1)}, bf16[256,1024]{1,0:T(8,128)(2,1)S(1)}, u32[]{:S(2)}, u32[]{:S(2)}) collective-permute-start(bf16[256,1024]{1,0:T(8,128)(2,1)} %solve_rows.1.rest_0_), channel_id=1, source_target_pairs={{0,8},{8,0},{16,24},{24,16},{1,9},{9,1},{17,25},{25,17},{2,10},{10... | collective-permute-start | bytes 1572872 | tf_op jit(solution)/shard_map/ppermute | solution.py:26
  181.6 6.3 %copy-start.1 = (bf16[256,1024]{1,0:T(8,128)(2,1)}, bf16[256,1024]{1,0:T(8,128)(2,1)S(1)}, u32[]{:S(2)}) copy-start(bf16[256,1024]{1,0:T(8,128)(2,1)S(1)} %collective-permute-done.18.rest_2_) | copy-start | bytes 1572868
  181.6 7.1 %collective-permute-start.20 = (bf16[128,1024]{1,0:T(8,128)(2,1)S(1)}, bf16[128,1024]{1,0:T(8,128)(2,1)S(1)}, u32[]{:S(2)}, u32[]{:S(2)}) collective-permute-start(bf16[128,1024]{1,0:T(8,128)(2,1)S(1)} %slice.21), channel_id=1, source_target_pairs={{0,8},{8,0},{16,24},{24,16},{1,9},{9,1},{17,25},{25,17},{2,10},{10... | collective-permute-start | bytes 786440 | tf_op jit(solution)/shard_map/ppermute | solution.py:26
  183.2 6.8 %collective-permute-start.19 = (bf16[128,1024]{1,0:T(8,128)(2,1)S(1)}, bf16[128,1024]{1,0:T(8,128)(2,1)S(1)}, u32[]{:S(2)}, u32[]{:S(2)}) collective-permute-start(bf16[128,1024]{1,0:T(8,128)(2,1)S(1)} %slice.20), channel_id=1, source_target_pairs={{0,16},{8,24},{16,0},{24,8},{1,17},{9,25},{17,1},{25,9},{2,18},{10... | collective-permute-start | bytes 786440 | tf_op jit(solution)/shard_map/ppermute | solution.py:26
  (3 other events, 12.9 us)

commit v2 on v1

v2 whole, which is shorter than its diff:
```python
import functools

import jax
import jax.numpy as jnp
from jax import lax
from jax.experimental import pallas as pl
from jax.experimental.pallas import tpu as pltpu
from jax.sharding import PartitionSpec as P


B = 1024
ITERS = 4
BF16 = jnp.bfloat16
F32 = jnp.float32


def shift_chip(x, n_col, step):
    return lax.ppermute(x, "col", [(i, (i + 2 * step) % n_col) for i in range(n_col)])


def swap_core(x, n_col):
    return lax.ppermute(x, "col", [(i, i ^ 1) for i in range(n_col)])


def swap_tok(x, n_tok, bit):
    return lax.ppermute(x, "tok", [(i, i ^ bit) for i in range(n_tok)])


TRANSPOSED = (((0,), (0,)), ((), ()))


def after(x, *others):
    return lax.optimization_barrier((x, *others))[0]


def joined(xs):
    return xs[0] if len(xs) == 1 else jnp.concatenate(xs, axis=1)


def block_kernel(rows, *refs):
    *panels, out_ref = refs
    column = 0
    for shard in rows:
        left = panels[2 * shard][...].T
        width = left.shape[0]
        for before in range(shard + 1):
            right = jnp.concatenate([panels[2 * before][...], panels[2 * before + 1][...]], axis=1)
            product = jnp.dot(left, right, preferred_element_type=F32)
            out_ref[:, column : column + 2 * width] = product.astype(BF16)
            column += 2 * width


def block_rows(panels, rows):
    width = panels[0].shape[1]
    count = sum(shard + 1 for shard in rows)
    return pl.pallas_call(
        functools.partial(block_kernel, rows),
        out_shape=jax.ShapeDtypeStruct((width, 2 * width * count), BF16),
        in_specs=[pl.BlockSpec(memory_space=pltpu.VMEM)] * len(panels),
        out_specs=pl.BlockSpec(memory_space=pltpu.VMEM),
        compiler_params=pltpu.CompilerParams(vmem_limit_bytes=16 << 20),
        cost_estimate=pl.CostEstimate(
            flops=4 * width * width * count * panels[0].shape[0],
            bytes_accessed=2 * len(panels) * panels[0].size,
            transcendentals=0,
        ),
        name="block_rows",
    )(*panels)


def panel_kernel(runs, index_ref, *refs):
    *panels, activations_ref, sent_ref, kept_ref = refs
    left = joined([ref[...] for ref in panels]).T
    sent, kept = runs
    width = kept_ref.shape[1] // len(kept)
    for out_ref, run in ((sent_ref, sent), (kept_ref, kept)):
        for place, m in enumerate(run):
            start = pl.multiple_of(jnp.bitwise_xor(index_ref[0], m) * width, width)
            product = jnp.dot(left, activations_ref[:, pl.ds(start, width)], preferred_element_type=F32)
            out_ref[:, place * width : (place + 1) * width] = product


def panel_products(*arguments):
    *panels, activations, bits = arguments
    kept = [0]
    for bit in reversed(bits[1:]):
        kept = kept + [m | bit for m in kept]
    sent = [m | bits[0] for m in kept]
    columns = activations.shape[1]
    width = columns // (2 * len(kept))
    index = lax.axis_index("tok").astype(jnp.int32)
    if width % 128:
        product = lax.dot_general(
            joined(panels), activations, TRANSPOSED, preferred_element_type=F32
        )
        runs = product.reshape(-1, 2 * len(kept), width)
        return [
            jnp.take(runs, jnp.array(run, jnp.int32) ^ index, axis=1).reshape(len(product), -1)
            for run in (sent, kept)
        ]
    height = sum(panel.shape[1] for panel in panels)
    shape = jax.ShapeDtypeStruct((height, width * len(kept)), F32)
    return pl.pallas_call(
        functools.partial(panel_kernel, (sent, kept)),
        out_shape=[shape, shape],
        in_specs=[pl.BlockSpec(memory_space=pltpu.SMEM)]
        + [pl.BlockSpec(memory_space=pltpu.VMEM)] * (len(panels) + 1),
        out_specs=[pl.BlockSpec(memory_space=pltpu.VMEM)] * 2,
        compiler_params=pltpu.CompilerParams(vmem_limit_bytes=16 << 20),
        cost_estimate=pl.CostEstimate(
            flops=2 * panels[0].shape[0] * height * columns, bytes_accessed=2 * activations.size, transcendentals=0
        ),
        name="panel_products",
    )(index.reshape(1), *panels, activations)


def scatter_tok(sent, kept, n_tok, bits):
    addends = [kept, swap_tok(sent, n_tok, bits[0])]
    width = kept.shape[1]
    for bit in bits[1:]:
        width //= 2
        total = addends[0][:, width : 2 * width]
        for x in addends[1:]:
            total = total + x[:, width : 2 * width]
        addends.append(swap_tok(total, n_tok, bit))
    return addends


def add_rounded(x, y):
    return (x.astype(F32) + y.astype(F32)).astype(BF16)


def sum_tok(x, n_tok, bits):
    for bit in bits:
        x = add_rounded(x, swap_tok(x, n_tok, bit))
    return x


def gather_tok(x, n_tok):
    if n_tok != 4:
        items = [x]
        bit = 1
        while bit < n_tok:
            items = items + [swap_tok(v, n_tok, bit) for v in items]
            bit *= 2
        return items
    half = x.shape[0] // 2
    over_x, over_y = swap_tok(x, n_tok, 1), swap_tok(x, n_tok, 2)
    upper = swap_tok(over_x[:half], n_tok, 2)
    lower = swap_tok(over_y[half:], n_tok, 1)
    return [x, over_x, over_y, jnp.concatenate([upper, lower], axis=0)]


def inverse_kernel(width, count, *refs):
    own, other = refs[:count], refs[count : 2 * count]
    v_hi_ref, v_lo_ref, scale_ref, q, v, qa, qb, vb = refs[2 * count :]
    size = q.shape[0]
    tile = 256 if size % 256 == 0 else size

    triangle = ((shard, before) for shard in range(size) for before in range(shard + 1))
    for mine, theirs in zip(own, other):
        for part in range(mine.shape[1] // (2 * width)):
            x = mine[:, part * 2 * width : (part + 1) * 2 * width].astype(F32)
            y = theirs[:, part * 2 * width : (part + 1) * 2 * width].astype(F32)
            y = jnp.concatenate([y[:, width:], y[:, :width]], axis=1)
            shard, before = next(triangle)
            rows = slice(2 * width * shard, 2 * width * (shard + 1))
            columns = slice(2 * width * before, 2 * width * (before + 1))
            x = jnp.concatenate([x, y], axis=0)
            q[rows, columns] = x
            if before < shard:
                q[columns, rows] = x.T

    squares, trace = F32(0.0), F32(0.0)
    eye = lax.broadcasted_iota(jnp.int32, (tile, tile), 0) == lax.broadcasted_iota(jnp.int32, (tile, tile), 1)
    spans = [slice(i, i + tile) for i in range(0, size, tile)]
    for rows in spans:
        x = q[rows, :]
        squares += jnp.sum(x * x)
        trace += jnp.sum(jnp.where(eye, q[rows, rows], 0.0))
    damping = 0.01 * trace / size
    total = squares + 2.0 * damping * trace + size * damping * damping
    scale = lax.rsqrt(jnp.full((8, 128), total, F32))
    scale_ref[...] = scale
    scale = scale[0:1, 0:1]
    for rows in spans:
        q[rows, rows] += jnp.where(eye, damping, 0.0)
        x = q[rows, :] * scale
        q[rows, :] = x
        v[rows, :] = x
        qa[rows, :] = x.astype(BF16)
        vb[rows, :] = x.astype(BF16)

    def put(ref, rows, part):
        ref[rows, : rows.stop] = part
        if rows.start:
            ref[: rows.start, rows] = part[:, : rows.start].T

    for rows in spans:
        n = rows.stop
        x = 2.0 * q[rows, :n] - jnp.dot(qa[rows, :], qa[:, :n], preferred_element_type=F32)
        q[rows, :n] = x
        put(qb, rows, x.astype(BF16))
    old, new = qb, qa
    weight = 2.0
    for step in range(1, ITERS):
        last = step == ITERS - 1
        for rows in spans:
            n = rows.stop
            qs = q[rows, :n]
            vs = 2.0 * v[rows, :n] + weight * qs
            vs = vs - jnp.dot(vb[rows, :], old[:, :n], preferred_element_type=F32)
            v[rows, :n] = vs
            if last:
                hi = vs.astype(BF16)
                put(v_hi_ref, rows, hi)
                put(v_lo_ref, rows, (vs - hi.astype(F32)).astype(BF16))
            else:
                qn = 2.0 * qs - jnp.dot(old[rows, :], old[:, :n], preferred_element_type=F32)
                q[rows, :n] = qn
                put(new, rows, qn.astype(BF16))
        if not last:
            for rows in spans:
                put(vb, rows, v[rows, : rows.stop].astype(BF16))
        old, new = new, old
        weight *= 2.0


def inverse(own, other):
    width = own[0].shape[0]
    size = B
    return pl.pallas_call(
        functools.partial(inverse_kernel, width, len(own)),
        out_shape=[
            jax.ShapeDtypeStruct((size, size), BF16),
            jax.ShapeDtypeStruct((size, size), BF16),
            jax.ShapeDtypeStruct((8, 128), F32),
        ],
        in_specs=[pl.BlockSpec(memory_space=pltpu.VMEM)] * (2 * len(own)),
        out_specs=[pl.BlockSpec(memory_space=pltpu.VMEM)] * 3,
        scratch_shapes=[
            pltpu.VMEM((size, size), F32),
            pltpu.VMEM((size, size), F32),
            pltpu.VMEM((size, size), BF16),
            pltpu.VMEM((size, size), BF16),
            pltpu.VMEM((size, size), BF16),
        ],
        compiler_params=pltpu.CompilerParams(vmem_limit_bytes=32 << 20),
        cost_estimate=pl.CostEstimate(flops=12 * size**3, bytes_accessed=8 * size**2, transcendentals=0),
        name="inverse",
    )(*own, *other)


def rows_kernel(counts, *refs):
    *h_refs, v_hi_ref, v_lo_ref, scale_ref, out_ref = refs
    width = out_ref.shape[1]
    parts = []
    for count in counts:
        addends, h_refs = h_refs[:count], h_refs[count:]
        total = addends[0][:, :width]
        for ref in addends[1:]:
            total = total + ref[:, :width]
        parts.append(total)
    h = jnp.concatenate(parts, axis=0)
    hi = h.astype(BF16)
    lo = (h - hi.astype(F32)).astype(BF16)
    times = functools.partial(jnp.dot, preferred_element_type=F32)
    product = times(v_hi_ref[...], hi) + times(v_hi_ref[...], lo) + times(v_lo_ref[...], hi)
    out_ref[...] = (scale_ref[0:1, 0:1] * (2.0**ITERS * h - product)).astype(BF16)


def solve_rows(parts, v_hi, v_lo, scale):
    width = parts[0][-1].shape[1]
    flat = [x for part in parts for x in part]
    return pl.pallas_call(
        functools.partial(rows_kernel, tuple(len(part) for part in parts)),
        out_shape=jax.ShapeDtypeStruct((v_hi.shape[0], width), BF16),
        in_specs=[pl.BlockSpec(memory_space=pltpu.VMEM)] * (len(flat) + 3),
        out_specs=pl.BlockSpec(memory_space=pltpu.VMEM),
        compiler_params=pltpu.CompilerParams(vmem_limit_bytes=24 << 20),
        cost_estimate=pl.CostEstimate(flops=6 * width * B * B, bytes_accessed=4 * B * B, transcendentals=0),
        name="solve_rows",
    )(*flat, v_hi, v_lo, scale)


def pruned_kernel(weight_ref, mask_ref, out_ref):
    out_ref[...] = jnp.where(mask_ref[...] == 0, weight_ref[...], jnp.zeros((), BF16))


def pruned_columns(weight, mask, width):
    if width % 128:
        return jnp.where(mask[:, :width] == 0, weight[:, :width], jnp.zeros((), BF16))
    block = pl.BlockSpec((weight.shape[0], width), lambda i: (0, 0))
    return pl.pallas_call(
        pruned_kernel,
        out_shape=jax.ShapeDtypeStruct((weight.shape[0], width), BF16),
        grid=(1,),
        in_specs=[block, block],
        out_specs=block,
        compiler_params=pltpu.CompilerParams(vmem_limit_bytes=8 << 20),
        cost_estimate=pl.CostEstimate(flops=0, bytes_accessed=8 * weight.shape[0] * width, transcendentals=0),
        name="pruned_columns",
    )(weight, mask)


def update_kernel(index_ref, weight_ref, mask_ref, pruned_ref, *rest):
    *pieces, out_ref = rest
    width = out_ref.shape[1] // len(pieces)
    for m, piece in enumerate(pieces):
        if len(pieces) > 1:
            place = jnp.bitwise_xor(index_ref[0], m)
            columns = pl.ds(pl.multiple_of(place * width, width), width)
        else:
            columns = slice(None)
        fix = jnp.dot(pruned_ref[...], piece[...], preferred_element_type=F32)
        kept = weight_ref[:, columns].astype(F32) - fix
        out_ref[:, columns] = (mask_ref[:, columns].astype(F32) * kept).astype(BF16)


def update(weight, mask, pruned, pieces):
    rows, columns = weight.shape
    tile = min(512, rows)
    index = lax.axis_index("tok").astype(jnp.int32)
    if pieces[0].shape[1] % 128:
        order = jnp.arange(len(pieces), dtype=jnp.int32) ^ index
        pieces = jnp.take(jnp.stack(pieces), order, axis=0)
        pieces = [jnp.moveaxis(pieces, 0, 1).reshape(pieces.shape[1], columns)]
    index = index.reshape(1)
    block = pl.BlockSpec((tile, columns), lambda i, *_: (i, 0))
    return pl.pallas_call(
        update_kernel,
        out_shape=jax.ShapeDtypeStruct((rows, columns), BF16),
        grid_spec=pltpu.PrefetchScalarGridSpec(
            num_scalar_prefetch=1,
            grid=(rows // tile,),
            in_specs=[block, block, pl.BlockSpec((tile, pruned.shape[1]), lambda i, *_: (i, 0))]
            + [pl.BlockSpec(memory_space=pltpu.VMEM)] * len(pieces),
            out_specs=block,
        ),
        compiler_params=pltpu.CompilerParams(vmem_limit_bytes=32 << 20),
        cost_estimate=pl.CostEstimate(
            flops=2 * rows * columns * B, bytes_accessed=10 * rows * columns, transcendentals=0
        ),
        name="update",
    )(index, weight, mask, pruned, *pieces)


def gather_and_sum(activations, n_col, n_tok, bits, turned):
    chips = n_col // 2
    own = activations[:, : B // n_col]
    panels, sums, parts = [], [], []
    for k in range(chips):
        mine = own if k == 0 else shift_chip(own, n_col, k)
        panels += [mine, swap_core(mine, n_col)]
        order = turned if k % 2 else bits
        if k:
            rows = (0, 1) if k == 1 else (k,)
            sums.append(sum_tok(block_rows(panels, rows), n_tok, order))
        parts.append(scatter_tok(*panel_products(*panels[-2:], activations, order), n_tok, order))
    return sums, [swap_core(x, n_col) for x in sums], parts, mine


def gather_and_sum_4(activations, n_col, n_tok, bits, turned):
    x, y = bits
    own = activations[:, : B // n_col]

    def swapped(array):
        return swap_core(array, n_col)

    def over(array, bit):
        return swap_tok(array, n_tok, bit)

    def added(a, b):
        return add_rounded(a, b)

    def second_step(kept, arrived, bit):
        width = kept.shape[1] // 2
        total = kept[:, width:] + arrived[:, width:]
        return [kept, arrived, over(total, bit)]

    first = shift_chip(own, n_col, 1)
    second = shift_chip(first, n_col, 1)
    third = shift_chip(own, n_col, -1)
    panels = [own, swapped(own)]
    sent, kept = panel_products(*panels, activations, bits)
    part_0 = second_step(kept, over(sent, x), y)

    panels += [first, swapped(first)]
    rows_1 = block_rows(panels, (0, 1))
    total_1 = added(rows_1, over(rows_1, x))
    sum_1 = added(total_1, over(total_1, y))
    sent, kept = panel_products(panels[2], activations, bits)
    part_1 = second_step(kept, over(sent, x), y)
    sent, kept = panel_products(panels[3], activations, turned)
    part_2 = second_step(kept, over(sent, y), x)

    panels += [second, swapped(second), third, swapped(third)]
    rows_3 = block_rows(panels, (2, 3))
    middle = rows_3.shape[1] // 2
    left, right = rows_3[:, :middle], rows_3[:, middle:]
    left = added(left, over(left, x))
    right = added(right, over(right, y))
    sum_3 = [added(left, over(left, y)), added(right, over(right, x))]
    sum_3 = jnp.concatenate(sum_3, axis=1)
    sent, kept = panel_products(*panels[4:6], after(activations, rows_3), bits)
    part_3 = second_step(kept, over(sent, x), y)
    sent, kept = panel_products(*panels[6:], after(activations, rows_3), turned)
    part_4 = second_step(kept, over(sent, y), x)

    sums = [sum_1, sum_3]
    others = [swapped(v) for v in sums]
    return sums, others, [part_0, part_1, part_2, part_3, part_4], rows_3


def per_device(activations, weight, keep_mask):
    n_col = lax.axis_size("col")
    n_tok = lax.axis_size("tok")
    panel_width = B // n_col
    chips = n_col // 2
    bits = [1 << k for k in range(n_tok.bit_length() - 1)]
    turned = bits[len(bits) // 2 :] + bits[: len(bits) // 2]

    gather = gather_and_sum_4 if (chips, n_tok) == (4, 4) else gather_and_sum
    sums, others, parts, _ = gather(activations, n_col, n_tok, bits, turned)
    v_hi, v_lo, scale = inverse(sums, others)
    solved = solve_rows(parts, v_hi, v_lo, scale)
    pieces = gather_tok(solved, n_tok)

    pruned = pruned_columns(weight, keep_mask, panel_width)
    steps = [1, 2, -1] if chips == 4 else range(1, chips)
    pruned = [pruned] + [shift_chip(pruned, n_col, s) for s in steps]
    pruned_panel = jnp.concatenate([x for a in pruned for x in (a, swap_core(a, n_col))], axis=1)
    return update(weight, keep_mask, pruned_panel, pieces)


def solution(mesh):
    return jax.shard_map(
        per_device,
        mesh=mesh,
        in_specs=(P("tok", "col"), P("tok", "col"), P("tok", "col")),
        out_specs=P("tok", "col"),
        check_vma=False,
    )
```

time: 205 us -> 175 us (0.85)
  the two profiles are of different devices: /device:TPU:0 before, /device:TPU:18 now
where the time goes in v2:
time: 175 us
  waiting for transfers between devices  106 us (61%)
  starting transfers between devices  30.6 us (17%)
  Pallas kernels  26.3 us (15%)
  local copies, waits for them, and re-layouts  11.3 us (6%)
    ppermute x20, waiting for transfers between devices, swap_tok(): return lax.ppermute(x, 'tok', [(i, i ^ bit) for i in range(n_tok)])  56.3 us
    ppermute x6, waiting for transfers between devices, shift_chip(): lax.ppermute(x, 'col', [(i, (i + 2 * step) % n_col) for i in range(n_col)])  49.1 us
    ppermute x20, starting transfers between devices, swap_tok(): return lax.ppermute(x, 'tok', [(i, i ^ bit) for i in range(n_tok)])  20 us
    unnamed x21, local copies, waits for them, and re-layouts  10 us
    pallas_call x1, Pallas kernels, inverse(): pl.pallas_call(functools.partial(inverse_kernel, width, len(own)), out_sh...  9.83 us
    ppermute x6, starting transfers between devices, shift_chip(): lax.ppermute(x, 'col', [(i, (i + 2 * step) % n_col) for i in range(n_col)])  8.62 us
    pallas_call x1, Pallas kernels, update(): pl.pallas_call(update_kernel, out_shape=jax.ShapeDtypeStruct((rows, colum...  6.88 us
    pallas_call x5, Pallas kernels, panel_products(): pl.pallas_call(functools.partial(panel_kernel, (sent, kept)), out_shape=[...  5.42 us
  transfers between devices with their start and end apart: 36, of which 12 were waited for; matrix products, arithmetic and copies ran while one was open for 2% of the time, Pallas kernels for 11%

profile of v2, /device:TPU:18, one launch (start us, length us, event | category | flops | bytes accessed | tf_op | source)
XLA Modules:
  0.0 174.7 jit_solution(6349256442133935412)
XLA Ops:
  1.1 1.6 collective-permute-start.10
  2.7 3.4 %copy-done.2 = s32[2048,1024]{1,0:T(8,128)S(1)} copy-done((s32[2048,1024]{1,0:T(8,128)S(1)}, s32[2048,1024]{1,0:T(8,128)}, u32[]{:S(2)}) %copy-start.2) | copy-done | bytes 8388632
  6.1 2.2 %copy-done.3 = bf16[2048,1024]{1,0:T(8,128)(2,1)S(1)} copy-done((bf16[2048,1024]{1,0:T(8,128)(2,1)S(1)}, bf16[2048,1024]{1,0:T(8,128)(2,1)}, u32[]{:S(2)}) %copy-start.3) | copy-done | bytes 4194328
  9.4 1.6 collective-permute-start.1
  11.1 16.0 %collective-permute-done.10.refs_0_.refs_2_ = bf16[2048,128]{1,0:T(8,128)(2,1)S(1)} collective-permute-done((bf16[2048,128]{1,0:T(8,128)(2,1)S(1)}, bf16[2048,128]{1,0:T(8,128)(2,1)S(1)}, u32[]{:S(2)}, u32[]{:S(2)}) %collective-permute-start.10) | collective-permute-done | bytes 524320 | tf_op jit(solution)/shard_map/ppermute | solution.py:18
  27.2 2.2 %copy-done = bf16[2048,1024]{1,0:T(8,128)(2,1)S(1)} copy-done((bf16[2048,1024]{1,0:T(8,128)(2,1)S(1)}, bf16[2048,1024]{1,0:T(8,128)(2,1)}, u32[]{:S(2)}) %copy-start) | copy-done | bytes 4194328
  30.7 1.6 collective-permute-start.16
  34.9 3.5 %collective-permute-done.1 = bf16[2048,128]{1,0:T(8,128)(2,1)S(1)} collective-permute-done((bf16[2048,128]{1,0:T(8,128)(2,1)S(1)}, bf16[2048,128]{1,0:T(8,128)(2,1)S(1)}, u32[]{:S(2)}, u32[]{:S(2)}) %collective-permute-start.1) | collective-permute-done | bytes 524320 | tf_op jit(solution)/shard_map/ppermute | solution.py:18
  39.1 2.0 %collective-permute-start.3 = (bf16[2048,128]{1,0:T(8,128)(2,1)S(1)}, bf16[2048,128]{1,0:T(8,128)(2,1)S(1)}, u32[]{:S(2)}, u32[]{:S(2)}) collective-permute-start(bf16[2048,128]{1,0:T(8,128)(2,1)S(1)} %pruned_columns.1), channel_id=1, source_target_pairs={{0,4},{1,5},{2,6},{3,7},{4,0},{5,1},{6,2},{7,3},{8,12},{9,13},{10,... | collective-permute-start | bytes 1572872 | tf_op jit(solution)/shard_map/ppermute | solution.py:18
  42.5 29.6 %collective-permute-done.16.refs_4_.refs_0_ = bf16[2048,128]{1,0:T(8,128)(2,1)S(1)} collective-permute-done((bf16[2048,128]{1,0:T(8,128)(2,1)S(1)}, bf16[2048,128]{1,0:T(8,128)(2,1)S(1)}, u32[]{:S(2)}, u32[]{:S(2)}) %collective-permute-start.16) | collective-permute-done | bytes 524320 | tf_op jit(solution)/shard_map/ppermute | solution.py:18
  74.7 6.3 %collective-permute-done.24 = bf16[128,768]{1,0:T(8,128)(2,1)S(1)} collective-permute-done((bf16[128,768]{1,0:T(8,128)(2,1)S(1)}, bf16[128,768]{1,0:T(8,128)(2,1)S(1)}, u32[]{:S(2)}, u32[]{:S(2)}) %collective-permute-start.24) | collective-permute-done | bytes 196640 | tf_op jit(solution)/shard_map/ppermute | solution.py:26
  85.0 6.1 %collective-permute-done.14.refs_7_ = f32[128,512]{1,0:T(8,128)S(1)} collective-permute-done((f32[128,512]{1,0:T(8,128)S(1)}, f32[128,512]{1,0:T(8,128)S(1)}, u32[]{:S(2)}, u32[]{:S(2)}) %collective-permute-start.14) | collective-permute-done | bytes 262176 | tf_op jit(solution)/shard_map/ppermute | solution.py:26
  93.2 6.3 %collective-permute-done.28 = bf16[128,896]{1,0:T(8,128)(2,1)S(1)} collective-permute-done((bf16[128,896]{1,0:T(8,128)(2,1)S(1)}, bf16[128,896]{1,0:T(8,128)(2,1)S(1)}, u32[]{:S(2)}, u32[]{:S(2)}) %collective-permute-start.28) | collective-permute-done | bytes 229408 | tf_op jit(solution)/shard_map/ppermute | solution.py:26
  99.7 1.6 collective-permute-start.27
  101.3 2.3 %collective-permute-done.25 = bf16[128,768]{1,0:T(8,128)(2,1)S(1)} collective-permute-done((bf16[128,768]{1,0:T(8,128)(2,1)S(1)}, bf16[128,768]{1,0:T(8,128)(2,1)S(1)}, u32[]{:S(2)}, u32[]{:S(2)}) %collective-permute-start.25) | collective-permute-done | bytes 196640 | tf_op jit(solution)/shard_map/ppermute | solution.py:26
  106.8 1.6 collective-permute-start.29
  108.4 10.3 %collective-permute-done.29 = bf16[128,896]{1,0:T(8,128)(2,1)S(1)} collective-permute-done((bf16[128,896]{1,0:T(8,128)(2,1)S(1)}, bf16[128,896]{1,0:T(8,128)(2,1)S(1)}, u32[]{:S(2)}, u32[]{:S(2)}) %collective-permute-start.29) | collective-permute-done | bytes 229408 | tf_op jit(solution)/shard_map/ppermute | solution.py:26
  120.5 7.4 %collective-permute-done.22.refs_13_ = f32[256,512]{1,0:T(8,128)S(1)} collective-permute-done((f32[256,512]{1,0:T(8,128)S(1)}, f32[256,512]{1,0:T(8,128)S(1)}, u32[]{:S(2)}, u32[]{:S(2)}) %collective-permute-start.22) | collective-permute-done | bytes 524320 | tf_op jit(solution)/shard_map/ppermute | solution.py:26
  132.6 9.8 %inverse.1 = (bf16[1024,1024]{1,0:T(8,128)(2,1)S(1)}, bf16[1024,1024]{1,0:T(8,128)(2,1)S(1)}, f32[8,128]{1,0:T(8,128)S(1)}) custom-call(bf16[128,768]{1,0:T(8,128)(2,1)S(1)} %add_convert_fusion.4.refs_0_, bf16[128,1792]{1,0:T(8,128)(2,1)S(1)} %pad_maximum_fusion.1.refs_1_, bf16[128,768]{1,0:T(8,128)(2,1)S(1)} %collective-permute-done.30.refs_2_, ...), custom_call_target="tpu_custom_call" | custom-call | flops 12884901888 | bytes 8388608 | tf_op jit(solution)/shard_map/inverse/pallas_call | solution.py:232
  143.0 1.9 %solve_rows.1.rest_0_ = bf16[1024,256]{1,0:T(8,128)(2,1)S(1)} custom-call(f32[256,512]{1,0:T(8,128)S(1)} %get-tuple-element.19.refs_0_, f32[256,512]{1,0:T(8,128)S(1)} %collective-permute-done.8.refs_1_, f32[256,256]{1,0:T(8,128)S(1)} %collective-permute-done.9.refs_2_, f32[128,512]{1,0:T(8,128)S(1)} %get-tuple-element.21.refs_3_, ...), custom_call_target="tpu_custom_call" | custom-call | flops 1610612736 | bytes 4194304 | tf_op jit(solution)/shard_map/solve_rows/pallas_call | solution.py:275
  147.6 11.3 %collective-permute-done.32.rest_1_ = bf16[1024,256]{1,0:T(8,128)(2,1)S(1)} collective-permute-done((bf16[1024,256]{1,0:T(8,128)(2,1)S(1)}, bf16[1024,256]{1,0:T(8,128)(2,1)S(1)}, u32[]{:S(2)}, u32[]{:S(2)}) %collective-permute-start.32) | collective-permute-done | bytes 524320 | tf_op jit(solution)/shard_map/ppermute | solution.py:26
  158.9 1.6 collective-permute-start.34
  161.5 5.0 %collective-permute-done.34 = bf16[512,256]{1,0:T(8,128)(2,1)S(1)} collective-permute-done((bf16[512,256]{1,0:T(8,128)(2,1)S(1)}, bf16[512,256]{1,0:T(8,128)(2,1)S(1)}, u32[]{:S(2)}, u32[]{:S(2)}) %collective-permute-start.34) | collective-permute-done | bytes 262176 | tf_op jit(solution)/shard_map/ppermute | solution.py:26
  167.9 6.9 %update.1 = bf16[2048,1024]{1,0:T(8,128)(2,1)} custom-call(s32[1]{0:T(128)} %bitcast.index_ref, bf16[2048,1024]{1,0:T(8,128)(2,1)S(1)} %copy-done.4, s32[2048,1024]{1,0:T(8,128)S(1)} %bitcast.2, bf16[2048,1024]{1,0:T(8,128)(2,1)S(1)} %constant_dynamic-update-slice_fusion.pruned_ref, bf16[1024,256]{1,0:T(8,128)(2,1)S(1)} %solve_rows.1.rest_0_, ...), custom_call_target="tpu_custom_call" | custom-call | flops 4294967296 | bytes 20971520 | tf_op jit(solution)/shard_map/update/pallas_call | solution.py:330
  (98 shorter events, 32.3 us)
Async XLA Ops:
  1.1 26.1 %collective-permute-start.10 = (bf16[2048,128]{1,0:T(8,128)(2,1)S(1)}, bf16[2048,128]{1,0:T(8,128)(2,1)S(1)}, u32[]{:S(2)}, u32[]{:S(2)}) collective-permute-start(bf16[2048,128]{1,0:T(8,128)(2,1)S(1)} %slice.45.refs_0_), channel_id=1, source_target_pairs={{0,2},{1,3},{2,4},{3,5},{4,6},{5,7},{6,0},{7,1},{8,10},{9,11},{10,... | collective-permute-start | bytes 1572872 | tf_op jit(solution)/shard_map/ppermute | solution.py:18
  8.7 22.0 %collective-permute-start = (bf16[2048,128]{1,0:T(8,128)(2,1)S(1)}, bf16[2048,128]{1,0:T(8,128)(2,1)}, u32[]{:S(2)}, u32[]{:S(2)}) collective-permute-start(bf16[2048,128]{1,0:T(8,128)(2,1)S(1)} %pruned_columns.1), channel_id=1, source_target_pairs={{0,1},{1,0},{2,3},{3,2},{4,5},{5,4},{6,7},{7,6},{8,9},{9,8},{10,11... | collective-permute-start | bytes 1572872 | tf_op jit(solution)/shard_map/ppermute | solution.py:22
  8.7 32.4 %collective-permute-start.18 = (bf16[2048,128]{1,0:T(8,128)(2,1)S(1)}, bf16[2048,128]{1,0:T(8,128)(2,1)S(1)}, u32[]{:S(2)}, u32[]{:S(2)}) collective-permute-start(bf16[2048,128]{1,0:T(8,128)(2,1)S(1)} %slice.45.refs_0_), channel_id=1, source_target_pairs={{0,6},{1,7},{2,0},{3,1},{4,2},{5,3},{6,4},{7,5},{8,14},{9,15},{10,... | collective-permute-start | bytes 1572872 | tf_op jit(solution)/shard_map/ppermute | solution.py:18
  9.2 24.3 %collective-permute-start.7 = (bf16[2048,128]{1,0:T(8,128)(2,1)S(1)}, bf16[2048,128]{1,0:T(8,128)(2,1)S(1)}, u32[]{:S(2)}, u32[]{:S(2)}) collective-permute-start(bf16[2048,128]{1,0:T(8,128)(2,1)S(1)} %slice.45.refs_0_), channel_id=1, source_target_pairs={{0,1},{1,0},{2,3},{3,2},{4,5},{5,4},{6,7},{7,6},{8,9},{9,8},{10,11... | collective-permute-start | bytes 1572872 | tf_op jit(solution)/shard_map/ppermute | solution.py:22
  9.4 29.0 %collective-permute-start.1 = (bf16[2048,128]{1,0:T(8,128)(2,1)S(1)}, bf16[2048,128]{1,0:T(8,128)(2,1)S(1)}, u32[]{:S(2)}, u32[]{:S(2)}) collective-permute-start(bf16[2048,128]{1,0:T(8,128)(2,1)S(1)} %pruned_columns.1), channel_id=1, source_target_pairs={{0,2},{1,3},{2,4},{3,5},{4,6},{5,7},{6,0},{7,1},{8,10},{9,11},{10,... | collective-permute-start | bytes 1572872 | tf_op jit(solution)/shard_map/ppermute | solution.py:18
  30.7 41.4 %collective-permute-start.16 = (bf16[2048,128]{1,0:T(8,128)(2,1)S(1)}, bf16[2048,128]{1,0:T(8,128)(2,1)S(1)}, u32[]{:S(2)}, u32[]{:S(2)}) collective-permute-start(bf16[2048,128]{1,0:T(8,128)(2,1)S(1)} %collective-permute-done.10.refs_0_.refs_2_), channel_id=1, source_target_pairs={{0,2},{1,3},{2,4},{3,5},{4,6},{5,7},{6,0},{7,1},{8,10},{9,11},{10,... | collective-permute-start | bytes 1572872 | tf_op jit(solution)/shard_map/ppermute | solution.py:18
  33.5 38.6 %collective-permute-start.13 = (bf16[2048,128]{1,0:T(8,128)(2,1)S(1)}, bf16[2048,128]{1,0:T(8,128)(2,1)S(1)}, u32[]{:S(2)}, u32[]{:S(2)}) collective-permute-start(bf16[2048,128]{1,0:T(8,128)(2,1)S(1)} %collective-permute-done.10.refs_0_.refs_2_), channel_id=1, source_target_pairs={{0,1},{1,0},{2,3},{3,2},{4,5},{5,4},{6,7},{7,6},{8,9},{9,8},{10,11... | collective-permute-start | bytes 1572872 | tf_op jit(solution)/shard_map/ppermute | solution.py:22
  38.4 35.6 %collective-permute-start.8 = (f32[256,512]{1,0:T(8,128)S(1)}, f32[256,512]{1,0:T(8,128)S(1)}, u32[]{:S(2)}, u32[]{:S(2)}) collective-permute-start(f32[256,512]{1,0:T(8,128)S(1)} %get-tuple-element.20), channel_id=1, source_target_pairs={{0,8},{8,0},{16,24},{24,16},{1,9},{9,1},{17,25},{25,17},{2,10},{10... | collective-permute-start | bytes 1572872 | tf_op jit(solution)/shard_map/ppermute | solution.py:26
  39.1 88.8 %collective-permute-start.3 = (bf16[2048,128]{1,0:T(8,128)(2,1)S(1)}, bf16[2048,128]{1,0:T(8,128)(2,1)S(1)}, u32[]{:S(2)}, u32[]{:S(2)}) collective-permute-start(bf16[2048,128]{1,0:T(8,128)(2,1)S(1)} %pruned_columns.1), channel_id=1, source_target_pairs={{0,4},{1,5},{2,6},{3,7},{4,0},{5,1},{6,2},{7,3},{8,12},{9,13},{10,... | collective-permute-start | bytes 1572872 | tf_op jit(solution)/shard_map/ppermute | solution.py:18
  41.2 87.3 %collective-permute-start.5 = (bf16[2048,128]{1,0:T(8,128)(2,1)S(1)}, bf16[2048,128]{1,0:T(8,128)(2,1)S(1)}, u32[]{:S(2)}, u32[]{:S(2)}) collective-permute-start(bf16[2048,128]{1,0:T(8,128)(2,1)S(1)} %pruned_columns.1), channel_id=1, source_target_pairs={{0,6},{1,7},{2,0},{3,1},{4,2},{5,3},{6,4},{7,5},{8,14},{9,15},{10,... | collective-permute-start | bytes 1572872 | tf_op jit(solution)/shard_map/ppermute | solution.py:18
  72.1 11.0 %collective-permute-start.17 = (bf16[2048,128]{1,0:T(8,128)(2,1)S(1)}, bf16[2048,128]{1,0:T(8,128)(2,1)S(1)}, u32[]{:S(2)}, u32[]{:S(2)}) collective-permute-start(bf16[2048,128]{1,0:T(8,128)(2,1)S(1)} %collective-permute-done.16.refs_4_.refs_0_), channel_id=1, source_target_pairs={{0,1},{1,0},{2,3},{3,2},{4,5},{5,4},{6,7},{7,6},{8,9},{9,8},{10,11... | collective-permute-start | bytes 1572872 | tf_op jit(solution)/shard_map/ppermute | solution.py:22
  80.9 49.1 %collective-permute-start.12 = (f32[128,256]{1,0:T(8,128)S(1)}, f32[128,256]{1,0:T(8,128)S(1)}, u32[]{:S(2)}, u32[]{:S(2)}) collective-permute-start(f32[128,256]{1,0:T(8,128)S(1)} %slice_add_fusion.4), channel_id=1, source_target_pairs={{0,16},{8,24},{16,0},{24,8},{1,17},{9,25},{17,1},{25,9},{2,18},{10... | collective-permute-start | bytes 393224 | tf_op jit(solution)/shard_map/ppermute | solution.py:26
  92.6 10.9 %collective-permute-start.25 = (bf16[128,768]{1,0:T(8,128)(2,1)S(1)}, bf16[128,768]{1,0:T(8,128)(2,1)S(1)}, u32[]{:S(2)}, u32[]{:S(2)}) collective-permute-start(bf16[128,768]{1,0:T(8,128)(2,1)S(1)} %add_convert_fusion.5), channel_id=1, source_target_pairs={{0,16},{8,24},{16,0},{24,8},{1,17},{9,25},{17,1},{25,9},{2,18},{10... | collective-permute-start | bytes 589832 | tf_op jit(solution)/shard_map/ppermute | solution.py:26
  104.9 15.4 %collective-permute-start.20 = (f32[256,512]{1,0:T(8,128)S(1)}, f32[256,512]{1,0:T(8,128)S(1)}, u32[]{:S(2)}, u32[]{:S(2)}) collective-permute-start(f32[256,512]{1,0:T(8,128)S(1)} %get-tuple-element.27), channel_id=1, source_target_pairs={{0,8},{8,0},{16,24},{24,16},{1,9},{9,1},{17,25},{25,17},{2,10},{10... | collective-permute-start | bytes 1572872 | tf_op jit(solution)/shard_map/ppermute | solution.py:26
  106.8 11.9 %collective-permute-start.29 = (bf16[128,896]{1,0:T(8,128)(2,1)S(1)}, bf16[128,896]{1,0:T(8,128)(2,1)S(1)}, u32[]{:S(2)}, u32[]{:S(2)}) collective-permute-start(bf16[128,896]{1,0:T(8,128)(2,1)S(1)} %get-tuple-element.34), channel_id=1, source_target_pairs={{0,8},{8,0},{16,24},{24,16},{1,9},{9,1},{17,25},{25,17},{2,10},{10... | collective-permute-start | bytes 688136 | tf_op jit(solution)/shard_map/ppermute | solution.py:26
  120.3 10.7 %collective-permute-start.31 = (bf16[128,1792]{1,0:T(8,128)(2,1)S(1)}, bf16[128,1792]{1,0:T(8,128)(2,1)S(1)}, u32[]{:S(2)}, u32[]{:S(2)}) collective-permute-start(bf16[128,1792]{1,0:T(8,128)(2,1)S(1)} %pad_maximum_fusion.1.refs_1_), channel_id=1, source_target_pairs={{0,1},{1,0},{2,3},{3,2},{4,5},{5,4},{6,7},{7,6},{8,9},{9,8},{10,11... | collective-permute-start | bytes 1376264 | tf_op jit(solution)/shard_map/ppermute | solution.py:22
  127.9 19.1 %collective-permute-start.2 = (bf16[2048,128]{1,0:T(8,128)(2,1)S(1)}, bf16[2048,128]{1,0:T(8,128)(2,1)S(1)}, u32[]{:S(2)}, u32[]{:S(2)}) collective-permute-start(bf16[2048,128]{1,0:T(8,128)(2,1)S(1)} %collective-permute-done.1), channel_id=1, source_target_pairs={{0,1},{1,0},{2,3},{3,2},{4,5},{5,4},{6,7},{7,6},{8,9},{9,8},{10,11... | collective-permute-start | bytes 1572872 | tf_op jit(solution)/shard_map/ppermute | solution.py:22
  128.5 13.9 %collective-permute-start.9 = (f32[256,256]{1,0:T(8,128)S(1)}, f32[256,256]{1,0:T(8,128)S(1)}, u32[]{:S(2)}, u32[]{:S(2)}) collective-permute-start(f32[256,256]{1,0:T(8,128)S(1)} %slice_add_fusion.2), channel_id=1, source_target_pairs={{0,16},{8,24},{16,0},{24,8},{1,17},{9,25},{17,1},{25,9},{2,18},{10... | collective-permute-start | bytes 786440 | tf_op jit(solution)/shard_map/ppermute | solution.py:26
  130.1 12.5 %collective-permute-start.15 = (f32[128,256]{1,0:T(8,128)S(1)}, f32[128,256]{1,0:T(8,128)S(1)}, u32[]{:S(2)}, u32[]{:S(2)}) collective-permute-start(f32[128,256]{1,0:T(8,128)S(1)} %slice_add_fusion.3), channel_id=1, source_target_pairs={{0,8},{8,0},{16,24},{24,16},{1,9},{9,1},{17,25},{25,17},{2,10},{10... | collective-permute-start | bytes 393224 | tf_op jit(solution)/shard_map/ppermute | solution.py:26
  130.5 12.5 %collective-permute-start.21 = (f32[256,256]{1,0:T(8,128)S(1)}, f32[256,256]{1,0:T(8,128)S(1)}, u32[]{:S(2)}, u32[]{:S(2)}) collective-permute-start(f32[256,256]{1,0:T(8,128)S(1)} %slice_add_fusion.1), channel_id=1, source_target_pairs={{0,16},{8,24},{16,0},{24,8},{1,17},{9,25},{17,1},{25,9},{2,18},{10... | collective-permute-start | bytes 786440 | tf_op jit(solution)/shard_map/ppermute | solution.py:26
  131.1 12.0 %collective-permute-start.23 = (f32[256,256]{1,0:T(8,128)S(1)}, f32[256,256]{1,0:T(8,128)S(1)}, u32[]{:S(2)}, u32[]{:S(2)}) collective-permute-start(f32[256,256]{1,0:T(8,128)S(1)} %slice_add_fusion), channel_id=1, source_target_pairs={{0,8},{8,0},{16,24},{24,16},{1,9},{9,1},{17,25},{25,17},{2,10},{10... | collective-permute-start | bytes 786440 | tf_op jit(solution)/shard_map/ppermute | solution.py:26
  142.5 18.8 %collective-permute-start.6 = (bf16[2048,128]{1,0:T(8,128)(2,1)S(1)}, bf16[2048,128]{1,0:T(8,128)(2,1)S(1)}, u32[]{:S(2)}, u32[]{:S(2)}) collective-permute-start(bf16[2048,128]{1,0:T(8,128)(2,1)S(1)} %collective-permute-done.5), channel_id=1, source_target_pairs={{0,1},{1,0},{2,3},{3,2},{4,5},{5,4},{6,7},{7,6},{8,9},{9,8},{10,11... | collective-permute-start | bytes 1572872 | tf_op jit(solution)/shard_map/ppermute | solution.py:22
  144.9 14.0 %collective-permute-start.32 = (bf16[1024,256]{1,0:T(8,128)(2,1)S(1)}, bf16[1024,256]{1,0:T(8,128)(2,1)S(1)}, u32[]{:S(2)}, u32[]{:S(2)}) collective-permute-start(bf16[1024,256]{1,0:T(8,128)(2,1)S(1)} %solve_rows.1.rest_0_), channel_id=1, source_target_pairs={{0,8},{8,0},{16,24},{24,16},{1,9},{9,1},{17,25},{25,17},{2,10},{10... | collective-permute-start | bytes 1572872 | tf_op jit(solution)/shard_map/ppermute | solution.py:26
  145.5 15.0 %collective-permute-start.33 = (bf16[1024,256]{1,0:T(8,128)(2,1)S(1)}, bf16[1024,256]{1,0:T(8,128)(2,1)S(1)}, u32[]{:S(2)}, u32[]{:S(2)}) collective-permute-start(bf16[1024,256]{1,0:T(8,128)(2,1)S(1)} %solve_rows.1.rest_0_), channel_id=1, source_target_pairs={{0,16},{8,24},{16,0},{24,8},{1,17},{9,25},{17,1},{25,9},{2,18},{10... | collective-permute-start | bytes 1572872 | tf_op jit(solution)/shard_map/ppermute | solution.py:26
  (19 other events, 174.7 us)

commit v3 on v2

--- a/solution.py
+++ b/solution.py
@@ -69,49 +69,50 @@
 
 
 def panel_kernel(runs, index_ref, *refs):
-    *panels, activations_ref, sent_ref, kept_ref = refs
+    outs = refs[-len(runs) :]
+    *panels, activations_ref = refs[: -len(runs)]
     left = joined([ref[...] for ref in panels]).T
-    sent, kept = runs
-    width = kept_ref.shape[1] // len(kept)
-    for out_ref, run in ((sent_ref, sent), (kept_ref, kept)):
+    width = outs[0].shape[1] // len(runs[0])
+    for out_ref, run in zip(outs, runs):
         for place, m in enumerate(run):
             start = pl.multiple_of(jnp.bitwise_xor(index_ref[0], m) * width, width)
             product = jnp.dot(left, activations_ref[:, pl.ds(start, width)], preferred_element_type=F32)
             out_ref[:, place * width : (place + 1) * width] = product
 
 
-def panel_products(*arguments):
-    *panels, activations, bits = arguments
+def panel_products(panels, activations, runs):
+    columns = activations.shape[1]
+    width = columns // sum(len(run) for run in runs)
+    index = lax.axis_index("tok").astype(jnp.int32)
+    if width % 128:
+        product = lax.dot_general(joined(panels), activations, TRANSPOSED, preferred_element_type=F32)
+        pieces = product.reshape(product.shape[0], -1, width)
+        return [
+            jnp.take(pieces, jnp.array(run, jnp.int32) ^ index, axis=1).reshape(product.shape[0], -1)
+            for run in runs
+        ]
+    height = sum(panel.shape[1] for panel in panels)
+    return pl.pallas_call(
+        functools.partial(panel_kernel, runs),
+        out_shape=[jax.ShapeDtypeStruct((height, width * len(run)), F32) for run in runs],
+        in_specs=[pl.BlockSpec(memory_space=pltpu.SMEM)]
+        + [pl.BlockSpec(memory_space=pltpu.VMEM)] * (len(panels) + 1),
+        out_specs=[pl.BlockSpec(memory_space=pltpu.VMEM)] * len(runs),
+        compiler_params=pltpu.CompilerParams(vmem_limit_bytes=16 << 20),
+        cost_estimate=pl.CostEstimate(
+            flops=2 * panels[0].shape[0] * height * columns,
+            bytes_accessed=2 * activations.size,
+            transcendentals=0,
+        ),
+        name="panel_products",
+    )(index.reshape(1), *panels, activations)
+
+
+def halving(bits):
     kept = [0]
     for bit in reversed(bits[1:]):
         kept = kept + [m | bit for m in kept]
-    sent = [m | bits[0] for m in kept]
-    columns = activations.shape[1]
-    width = columns // (2 * len(kept))
-    index = lax.axis_index("tok").astype(jnp.int32)
-    if width % 128:
-        product = lax.dot_general(
-            joined(panels), activations, TRANSPOSED, preferred_element_type=F32
-        )
-        runs = product.reshape(-1, 2 * len(kept), width)
-        return [
-            jnp.take(runs, jnp.array(run, jnp.int32) ^ index, axis=1).reshape(len(product), -1)
-            for run in (sent, kept)
-        ]
-    height = sum(panel.shape[1] for panel in panels)
-    shape = jax.ShapeDtypeStruct((height, width * len(kept)), F32)
-    return pl.pallas_call(
-        functools.partial(panel_kernel, (sent, kept)),
-        out_shape=[shape, shape],
-        in_specs=[pl.BlockSpec(memory_space=pltpu.SMEM)]
-        + [pl.BlockSpec(memory_space=pltpu.VMEM)] * (len(panels) + 1),
-        out_specs=[pl.BlockSpec(memory_space=pltpu.VMEM)] * 2,
-        compiler_params=pltpu.CompilerParams(vmem_limit_bytes=16 << 20),
-        cost_estimate=pl.CostEstimate(
-            flops=2 * panels[0].shape[0] * height * columns, bytes_accessed=2 * activations.size, transcendentals=0
-        ),
-        name="panel_products",
-    )(index.reshape(1), *panels, activations)
+    return [m | bits[0] for m in kept], kept
 
 
 def scatter_tok(sent, kept, n_tok, bits):
@@ -245,7 +246,7 @@
             pltpu.VMEM((size, size), BF16),
             pltpu.VMEM((size, size), BF16),
         ],
-        compiler_params=pltpu.CompilerParams(vmem_limit_bytes=32 << 20),
+        compiler_params=pltpu.CompilerParams(vmem_limit_bytes=24 << 20),
         cost_estimate=pl.CostEstimate(flops=12 * size**3, bytes_accessed=8 * size**2, transcendentals=0),
         name="inverse",
     )(*own, *other)
@@ -283,66 +284,91 @@
     )(*flat, v_hi, v_lo, scale)
 
 
-def pruned_kernel(weight_ref, mask_ref, out_ref):
-    out_ref[...] = jnp.where(mask_ref[...] == 0, weight_ref[...], jnp.zeros((), BF16))
+def pruned_kernel(weight_ref, mask_ref, pruned_ref, kept_ref):
+    kept = mask_ref[...].astype(F32).astype(BF16)
+    kept_ref[...] = kept
+    width = weight_ref.shape[1]
+    pruned_ref[...] = jnp.where(mask_ref[:, :width] == 0, weight_ref[...], jnp.zeros((), BF16))
 
 
 def pruned_columns(weight, mask, width):
     if width % 128:
-        return jnp.where(mask[:, :width] == 0, weight[:, :width], jnp.zeros((), BF16))
-    block = pl.BlockSpec((weight.shape[0], width), lambda i: (0, 0))
+        return jnp.where(mask[:, :width] == 0, weight[:, :width], jnp.zeros((), BF16)), mask.astype(BF16)
+    rows, columns = weight.shape
+    tile = min(512, rows)
+    narrow = pl.BlockSpec((tile, width), lambda i: (i, 0))
+    wide = pl.BlockSpec((tile, columns), lambda i: (i, 0))
     return pl.pallas_call(
         pruned_kernel,
-        out_shape=jax.ShapeDtypeStruct((weight.shape[0], width), BF16),
-        grid=(1,),
-        in_specs=[block, block],
-        out_specs=block,
-        compiler_params=pltpu.CompilerParams(vmem_limit_bytes=8 << 20),
-        cost_estimate=pl.CostEstimate(flops=0, bytes_accessed=8 * weight.shape[0] * width, transcendentals=0),
+        out_shape=[
+            jax.ShapeDtypeStruct((rows, width), BF16),
+            jax.ShapeDtypeStruct((rows, columns), BF16),
+        ],
+        grid=(rows // tile,),
+        in_specs=[narrow, wide],
+        out_specs=[narrow, wide],
+        compiler_params=pltpu.CompilerParams(vmem_limit_bytes=12 << 20),
+        cost_estimate=pl.CostEstimate(flops=0, bytes_accessed=6 * weight.size, transcendentals=0),
         name="pruned_columns",
     )(weight, mask)
 
 
-def update_kernel(index_ref, weight_ref, mask_ref, pruned_ref, *rest):
-    *pieces, out_ref = rest
-    width = out_ref.shape[1] // len(pieces)
-    for m, piece in enumerate(pieces):
-        if len(pieces) > 1:
-            place = jnp.bitwise_xor(index_ref[0], m)
-            columns = pl.ds(pl.multiple_of(place * width, width), width)
-        else:
-            columns = slice(None)
-        fix = jnp.dot(pruned_ref[...], piece[...], preferred_element_type=F32)
-        kept = weight_ref[:, columns].astype(F32) - fix
-        out_ref[:, columns] = (mask_ref[:, columns].astype(F32) * kept).astype(BF16)
-
-
-def update(weight, mask, pruned, pieces):
+def update_kernel(runs, index_ref, weight_ref, mask_ref, pruned_ref, *rest):
+    pieces = rest[: len(runs)]
+    out_ref, stage, sems = rest[-3:]
+    rows = weight_ref.shape[0]
+    _, tile, width = stage.shape
+    copies = []
+    for i in range(0, rows, tile):
+        for m, piece in zip(runs, pieces):
+            slot = len(copies)
+            place = (slice(i, i + tile), pl.ds(pl.multiple_of((index_ref[0] ^ m) * width, width), width))
+            fix = jnp.dot(pruned_ref[i : i + tile, :], piece[...], preferred_element_type=F32)
+            kept = weight_ref[place].astype(F32) - fix
+            stage[slot] = (mask_ref[place].astype(F32) * kept).astype(BF16)
+            copy = pltpu.make_async_copy(stage.at[slot], out_ref.at[place], sems.at[slot])
+            copy.start()
+            copies.append(copy)
+    for copy in copies:
+        copy.wait()
+
+
+def update(weight, mask, pruned, pieces, runs, result=None):
     rows, columns = weight.shape
+    width = pieces[0].shape[1]
     tile = min(512, rows)
-    index = lax.axis_index("tok").astype(jnp.int32)
-    if pieces[0].shape[1] % 128:
-        order = jnp.arange(len(pieces), dtype=jnp.int32) ^ index
-        pieces = jnp.take(jnp.stack(pieces), order, axis=0)
-        pieces = [jnp.moveaxis(pieces, 0, 1).reshape(pieces.shape[1], columns)]
-    index = index.reshape(1)
-    block = pl.BlockSpec((tile, columns), lambda i, *_: (i, 0))
-    return pl.pallas_call(
-        update_kernel,
+    index = lax.axis_index("tok").astype(jnp.int32).reshape(1)
+    extra = [] if result is None else [result]
+    count = rows // tile * len(runs)
+    return pl.pallas_call(
+        functools.partial(update_kernel, runs),
         out_shape=jax.ShapeDtypeStruct((rows, columns), BF16),
-        grid_spec=pltpu.PrefetchScalarGridSpec(
-            num_scalar_prefetch=1,
-            grid=(rows // tile,),
-            in_specs=[block, block, pl.BlockSpec((tile, pruned.shape[1]), lambda i, *_: (i, 0))]
-            + [pl.BlockSpec(memory_space=pltpu.VMEM)] * len(pieces),
-            out_specs=block,
-        ),
-        compiler_params=pltpu.CompilerParams(vmem_limit_bytes=32 << 20),
+        in_specs=[pl.BlockSpec(memory_space=pltpu.SMEM)]
+        + [pl.BlockSpec(memory_space=pltpu.VMEM)] * (3 + len(pieces))
+        + [pl.BlockSpec(memory_space=pl.ANY)] * len(extra),
+        out_specs=pl.BlockSpec(memory_space=pl.ANY),
+        scratch_shapes=[pltpu.VMEM((count, tile, width), BF16), pltpu.SemaphoreType.DMA((count,))],
+        input_output_aliases={4 + len(pieces): 0} if extra else {},
+        compiler_params=pltpu.CompilerParams(vmem_limit_bytes=20 << 20),
         cost_estimate=pl.CostEstimate(
-            flops=2 * rows * columns * B, bytes_accessed=10 * rows * columns, transcendentals=0
+            flops=2 * rows * width * len(runs) * B,
+            bytes_accessed=6 * rows * width * len(runs),
+            transcendentals=0,
         ),
         name="update",
-    )(index, weight, mask, pruned, *pieces)
+    )(index, weight, mask, pruned, *pieces, *extra)
+
+
+def updated(weight, mask, pruned, pieces):
+    width = pieces[0].shape[1]
+    if width % 128:
+        order = jnp.arange(len(pieces), dtype=jnp.int32) ^ lax.axis_index("tok")
+        whole = jnp.take(jnp.stack(pieces, axis=1), order, axis=1).reshape(B, -1)
+        fix = jnp.dot(pruned, whole, preferred_element_type=F32)
+        return (mask.astype(F32) * (weight.astype(F32) - fix)).astype(BF16)
+    *most, last = pieces
+    result = update(weight, mask, pruned, most, tuple(range(len(most))))
+    return update(weight, mask, pruned, [last], (len(most),), result)
 
 
 def gather_and_sum(activations, n_col, n_tok, bits, turned):
@@ -356,7 +382,8 @@
         if k:
             rows = (0, 1) if k == 1 else (k,)
             sums.append(sum_tok(block_rows(panels, rows), n_tok, order))
-        parts.append(scatter_tok(*panel_products(*panels[-2:], activations, order), n_tok, order))
+        products = panel_products(panels[-2:], activations, halving(order))
+        parts.append(scatter_tok(*products, n_tok, order))
     return sums, [swap_core(x, n_col) for x in sums], parts, mine
 
 
@@ -382,19 +409,27 @@
     second = shift_chip(first, n_col, 1)
     third = shift_chip(own, n_col, -1)
     panels = [own, swapped(own)]
-    sent, kept = panel_products(*panels, activations, bits)
+    sent, kept = panel_products(panels[:1], activations, halving(bits))
     part_0 = second_step(kept, over(sent, x), y)
+    sent, kept = panel_products(panels[1:], activations, halving(turned))
+    part_0b = second_step(kept, over(sent, y), x)
 
     panels += [first, swapped(first)]
     rows_1 = block_rows(panels, (0, 1))
     total_1 = added(rows_1, over(rows_1, x))
     sum_1 = added(total_1, over(total_1, y))
-    sent, kept = panel_products(panels[2], activations, bits)
+    sent, kept = panel_products(panels[2:3], activations, halving(bits))
     part_1 = second_step(kept, over(sent, x), y)
-    sent, kept = panel_products(panels[3], activations, turned)
+    sent, kept = panel_products(panels[3:], activations, halving(turned))
     part_2 = second_step(kept, over(sent, y), x)
 
-    panels += [second, swapped(second), third, swapped(third)]
+    panels += [second, swapped(second)]
+    sent, kept = panel_products(panels[4:5], activations, halving(bits))
+    part_3 = second_step(kept, over(sent, x), y)
+    sent, kept = panel_products(panels[5:], activations, halving(turned))
+    part_4 = second_step(kept, over(sent, y), x)
+
+    panels += [third, swapped(third)]
     rows_3 = block_rows(panels, (2, 3))
     middle = rows_3.shape[1] // 2
     left, right = rows_3[:, :middle], rows_3[:, middle:]
@@ -402,14 +437,12 @@
     right = added(right, over(right, y))
     sum_3 = [added(left, over(left, y)), added(right, over(right, x))]
     sum_3 = jnp.concatenate(sum_3, axis=1)
-    sent, kept = panel_products(*panels[4:6], after(activations, rows_3), bits)
-    part_3 = second_step(kept, over(sent, x), y)
-    sent, kept = panel_products(*panels[6:], after(activations, rows_3), turned)
-    part_4 = second_step(kept, over(sent, y), x)
+    products = panel_products(panels[6:], after(activations, rows_3), ((0,), (1,), (2,), (3,)))
+    part_5 = [products[0]] + [over(products[m], m) for m in (x, y, x | y)]
 
     sums = [sum_1, sum_3]
     others = [swapped(v) for v in sums]
-    return sums, others, [part_0, part_1, part_2, part_3, part_4], rows_3
+    return sums, others, [part_0, part_0b, part_1, part_2, part_3, part_4, part_5], rows_3
 
 
 def per_device(activations, weight, keep_mask):
@@ -426,11 +459,15 @@
     solved = solve_rows(parts, v_hi, v_lo, scale)
     pieces = gather_tok(solved, n_tok)
 
-    pruned = pruned_columns(weight, keep_mask, panel_width)
-    steps = [1, 2, -1] if chips == 4 else range(1, chips)
-    pruned = [pruned] + [shift_chip(pruned, n_col, s) for s in steps]
+    pruned, mask = pruned_columns(weight, keep_mask, panel_width)
+    if chips == 4:
+        second = shift_chip(pruned, n_col, 1)
+        third = shift_chip(second, n_col, 1)
+        pruned = [pruned, second, third, shift_chip(pruned, n_col, -1)]
+    else:
+        pruned = [pruned] + [shift_chip(pruned, n_col, k) for k in range(1, chips)]
     pruned_panel = jnp.concatenate([x for a in pruned for x in (a, swap_core(a, n_col))], axis=1)
-    return update(weight, keep_mask, pruned_panel, pieces)
+    return updated(weight, mask, pruned_panel, pieces)
 
 
 def solution(mesh):

time: 175 us -> 159 us (0.909)
  the two profiles are of different devices: /device:TPU:18 before, /device:TPU:24 now
where the time goes in v3:
time: 159 us
  waiting for transfers between devices  86.5 us (54%)
  starting transfers between devices  36.1 us (23%)
  Pallas kernels  27.4 us (17%)
  local copies, waits for them, and re-layouts  8.1 us (5%)
    ppermute x25, waiting for transfers between devices, swap_tok(): return lax.ppermute(x, 'tok', [(i, i ^ bit) for i in range(n_tok)])  44.1 us
    ppermute x6, waiting for transfers between devices, shift_chip(): lax.ppermute(x, 'col', [(i, (i + 2 * step) % n_col) for i in range(n_col)])  42.4 us
    ppermute x25, starting transfers between devices, swap_tok(): return lax.ppermute(x, 'tok', [(i, i ^ bit) for i in range(n_tok)])  27.8 us
    pallas_call x1, Pallas kernels, inverse(): pl.pallas_call(functools.partial(inverse_kernel, width, len(own)), out_sh...  9.83 us
    pallas_call x2, Pallas kernels, update(): pl.pallas_call(functools.partial(update_kernel, runs), out_shape=jax.Shap...  7.12 us
    unnamed x15, local copies, waits for them, and re-layouts  6.77 us
    ppermute x6, starting transfers between devices, shift_chip(): lax.ppermute(x, 'col', [(i, (i + 2 * step) % n_col) for i in range(n_col)])  6.76 us
    pallas_call x7, Pallas kernels, panel_products(): pl.pallas_call(functools.partial(panel_kernel, runs), out_shape=[jax.Shap...  5.85 us
  transfers between devices with their start and end apart: 41, of which 17 were waited for; matrix products, arithmetic and copies ran while one was open for 1% of the time, Pallas kernels for 16%

profile of v3, /device:TPU:24, one launch (start us, length us, event | category | flops | bytes accessed | tf_op | source)
XLA Modules:
  0.0 159.2 jit_solution(15519341331520153355)
XLA Ops:
  1.2 2.2 %copy-done = bf16[2048,1024]{1,0:T(8,128)(2,1)S(1)} copy-done((bf16[2048,1024]{1,0:T(8,128)(2,1)S(1)}, bf16[2048,1024]{1,0:T(8,128)(2,1)}, u32[]{:S(2)}) %copy-start) | copy-done | bytes 4194328
  5.9 1.8 %collective-permute-start.24 = (bf16[2048,128]{1,0:T(8,128)(2,1)S(1)}, bf16[2048,128]{1,0:T(8,128)(2,1)S(1)}, u32[]{:S(2)}, u32[]{:S(2)}) collective-permute-start(bf16[2048,128]{1,0:T(8,128)(2,1)S(1)} %slice.51.refs_0_), channel_id=1, source_target_pairs={{0,6},{1,7},{2,0},{3,1},{4,2},{5,3},{6,4},{7,5},{8,14},{9,15},{10,... | collective-permute-start | bytes 1572872 | tf_op jit(solution)/shard_map/ppermute | solution.py:18
  7.7 3.4 %copy-done.3 = s32[2048,1024]{1,0:T(8,128)S(1)} copy-done((s32[2048,1024]{1,0:T(8,128)S(1)}, s32[2048,1024]{1,0:T(8,128)}, u32[]{:S(2)}) %copy-start.3) | copy-done | bytes 8388632
  12.3 2.1 %collective-permute-start.1 = (bf16[2048,128]{1,0:T(8,128)(2,1)S(1)}, bf16[2048,128]{1,0:T(8,128)(2,1)S(1)}, u32[]{:S(2)}, u32[]{:S(2)}) collective-permute-start(bf16[2048,128]{1,0:T(8,128)(2,1)S(1)} %get-tuple-element.28), channel_id=1, source_target_pairs={{0,2},{1,3},{2,4},{3,5},{4,6},{5,7},{6,0},{7,1},{8,10},{9,11},{10,... | collective-permute-start | bytes 1572872 | tf_op jit(solution)/shard_map/ppermute | solution.py:18
  14.4 11.5 %collective-permute-done.12.refs_0_.refs_2_ = bf16[2048,128]{1,0:T(8,128)(2,1)S(1)} collective-permute-done((bf16[2048,128]{1,0:T(8,128)(2,1)S(1)}, bf16[2048,128]{1,0:T(8,128)(2,1)S(1)}, u32[]{:S(2)}, u32[]{:S(2)}) %collective-permute-start.12) | collective-permute-done | bytes 524320 | tf_op jit(solution)/shard_map/ppermute | solution.py:18
  26.7 2.5 %collective-permute-start.13 = (f32[128,512]{1,0:T(8,128)S(1)}, f32[128,512]{1,0:T(8,128)S(1)}, u32[]{:S(2)}, u32[]{:S(2)}) collective-permute-start(f32[128,512]{1,0:T(8,128)S(1)} %get-tuple-element.34), channel_id=1, source_target_pairs={{0,8},{8,0},{16,24},{24,16},{1,9},{9,1},{17,25},{25,17},{2,10},{10... | collective-permute-start | bytes 786440 | tf_op jit(solution)/shard_map/ppermute | solution.py:26
  31.8 5.9 %collective-permute-done.1 = bf16[2048,128]{1,0:T(8,128)(2,1)S(1)} collective-permute-done((bf16[2048,128]{1,0:T(8,128)(2,1)S(1)}, bf16[2048,128]{1,0:T(8,128)(2,1)S(1)}, u32[]{:S(2)}, u32[]{:S(2)}) %collective-permute-start.1) | collective-permute-done | bytes 524320 | tf_op jit(solution)/shard_map/ppermute | solution.py:18
  38.5 2.6 %collective-permute-start.3 = (bf16[2048,128]{1,0:T(8,128)(2,1)S(1)}, bf16[2048,128]{1,0:T(8,128)(2,1)S(1)}, u32[]{:S(2)}, u32[]{:S(2)}) collective-permute-start(bf16[2048,128]{1,0:T(8,128)(2,1)S(1)} %collective-permute-done.1), channel_id=1, source_target_pairs={{0,2},{1,3},{2,4},{3,5},{4,6},{5,7},{6,0},{7,1},{8,10},{9,11},{10,... | collective-permute-start | bytes 1572872 | tf_op jit(solution)/shard_map/ppermute | solution.py:18
  42.8 1.8 %collective-permute-start.8 = (f32[128,256]{1,0:T(8,128)S(1)}, f32[128,256]{1,0:T(8,128)S(1)}, u32[]{:S(2)}, u32[]{:S(2)}) collective-permute-start(f32[128,256]{1,0:T(8,128)S(1)} %slice_add_fusion.5), channel_id=1, source_target_pairs={{0,16},{8,24},{16,0},{24,8},{1,17},{9,25},{17,1},{25,9},{2,18},{10... | collective-permute-start | bytes 393224 | tf_op jit(solution)/shard_map/ppermute | solution.py:26
  44.6 4.3 %collective-permute-done.18.refs_0_.refs_4_ = bf16[2048,128]{1,0:T(8,128)(2,1)S(1)} collective-permute-done((bf16[2048,128]{1,0:T(8,128)(2,1)S(1)}, bf16[2048,128]{1,0:T(8,128)(2,1)S(1)}, u32[]{:S(2)}, u32[]{:S(2)}) %collective-permute-start.18) | collective-permute-done | bytes 524320 | tf_op jit(solution)/shard_map/ppermute | solution.py:18
  50.4 20.6 %collective-permute-done.3 = bf16[2048,128]{1,0:T(8,128)(2,1)S(1)} collective-permute-done((bf16[2048,128]{1,0:T(8,128)(2,1)S(1)}, bf16[2048,128]{1,0:T(8,128)(2,1)S(1)}, u32[]{:S(2)}, u32[]{:S(2)}) %collective-permute-start.3) | collective-permute-done | bytes 524320 | tf_op jit(solution)/shard_map/ppermute | solution.py:18
  72.6 4.0 %collective-permute-done.29 = bf16[128,768]{1,0:T(8,128)(2,1)S(1)} collective-permute-done((bf16[128,768]{1,0:T(8,128)(2,1)S(1)}, bf16[128,768]{1,0:T(8,128)(2,1)S(1)}, u32[]{:S(2)}, u32[]{:S(2)}) %collective-permute-start.29) | collective-permute-done | bytes 196640 | tf_op jit(solution)/shard_map/ppermute | solution.py:26
  81.7 4.0 %collective-permute-done.16.refs_10_ = f32[128,512]{1,0:T(8,128)S(1)} collective-permute-done((f32[128,512]{1,0:T(8,128)S(1)}, f32[128,512]{1,0:T(8,128)S(1)}, u32[]{:S(2)}, u32[]{:S(2)}) %collective-permute-start.16) | collective-permute-done | bytes 262176 | tf_op jit(solution)/shard_map/ppermute | solution.py:26
  87.9 3.9 %collective-permute-done.33 = bf16[128,896]{1,0:T(8,128)(2,1)S(1)} collective-permute-done((bf16[128,896]{1,0:T(8,128)(2,1)S(1)}, bf16[128,896]{1,0:T(8,128)(2,1)S(1)}, u32[]{:S(2)}, u32[]{:S(2)}) %collective-permute-start.33) | collective-permute-done | bytes 229408 | tf_op jit(solution)/shard_map/ppermute | solution.py:26
  94.8 6.1 %collective-permute-done.32 = bf16[128,896]{1,0:T(8,128)(2,1)S(1)} collective-permute-done((bf16[128,896]{1,0:T(8,128)(2,1)S(1)}, bf16[128,896]{1,0:T(8,128)(2,1)S(1)}, u32[]{:S(2)}, u32[]{:S(2)}) %collective-permute-start.32) | collective-permute-done | bytes 229408 | tf_op jit(solution)/shard_map/ppermute | solution.py:26
  101.2 5.7 %collective-permute-done.34 = bf16[128,896]{1,0:T(8,128)(2,1)S(1)} collective-permute-done((bf16[128,896]{1,0:T(8,128)(2,1)S(1)}, bf16[128,896]{1,0:T(8,128)(2,1)S(1)}, u32[]{:S(2)}, u32[]{:S(2)}) %collective-permute-start.34) | collective-permute-done | bytes 229408 | tf_op jit(solution)/shard_map/ppermute | solution.py:26
  113.3 3.1 %collective-permute-done.11.refs_5_ = f32[128,256]{1,0:T(8,128)S(1)} collective-permute-done((f32[128,256]{1,0:T(8,128)S(1)}, f32[128,256]{1,0:T(8,128)S(1)}, u32[]{:S(2)}, u32[]{:S(2)}) %collective-permute-start.11) | collective-permute-done | bytes 131104 | tf_op jit(solution)/shard_map/ppermute | solution.py:26
  116.4 2.3 %collective-permute-done.17.refs_11_ = f32[128,256]{1,0:T(8,128)S(1)} collective-permute-done((f32[128,256]{1,0:T(8,128)S(1)}, f32[128,256]{1,0:T(8,128)S(1)}, u32[]{:S(2)}, u32[]{:S(2)}) %collective-permute-start.17) | collective-permute-done | bytes 131104 | tf_op jit(solution)/shard_map/ppermute | solution.py:26
  119.6 2.7 %collective-permute-start.28 = (f32[256,256]{1,0:T(8,128)S(1)}, f32[256,256]{1,0:T(8,128)S(1)}, u32[]{:S(2)}, u32[]{:S(2)}) collective-permute-start(f32[256,256]{1,0:T(8,128)S(1)} %get-tuple-element.45), channel_id=1, source_target_pairs={{0,24},{8,16},{16,8},{24,0},{1,25},{9,17},{17,9},{25,1},{2,26},{10... | collective-permute-start | bytes 786440 | tf_op jit(solution)/shard_map/ppermute | solution.py:26
  122.5 9.8 %inverse.1 = (bf16[1024,1024]{1,0:T(8,128)(2,1)S(1)}, bf16[1024,1024]{1,0:T(8,128)(2,1)S(1)}, f32[8,128]{1,0:T(8,128)S(1)}) custom-call(bf16[128,768]{1,0:T(8,128)(2,1)S(1)} %add_convert_fusion.4.refs_0_, bf16[128,1792]{1,0:T(8,128)(2,1)S(1)} %pad_maximum_fusion.1.refs_1_, bf16[128,768]{1,0:T(8,128)(2,1)S(1)} %collective-permute-done.35.refs_2_, ...), custom_call_target="tpu_custom_call" | custom-call | flops 12884901888 | bytes 8388608 | tf_op jit(solution)/shard_map/inverse/pallas_call | solution.py:233
  135.0 1.9 %solve_rows.1.rest_0_ = bf16[1024,256]{1,0:T(8,128)(2,1)S(1)} custom-call(f32[128,512]{1,0:T(8,128)S(1)} %get-tuple-element.29.refs_0_, f32[128,512]{1,0:T(8,128)S(1)} %collective-permute-done.7.refs_1_, f32[128,256]{1,0:T(8,128)S(1)} %collective-permute-done.8.refs_2_, f32[128,512]{1,0:T(8,128)S(1)} %get-tuple-element.31.refs_3_, ...), custom_call_target="tpu_custom_call" | custom-call | flops 1610612736 | bytes 4194304 | tf_op jit(solution)/shard_map/solve_rows/pallas_call | solution.py:276
  138.4 11.2 %collective-permute-done.37.rest_1_ = bf16[1024,256]{1,0:T(8,128)(2,1)S(1)} collective-permute-done((bf16[1024,256]{1,0:T(8,128)(2,1)S(1)}, bf16[1024,256]{1,0:T(8,128)(2,1)S(1)}, u32[]{:S(2)}, u32[]{:S(2)}) %collective-permute-start.37) | collective-permute-done | bytes 524320 | tf_op jit(solution)/shard_map/ppermute | solution.py:26
  151.4 4.9 %update.2.rest_1_ = bf16[2048,1024]{1,0:T(8,128)(2,1)} custom-call(s32[1]{0:T(128)} %bitcast.index_ref, bf16[2048,1024]{1,0:T(8,128)(2,1)S(1)} %copy-done.2, bf16[2048,1024]{1,0:T(8,128)(2,1)S(1)} %get-tuple-element.27.mask_ref, bf16[2048,1024]{1,0:T(8,128)(2,1)S(1)} %constant_dynamic-update-slice_fusion.pruned_ref, ...), custom_call_target="tpu_custom_call" | custom-call | flops 3221225472 | bytes 9437184 | tf_op jit(solution)/shard_map/update/pallas_call | solution.py:343
  156.8 2.3 %update.3 = bf16[2048,1024]{1,0:T(8,128)(2,1)} custom-call(s32[1]{0:T(128)} %bitcast.index_ref, bf16[2048,1024]{1,0:T(8,128)(2,1)S(1)} %copy-done.2, bf16[2048,1024]{1,0:T(8,128)(2,1)S(1)} %get-tuple-element.27.mask_ref, bf16[2048,1024]{1,0:T(8,128)(2,1)S(1)} %constant_dynamic-update-slice_fusion.pruned_ref, ...), custom_call_target="tpu_custom_call", output_to_operand_aliasing={{}: (5, {})} | custom-call | flops 1073741824 | bytes 3145728 | tf_op jit(solution)/shard_map/update/pallas_call | solution.py:343
  (105 shorter events, 38.1 us)
Async XLA Ops:
  1.1 24.9 %collective-permute-start.12 = (bf16[2048,128]{1,0:T(8,128)(2,1)S(1)}, bf16[2048,128]{1,0:T(8,128)(2,1)S(1)}, u32[]{:S(2)}, u32[]{:S(2)}) collective-permute-start(bf16[2048,128]{1,0:T(8,128)(2,1)S(1)} %slice.51.refs_0_), channel_id=1, source_target_pairs={{0,2},{1,3},{2,4},{3,5},{4,6},{5,7},{6,0},{7,1},{8,10},{9,11},{10,... | collective-permute-start | bytes 1572872 | tf_op jit(solution)/shard_map/ppermute | solution.py:18
  5.9 23.4 %collective-permute-start.9 = (bf16[2048,128]{1,0:T(8,128)(2,1)S(1)}, bf16[2048,128]{1,0:T(8,128)(2,1)S(1)}, u32[]{:S(2)}, u32[]{:S(2)}) collective-permute-start(bf16[2048,128]{1,0:T(8,128)(2,1)S(1)} %slice.51.refs_0_), channel_id=1, source_target_pairs={{0,1},{1,0},{2,3},{3,2},{4,5},{5,4},{6,7},{7,6},{8,9},{9,8},{10,11... | collective-permute-start | bytes 1572872 | tf_op jit(solution)/shard_map/ppermute | solution.py:22
  5.9 36.9 %collective-permute-start.24 = (bf16[2048,128]{1,0:T(8,128)(2,1)S(1)}, bf16[2048,128]{1,0:T(8,128)(2,1)S(1)}, u32[]{:S(2)}, u32[]{:S(2)}) collective-permute-start(bf16[2048,128]{1,0:T(8,128)(2,1)S(1)} %slice.51.refs_0_), channel_id=1, source_target_pairs={{0,6},{1,7},{2,0},{3,1},{4,2},{5,3},{6,4},{7,5},{8,14},{9,15},{10,... | collective-permute-start | bytes 1572872 | tf_op jit(solution)/shard_map/ppermute | solution.py:18
  11.9 19.7 %collective-permute-start = (bf16[2048,128]{1,0:T(8,128)(2,1)S(1)}, bf16[2048,128]{1,0:T(8,128)(2,1)S(1)}, u32[]{:S(2)}, u32[]{:S(2)}) collective-permute-start(bf16[2048,128]{1,0:T(8,128)(2,1)S(1)} %get-tuple-element.28), channel_id=1, source_target_pairs={{0,1},{1,0},{2,3},{3,2},{4,5},{5,4},{6,7},{7,6},{8,9},{9,8},{10,11... | collective-permute-start | bytes 1572872 | tf_op jit(solution)/shard_map/ppermute | solution.py:22
  12.3 25.4 %collective-permute-start.1 = (bf16[2048,128]{1,0:T(8,128)(2,1)S(1)}, bf16[2048,128]{1,0:T(8,128)(2,1)S(1)}, u32[]{:S(2)}, u32[]{:S(2)}) collective-permute-start(bf16[2048,128]{1,0:T(8,128)(2,1)S(1)} %get-tuple-element.28), channel_id=1, source_target_pairs={{0,2},{1,3},{2,4},{3,5},{4,6},{5,7},{6,0},{7,1},{8,10},{9,11},{10,... | collective-permute-start | bytes 1572872 | tf_op jit(solution)/shard_map/ppermute | solution.py:18
  26.7 11.2 %collective-permute-start.13 = (f32[128,512]{1,0:T(8,128)S(1)}, f32[128,512]{1,0:T(8,128)S(1)}, u32[]{:S(2)}, u32[]{:S(2)}) collective-permute-start(f32[128,512]{1,0:T(8,128)S(1)} %get-tuple-element.34), channel_id=1, source_target_pairs={{0,8},{8,0},{16,24},{24,16},{1,9},{9,1},{17,25},{25,17},{2,10},{10... | collective-permute-start | bytes 786440 | tf_op jit(solution)/shard_map/ppermute | solution.py:26
  31.6 17.3 %collective-permute-start.18 = (bf16[2048,128]{1,0:T(8,128)(2,1)S(1)}, bf16[2048,128]{1,0:T(8,128)(2,1)S(1)}, u32[]{:S(2)}, u32[]{:S(2)}) collective-permute-start(bf16[2048,128]{1,0:T(8,128)(2,1)S(1)} %collective-permute-done.12.refs_0_.refs_2_), channel_id=1, source_target_pairs={{0,2},{1,3},{2,4},{3,5},{4,6},{5,7},{6,0},{7,1},{8,10},{9,11},{10,... | collective-permute-start | bytes 1572872 | tf_op jit(solution)/shard_map/ppermute | solution.py:18
  37.9 11.0 %collective-permute-start.2 = (bf16[2048,128]{1,0:T(8,128)(2,1)S(1)}, bf16[2048,128]{1,0:T(8,128)(2,1)S(1)}, u32[]{:S(2)}, u32[]{:S(2)}) collective-permute-start(bf16[2048,128]{1,0:T(8,128)(2,1)S(1)} %collective-permute-done.1), channel_id=1, source_target_pairs={{0,1},{1,0},{2,3},{3,2},{4,5},{5,4},{6,7},{7,6},{8,9},{9,8},{10,11... | collective-permute-start | bytes 1572872 | tf_op jit(solution)/shard_map/ppermute | solution.py:22
  38.5 32.5 %collective-permute-start.3 = (bf16[2048,128]{1,0:T(8,128)(2,1)S(1)}, bf16[2048,128]{1,0:T(8,128)(2,1)S(1)}, u32[]{:S(2)}, u32[]{:S(2)}) collective-permute-start(bf16[2048,128]{1,0:T(8,128)(2,1)S(1)} %collective-permute-done.1), channel_id=1, source_target_pairs={{0,2},{1,3},{2,4},{3,5},{4,6},{5,7},{6,0},{7,1},{8,10},{9,11},{10,... | collective-permute-start | bytes 1572872 | tf_op jit(solution)/shard_map/ppermute | solution.py:18
  41.1 69.2 %collective-permute-start.5 = (bf16[2048,128]{1,0:T(8,128)(2,1)S(1)}, bf16[2048,128]{1,0:T(8,128)(2,1)S(1)}, u32[]{:S(2)}, u32[]{:S(2)}) collective-permute-start(bf16[2048,128]{1,0:T(8,128)(2,1)S(1)} %get-tuple-element.28), channel_id=1, source_target_pairs={{0,6},{1,7},{2,0},{3,1},{4,2},{5,3},{6,4},{7,5},{8,14},{9,15},{10,... | collective-permute-start | bytes 1572872 | tf_op jit(solution)/shard_map/ppermute | solution.py:18
  42.8 67.2 %collective-permute-start.8 = (f32[128,256]{1,0:T(8,128)S(1)}, f32[128,256]{1,0:T(8,128)S(1)}, u32[]{:S(2)}, u32[]{:S(2)}) collective-permute-start(f32[128,256]{1,0:T(8,128)S(1)} %slice_add_fusion.5), channel_id=1, source_target_pairs={{0,16},{8,24},{16,0},{24,8},{1,17},{9,25},{17,1},{25,9},{2,18},{10... | collective-permute-start | bytes 393224 | tf_op jit(solution)/shard_map/ppermute | solution.py:26
  48.9 29.3 %collective-permute-start.25 = (bf16[2048,128]{1,0:T(8,128)(2,1)S(1)}, bf16[2048,128]{1,0:T(8,128)(2,1)S(1)}, u32[]{:S(2)}, u32[]{:S(2)}) collective-permute-start(bf16[2048,128]{1,0:T(8,128)(2,1)S(1)} %collective-permute-done.24.refs_6_.refs_0_), channel_id=1, source_target_pairs={{0,1},{1,0},{2,3},{3,2},{4,5},{5,4},{6,7},{7,6},{8,9},{9,8},{10,11... | collective-permute-start | bytes 1572872 | tf_op jit(solution)/shard_map/ppermute | solution.py:22
  49.0 30.8 %collective-permute-start.21 = (bf16[2048,128]{1,0:T(8,128)(2,1)S(1)}, bf16[2048,128]{1,0:T(8,128)(2,1)S(1)}, u32[]{:S(2)}, u32[]{:S(2)}) collective-permute-start(bf16[2048,128]{1,0:T(8,128)(2,1)S(1)} %collective-permute-done.18.refs_0_.refs_4_), channel_id=1, source_target_pairs={{0,1},{1,0},{2,3},{3,2},{4,5},{5,4},{6,7},{7,6},{8,9},{9,8},{10,11... | collective-permute-start | bytes 1572872 | tf_op jit(solution)/shard_map/ppermute | solution.py:22
  78.2 15.2 %collective-permute-start.19 = (f32[128,512]{1,0:T(8,128)S(1)}, f32[128,512]{1,0:T(8,128)S(1)}, u32[]{:S(2)}, u32[]{:S(2)}) collective-permute-start(f32[128,512]{1,0:T(8,128)S(1)} %get-tuple-element.38), channel_id=1, source_target_pairs={{0,8},{8,0},{16,24},{24,16},{1,9},{9,1},{17,25},{25,17},{2,10},{10... | collective-permute-start | bytes 786440 | tf_op jit(solution)/shard_map/ppermute | solution.py:26
  87.3 24.8 %collective-permute-start.14 = (f32[128,256]{1,0:T(8,128)S(1)}, f32[128,256]{1,0:T(8,128)S(1)}, u32[]{:S(2)}, u32[]{:S(2)}) collective-permute-start(f32[128,256]{1,0:T(8,128)S(1)} %slice_add_fusion.3), channel_id=1, source_target_pairs={{0,16},{8,24},{16,0},{24,8},{1,17},{9,25},{17,1},{25,9},{2,18},{10... | collective-permute-start | bytes 393224 | tf_op jit(solution)/shard_map/ppermute | solution.py:26
  91.7 16.8 %collective-permute-start.30 = (bf16[128,768]{1,0:T(8,128)(2,1)S(1)}, bf16[128,768]{1,0:T(8,128)(2,1)S(1)}, u32[]{:S(2)}, u32[]{:S(2)}) collective-permute-start(bf16[128,768]{1,0:T(8,128)(2,1)S(1)} %add_convert_fusion.5), channel_id=1, source_target_pairs={{0,16},{8,24},{16,0},{24,8},{1,17},{9,25},{17,1},{25,9},{2,18},{10... | collective-permute-start | bytes 589832 | tf_op jit(solution)/shard_map/ppermute | solution.py:26
  108.5 13.7 %collective-permute-start.36 = (bf16[128,1792]{1,0:T(8,128)(2,1)S(1)}, bf16[128,1792]{1,0:T(8,128)(2,1)S(1)}, u32[]{:S(2)}, u32[]{:S(2)}) collective-permute-start(bf16[128,1792]{1,0:T(8,128)(2,1)S(1)} %pad_maximum_fusion.1.refs_1_), channel_id=1, source_target_pairs={{0,1},{1,0},{2,3},{3,2},{4,5},{5,4},{6,7},{7,6},{8,9},{9,8},{10,11... | collective-permute-start | bytes 1376264 | tf_op jit(solution)/shard_map/ppermute | solution.py:22
  116.4 21.4 %collective-permute-start.4 = (bf16[2048,128]{1,0:T(8,128)(2,1)S(1)}, bf16[2048,128]{1,0:T(8,128)(2,1)S(1)}, u32[]{:S(2)}, u32[]{:S(2)}) collective-permute-start(bf16[2048,128]{1,0:T(8,128)(2,1)S(1)} %collective-permute-done.3), channel_id=1, source_target_pairs={{0,1},{1,0},{2,3},{3,2},{4,5},{5,4},{6,7},{7,6},{8,9},{9,8},{10,11... | collective-permute-start | bytes 1572872 | tf_op jit(solution)/shard_map/ppermute | solution.py:22
  118.7 13.6 %collective-permute-start.26 = (f32[256,256]{1,0:T(8,128)S(1)}, f32[256,256]{1,0:T(8,128)S(1)}, u32[]{:S(2)}, u32[]{:S(2)}) collective-permute-start(f32[256,256]{1,0:T(8,128)S(1)} %get-tuple-element.43), channel_id=1, source_target_pairs={{0,8},{8,0},{16,24},{24,16},{1,9},{9,1},{17,25},{25,17},{2,10},{10... | collective-permute-start | bytes 786440 | tf_op jit(solution)/shard_map/ppermute | solution.py:26
  119.0 13.4 %collective-permute-start.27 = (f32[256,256]{1,0:T(8,128)S(1)}, f32[256,256]{1,0:T(8,128)S(1)}, u32[]{:S(2)}, u32[]{:S(2)}) collective-permute-start(f32[256,256]{1,0:T(8,128)S(1)} %get-tuple-element.44), channel_id=1, source_target_pairs={{0,16},{8,24},{16,0},{24,8},{1,17},{9,25},{17,1},{25,9},{2,18},{10... | collective-permute-start | bytes 786440 | tf_op jit(solution)/shard_map/ppermute | solution.py:26
  119.6 13.9 %collective-permute-start.28 = (f32[256,256]{1,0:T(8,128)S(1)}, f32[256,256]{1,0:T(8,128)S(1)}, u32[]{:S(2)}, u32[]{:S(2)}) collective-permute-start(f32[256,256]{1,0:T(8,128)S(1)} %get-tuple-element.45), channel_id=1, source_target_pairs={{0,24},{8,16},{16,8},{24,0},{1,25},{9,17},{17,9},{25,1},{2,26},{10... | collective-permute-start | bytes 786440 | tf_op jit(solution)/shard_map/ppermute | solution.py:26
  122.2 12.8 %collective-permute-start.23 = (f32[128,256]{1,0:T(8,128)S(1)}, f32[128,256]{1,0:T(8,128)S(1)}, u32[]{:S(2)}, u32[]{:S(2)}) collective-permute-start(f32[128,256]{1,0:T(8,128)S(1)} %slice_add_fusion), channel_id=1, source_target_pairs={{0,8},{8,0},{16,24},{24,16},{1,9},{9,1},{17,25},{25,17},{2,10},{10... | collective-permute-start | bytes 393224 | tf_op jit(solution)/shard_map/ppermute | solution.py:26
  136.9 12.7 %collective-permute-start.37 = (bf16[1024,256]{1,0:T(8,128)(2,1)S(1)}, bf16[1024,256]{1,0:T(8,128)(2,1)S(1)}, u32[]{:S(2)}, u32[]{:S(2)}) collective-permute-start(bf16[1024,256]{1,0:T(8,128)(2,1)S(1)} %solve_rows.1.rest_0_), channel_id=1, source_target_pairs={{0,8},{8,0},{16,24},{24,16},{1,9},{9,1},{17,25},{25,17},{2,10},{10... | collective-permute-start | bytes 1572872 | tf_op jit(solution)/shard_map/ppermute | solution.py:26
  137.3 13.0 %collective-permute-start.39 = (bf16[1024,256]{1,0:T(8,128)(2,1)S(1)}, bf16[1024,256]{1,0:T(8,128)(2,1)S(1)}, u32[]{:S(2)}, u32[]{:S(2)}) collective-permute-start(bf16[1024,256]{1,0:T(8,128)(2,1)S(1)} %solve_rows.1.rest_0_), channel_id=1, source_target_pairs={{0,16},{8,24},{16,0},{24,8},{1,17},{9,25},{17,1},{25,9},{2,18},{10... | collective-permute-start | bytes 1572872 | tf_op jit(solution)/shard_map/ppermute | solution.py:26
  (21 other events, 145.7 us)

commit v4 on v3

--- a/solution.py
+++ b/solution.py
@@ -144,12 +144,15 @@
         while bit < n_tok:
             items = items + [swap_tok(v, n_tok, bit) for v in items]
             bit *= 2
-        return items
+        return [[v] for v in items]
     half = x.shape[0] // 2
-    over_x, over_y = swap_tok(x, n_tok, 1), swap_tok(x, n_tok, 2)
-    upper = swap_tok(over_x[:half], n_tok, 2)
-    lower = swap_tok(over_y[half:], n_tok, 1)
-    return [x, over_x, over_y, jnp.concatenate([upper, lower], axis=0)]
+    upper, lower = x[:half], x[half:]
+    over_x = [swap_tok(upper, n_tok, 1)]
+    over_y = [swap_tok(lower, n_tok, 2)]
+    over_x += [swap_tok(lower, n_tok, 1)]
+    over_y = [swap_tok(upper, n_tok, 2)] + over_y
+    both = [swap_tok(over_x[0], n_tok, 2), swap_tok(over_y[1], n_tok, 1)]
+    return [[x], over_x, over_y, both]
 
 
 def inverse_kernel(width, count, *refs):
@@ -284,38 +287,51 @@
     )(*flat, v_hi, v_lo, scale)
 
 
-def pruned_kernel(weight_ref, mask_ref, pruned_ref, kept_ref):
-    kept = mask_ref[...].astype(F32).astype(BF16)
-    kept_ref[...] = kept
-    width = weight_ref.shape[1]
-    pruned_ref[...] = jnp.where(mask_ref[:, :width] == 0, weight_ref[...], jnp.zeros((), BF16))
+def pruned_kernel(weight_ref, mask_ref, out_ref):
+    out_ref[...] = jnp.where(mask_ref[...] == 0, weight_ref[...], jnp.zeros((), BF16))
+
+
+def narrow_kernel(mask_ref, out_ref):
+    out_ref[...] = mask_ref[...].astype(F32).astype(BF16)
 
 
 def pruned_columns(weight, mask, width):
     if width % 128:
-        return jnp.where(mask[:, :width] == 0, weight[:, :width], jnp.zeros((), BF16)), mask.astype(BF16)
-    rows, columns = weight.shape
-    tile = min(512, rows)
-    narrow = pl.BlockSpec((tile, width), lambda i: (i, 0))
-    wide = pl.BlockSpec((tile, columns), lambda i: (i, 0))
+        return jnp.where(mask[:, :width] == 0, weight[:, :width], jnp.zeros((), BF16))
+    block = pl.BlockSpec((weight.shape[0], width), lambda i: (0, 0))
     return pl.pallas_call(
         pruned_kernel,
-        out_shape=[
-            jax.ShapeDtypeStruct((rows, width), BF16),
-            jax.ShapeDtypeStruct((rows, columns), BF16),
-        ],
-        grid=(rows // tile,),
-        in_specs=[narrow, wide],
-        out_specs=[narrow, wide],
-        compiler_params=pltpu.CompilerParams(vmem_limit_bytes=12 << 20),
-        cost_estimate=pl.CostEstimate(flops=0, bytes_accessed=6 * weight.size, transcendentals=0),
+        out_shape=jax.ShapeDtypeStruct((weight.shape[0], width), BF16),
+        grid=(1,),
+        in_specs=[block, block],
+        out_specs=block,
+        compiler_params=pltpu.CompilerParams(vmem_limit_bytes=8 << 20),
+        cost_estimate=pl.CostEstimate(flops=0, bytes_accessed=8 * weight.shape[0] * width, transcendentals=0),
         name="pruned_columns",
     )(weight, mask)
 
 
-def update_kernel(runs, index_ref, weight_ref, mask_ref, pruned_ref, *rest):
-    pieces = rest[: len(runs)]
+def narrowed(mask):
+    rows, columns = mask.shape
+    block = pl.BlockSpec((min(512, rows), columns), lambda i: (i, 0))
+    return pl.pallas_call(
+        narrow_kernel,
+        out_shape=jax.ShapeDtypeStruct(mask.shape, BF16),
+        grid=(rows // min(512, rows),),
+        in_specs=[block],
+        out_specs=block,
+        compiler_params=pltpu.CompilerParams(vmem_limit_bytes=12 << 20),
+        cost_estimate=pl.CostEstimate(flops=0, bytes_accessed=6 * mask.size, transcendentals=0),
+        name="narrowed",
+    )(mask)
+
+
+def update_kernel(runs, counts, index_ref, weight_ref, mask_ref, pruned_ref, *rest):
     out_ref, stage, sems = rest[-3:]
+    pieces = []
+    for count in counts:
+        pieces.append(rest[:count])
+        rest = rest[count:]
     rows = weight_ref.shape[0]
     _, tile, width = stage.shape
     copies = []
@@ -323,7 +339,11 @@
         for m, piece in zip(runs, pieces):
             slot = len(copies)
             place = (slice(i, i + tile), pl.ds(pl.multiple_of((index_ref[0] ^ m) * width, width), width))
-            fix = jnp.dot(pruned_ref[i : i + tile, :], piece[...], preferred_element_type=F32)
+            fix, start = 0.0, 0
+            for part in piece:
+                left = pruned_ref[i : i + tile, start : start + part.shape[0]]
+                fix += jnp.dot(left, part[...], preferred_element_type=F32)
+                start += part.shape[0]
             kept = weight_ref[place].astype(F32) - fix
             stage[slot] = (mask_ref[place].astype(F32) * kept).astype(BF16)
             copy = pltpu.make_async_copy(stage.at[slot], out_ref.at[place], sems.at[slot])
@@ -335,13 +355,15 @@
 
 def update(weight, mask, pruned, pieces, runs, result=None):
     rows, columns = weight.shape
-    width = pieces[0].shape[1]
+    width = pieces[0][0].shape[1]
+    counts = tuple(len(piece) for piece in pieces)
+    pieces = [part for piece in pieces for part in piece]
     tile = min(512, rows)
     index = lax.axis_index("tok").astype(jnp.int32).reshape(1)
     extra = [] if result is None else [result]
     count = rows // tile * len(runs)
     return pl.pallas_call(
-        functools.partial(update_kernel, runs),
+        functools.partial(update_kernel, runs, counts),
         out_shape=jax.ShapeDtypeStruct((rows, columns), BF16),
         in_specs=[pl.BlockSpec(memory_space=pltpu.SMEM)]
         + [pl.BlockSpec(memory_space=pltpu.VMEM)] * (3 + len(pieces))
@@ -360,10 +382,11 @@
 
 
 def updated(weight, mask, pruned, pieces):
-    width = pieces[0].shape[1]
+    width = pieces[0][0].shape[1]
     if width % 128:
         order = jnp.arange(len(pieces), dtype=jnp.int32) ^ lax.axis_index("tok")
-        whole = jnp.take(jnp.stack(pieces, axis=1), order, axis=1).reshape(B, -1)
+        whole = [jnp.concatenate(piece, axis=0) for piece in pieces]
+        whole = jnp.take(jnp.stack(whole, axis=1), order, axis=1).reshape(B, -1)
         fix = jnp.dot(pruned, whole, preferred_element_type=F32)
         return (mask.astype(F32) * (weight.astype(F32) - fix)).astype(BF16)
     *most, last = pieces
@@ -406,8 +429,8 @@
         return [kept, arrived, over(total, bit)]
 
     first = shift_chip(own, n_col, 1)
-    second = shift_chip(first, n_col, 1)
-    third = shift_chip(own, n_col, -1)
+    second = shift_chip(own, n_col, -1)
+    third = shift_chip(first, n_col, 1)
     panels = [own, swapped(own)]
     sent, kept = panel_products(panels[:1], activations, halving(bits))
     part_0 = second_step(kept, over(sent, x), y)
@@ -459,14 +482,16 @@
     solved = solve_rows(parts, v_hi, v_lo, scale)
     pieces = gather_tok(solved, n_tok)
 
-    pruned, mask = pruned_columns(weight, keep_mask, panel_width)
+    pruned = pruned_columns(weight, keep_mask, panel_width)
+    mask = narrowed(keep_mask)
     if chips == 4:
         second = shift_chip(pruned, n_col, 1)
         third = shift_chip(second, n_col, 1)
-        pruned = [pruned, second, third, shift_chip(pruned, n_col, -1)]
+        pruned = [pruned, second, shift_chip(pruned, n_col, -1), third]
     else:
         pruned = [pruned] + [shift_chip(pruned, n_col, k) for k in range(1, chips)]
-    pruned_panel = jnp.concatenate([x for a in pruned for x in (a, swap_core(a, n_col))], axis=1)
+    others = [swap_core(v, n_col) for v in pruned]
+    pruned_panel = jnp.concatenate([x for pair in zip(pruned, others) for x in pair], axis=1)
     return updated(weight, mask, pruned_panel, pieces)
 
 

time: 159 us -> 159 us (level)
  the two profiles are of different devices: /device:TPU:24 before, /device:TPU:0 now
where the time goes in v4:
time: 159 us; the launch traced here: 158 us
  waiting for transfers between devices  70.3 us (44%)
  starting transfers between devices  48.6 us (31%)
  Pallas kernels  27.5 us (17%)
  local copies, waits for them, and re-layouts  10.8 us (7%)
    ppermute x27, waiting for transfers between devices, swap_tok(): return lax.ppermute(x, 'tok', [(i, i ^ bit) for i in range(n_tok)])  46.5 us
    ppermute x27, starting transfers between devices, swap_tok(): return lax.ppermute(x, 'tok', [(i, i ^ bit) for i in range(n_tok)])  30.3 us
    ppermute x6, waiting for transfers between devices, shift_chip(): lax.ppermute(x, 'col', [(i, (i + 2 * step) % n_col) for i in range(n_col)])  23.3 us
    ppermute x6, starting transfers between devices, shift_chip(): lax.ppermute(x, 'col', [(i, (i + 2 * step) % n_col) for i in range(n_col)])  17.3 us
    pallas_call x1, Pallas kernels, inverse(): pl.pallas_call(functools.partial(inverse_kernel, width, len(own)), out_sh...  9.83 us
    unnamed x17, local copies, waits for them, and re-layouts  9.46 us
    pallas_call x2, Pallas kernels, update(): pl.pallas_call(functools.partial(update_kernel, runs, counts), out_shape=...  7.13 us
    pallas_call x7, Pallas kernels, panel_products(): pl.pallas_call(functools.partial(panel_kernel, runs), out_shape=[jax.Shap...  5.86 us
  transfers between devices with their start and end apart: 43, of which 15 were waited for; matrix products, arithmetic and copies ran while one was open for 1% of the time, Pallas kernels for 16%

profile of v4, /device:TPU:0, one launch (start us, length us, event | category | flops | bytes accessed | tf_op | source)
XLA Modules:
  0.0 158.3 jit_solution(3835936331654762401)
XLA Ops:
  1.1 3.1 %collective-permute-start.12 = (bf16[2048,128]{1,0:T(8,128)(2,1)S(1)}, bf16[2048,128]{1,0:T(8,128)(2,1)S(1)}, u32[]{:S(2)}, u32[]{:S(2)}) collective-permute-start(bf16[2048,128]{1,0:T(8,128)(2,1)S(1)} %slice.51.refs_0_), channel_id=1, source_target_pairs={{0,2},{1,3},{2,4},{3,5},{4,6},{5,7},{6,0},{7,1},{8,10},{9,11},{10,... | collective-permute-start | bytes 1572872 | tf_op jit(solution)/shard_map/ppermute | solution.py:18
  4.2 2.2 %copy-done = bf16[2048,1024]{1,0:T(8,128)(2,1)S(1)} copy-done((bf16[2048,1024]{1,0:T(8,128)(2,1)S(1)}, bf16[2048,1024]{1,0:T(8,128)(2,1)}, u32[]{:S(2)}) %copy-start) | copy-done | bytes 4194328
  7.1 1.6 %collective-permute-start.7 = (f32[128,512]{1,0:T(8,128)S(1)}, f32[128,512]{1,0:T(8,128)S(1)}, u32[]{:S(2)}, u32[]{:S(2)}) collective-permute-start(f32[128,512]{1,0:T(8,128)S(1)} %get-tuple-element.26), channel_id=1, source_target_pairs={{0,8},{8,0},{16,24},{24,16},{1,9},{9,1},{17,25},{25,17},{2,10},{10... | collective-permute-start | bytes 786440 | tf_op jit(solution)/shard_map/ppermute | solution.py:26
  8.7 2.2 %collective-permute-start.18 = (bf16[2048,128]{1,0:T(8,128)(2,1)S(1)}, bf16[2048,128]{1,0:T(8,128)(2,1)S(1)}, u32[]{:S(2)}, u32[]{:S(2)}) collective-permute-start(bf16[2048,128]{1,0:T(8,128)(2,1)S(1)} %slice.51.refs_0_), channel_id=1, source_target_pairs={{0,6},{1,7},{2,0},{3,1},{4,2},{5,3},{6,4},{7,5},{8,14},{9,15},{10,... | collective-permute-start | bytes 1572872 | tf_op jit(solution)/shard_map/ppermute | solution.py:18
  11.0 3.4 %copy-done.3 = s32[2048,1024]{1,0:T(8,128)S(1)} copy-done((s32[2048,1024]{1,0:T(8,128)S(1)}, s32[2048,1024]{1,0:T(8,128)}, u32[]{:S(2)}) %copy-start.3) | copy-done | bytes 8388632
  15.0 2.7 %copy-done.4 = s32[2048,1024]{1,0:T(8,128)S(1)} copy-done((s32[2048,1024]{1,0:T(8,128)S(1)}, s32[2048,1024]{1,0:T(8,128)}, u32[]{:S(2)}) %copy-start.4) | copy-done | bytes 8388632
  19.0 11.4 %collective-permute-start.3 = (bf16[2048,128]{1,0:T(8,128)(2,1)S(1)}, bf16[2048,128]{1,0:T(8,128)(2,1)S(1)}, u32[]{:S(2)}, u32[]{:S(2)}) collective-permute-start(bf16[2048,128]{1,0:T(8,128)(2,1)S(1)} %pruned_columns.1), channel_id=1, source_target_pairs={{0,6},{1,7},{2,0},{3,1},{4,2},{5,3},{6,4},{7,5},{8,14},{9,15},{10,... | collective-permute-start | bytes 1572872 | tf_op jit(solution)/shard_map/ppermute | solution.py:18
  33.5 1.6 %collective-permute-start.10 = (f32[128,512]{1,0:T(8,128)S(1)}, f32[128,512]{1,0:T(8,128)S(1)}, u32[]{:S(2)}, u32[]{:S(2)}) collective-permute-start(f32[128,512]{1,0:T(8,128)S(1)} %get-tuple-element.28), channel_id=1, source_target_pairs={{0,16},{8,24},{16,0},{24,8},{1,17},{9,25},{17,1},{25,9},{2,18},{10... | collective-permute-start | bytes 786440 | tf_op jit(solution)/shard_map/ppermute | solution.py:26
  36.7 4.9 %collective-permute-done.1 = bf16[2048,128]{1,0:T(8,128)(2,1)S(1)} collective-permute-done((bf16[2048,128]{1,0:T(8,128)(2,1)S(1)}, bf16[2048,128]{1,0:T(8,128)(2,1)S(1)}, u32[]{:S(2)}, u32[]{:S(2)}) %collective-permute-start.1) | collective-permute-done | bytes 524320 | tf_op jit(solution)/shard_map/ppermute | solution.py:18
  43.7 1.7 %collective-permute-start.8 = (f32[128,256]{1,0:T(8,128)S(1)}, f32[128,256]{1,0:T(8,128)S(1)}, u32[]{:S(2)}, u32[]{:S(2)}) collective-permute-start(f32[128,256]{1,0:T(8,128)S(1)} %slice_add_fusion.5), channel_id=1, source_target_pairs={{0,16},{8,24},{16,0},{24,8},{1,17},{9,25},{17,1},{25,9},{2,18},{10... | collective-permute-start | bytes 393224 | tf_op jit(solution)/shard_map/ppermute | solution.py:26
  46.9 5.7 %collective-permute-done.3 = bf16[2048,128]{1,0:T(8,128)(2,1)S(1)} collective-permute-done((bf16[2048,128]{1,0:T(8,128)(2,1)S(1)}, bf16[2048,128]{1,0:T(8,128)(2,1)S(1)}, u32[]{:S(2)}, u32[]{:S(2)}) %collective-permute-start.3) | collective-permute-done | bytes 524320 | tf_op jit(solution)/shard_map/ppermute | solution.py:18
  53.4 12.1 %collective-permute-done.24.refs_6_.refs_0_ = bf16[2048,128]{1,0:T(8,128)(2,1)S(1)} collective-permute-done((bf16[2048,128]{1,0:T(8,128)(2,1)S(1)}, bf16[2048,128]{1,0:T(8,128)(2,1)S(1)}, u32[]{:S(2)}, u32[]{:S(2)}) %collective-permute-start.24) | collective-permute-done | bytes 524320 | tf_op jit(solution)/shard_map/ppermute | solution.py:18
  72.7 6.2 %collective-permute-done.31 = bf16[128,896]{1,0:T(8,128)(2,1)S(1)} collective-permute-done((bf16[128,896]{1,0:T(8,128)(2,1)S(1)}, bf16[128,896]{1,0:T(8,128)(2,1)S(1)}, u32[]{:S(2)}, u32[]{:S(2)}) %collective-permute-start.31) | collective-permute-done | bytes 229408 | tf_op jit(solution)/shard_map/ppermute | solution.py:26
  79.5 2.7 %collective-permute-done.33 = bf16[128,896]{1,0:T(8,128)(2,1)S(1)} collective-permute-done((bf16[128,896]{1,0:T(8,128)(2,1)S(1)}, bf16[128,896]{1,0:T(8,128)(2,1)S(1)}, u32[]{:S(2)}, u32[]{:S(2)}) %collective-permute-start.33) | collective-permute-done | bytes 229408 | tf_op jit(solution)/shard_map/ppermute | solution.py:26
  84.4 10.6 %collective-permute-done.32 = bf16[128,896]{1,0:T(8,128)(2,1)S(1)} collective-permute-done((bf16[128,896]{1,0:T(8,128)(2,1)S(1)}, bf16[128,896]{1,0:T(8,128)(2,1)S(1)}, u32[]{:S(2)}, u32[]{:S(2)}) %collective-permute-start.32) | collective-permute-done | bytes 229408 | tf_op jit(solution)/shard_map/ppermute | solution.py:26
  95.6 5.8 %collective-permute-done.34 = bf16[128,896]{1,0:T(8,128)(2,1)S(1)} collective-permute-done((bf16[128,896]{1,0:T(8,128)(2,1)S(1)}, bf16[128,896]{1,0:T(8,128)(2,1)S(1)}, u32[]{:S(2)}, u32[]{:S(2)}) %collective-permute-start.34) | collective-permute-done | bytes 229408 | tf_op jit(solution)/shard_map/ppermute | solution.py:26
  103.0 4.0 %collective-permute-done.30 = bf16[128,768]{1,0:T(8,128)(2,1)S(1)} collective-permute-done((bf16[128,768]{1,0:T(8,128)(2,1)S(1)}, bf16[128,768]{1,0:T(8,128)(2,1)S(1)}, u32[]{:S(2)}, u32[]{:S(2)}) %collective-permute-start.30) | collective-permute-done | bytes 196640 | tf_op jit(solution)/shard_map/ppermute | solution.py:26
  110.6 2.5 %collective-permute-done.11.refs_5_ = f32[128,256]{1,0:T(8,128)S(1)} collective-permute-done((f32[128,256]{1,0:T(8,128)S(1)}, f32[128,256]{1,0:T(8,128)S(1)}, u32[]{:S(2)}, u32[]{:S(2)}) %collective-permute-start.11) | collective-permute-done | bytes 131104 | tf_op jit(solution)/shard_map/ppermute | solution.py:26
  118.7 9.8 %inverse.1 = (bf16[1024,1024]{1,0:T(8,128)(2,1)S(1)}, bf16[1024,1024]{1,0:T(8,128)(2,1)S(1)}, f32[8,128]{1,0:T(8,128)S(1)}) custom-call(bf16[128,768]{1,0:T(8,128)(2,1)S(1)} %add_convert_fusion.4.refs_0_, bf16[128,1792]{1,0:T(8,128)(2,1)S(1)} %pad_maximum_fusion.refs_1_, bf16[128,768]{1,0:T(8,128)(2,1)S(1)} %collective-permute-done.35.refs_2_, ...), custom_call_target="tpu_custom_call" | custom-call | flops 12884901888 | bytes 8388608 | tf_op jit(solution)/shard_map/inverse/pallas_call | solution.py:236
  128.6 4.6 %collective-permute-done.28.refs_21_ = f32[256,256]{1,0:T(8,128)S(1)} collective-permute-done((f32[256,256]{1,0:T(8,128)S(1)}, f32[256,256]{1,0:T(8,128)S(1)}, u32[]{:S(2)}, u32[]{:S(2)}) %collective-permute-start.28) | collective-permute-done | bytes 262176 | tf_op jit(solution)/shard_map/ppermute | solution.py:26
  133.2 1.9 %solve_rows.1.rest_0_ = bf16[1024,256]{1,0:T(8,128)(2,1)S(1)} custom-call(f32[128,512]{1,0:T(8,128)S(1)} %get-tuple-element.25.refs_0_, f32[128,512]{1,0:T(8,128)S(1)} %collective-permute-done.7.refs_1_, f32[128,256]{1,0:T(8,128)S(1)} %collective-permute-done.8.refs_2_, f32[128,512]{1,0:T(8,128)S(1)} %get-tuple-element.27.refs_3_, ...), custom_call_target="tpu_custom_call" | custom-call | flops 1610612736 | bytes 4194304 | tf_op jit(solution)/shard_map/solve_rows/pallas_call | solution.py:279
  139.6 8.4 %collective-permute-done.37.rest_1_ = bf16[512,256]{1,0:T(8,128)(2,1)S(1)} collective-permute-done((bf16[512,256]{1,0:T(8,128)(2,1)S(1)}, bf16[512,256]{1,0:T(8,128)(2,1)S(1)}, u32[]{:S(2)}, u32[]{:S(2)}) %collective-permute-start.37) | collective-permute-done | bytes 262176 | tf_op jit(solution)/shard_map/ppermute | solution.py:26
  150.1 4.9 %update.2.rest_2_ = bf16[2048,1024]{1,0:T(8,128)(2,1)} custom-call(s32[1]{0:T(128)} %bitcast.index_ref, bf16[2048,1024]{1,0:T(8,128)(2,1)S(1)} %copy-done.2, bf16[2048,1024]{1,0:T(8,128)(2,1)S(1)} %narrowed.1.mask_ref, bf16[2048,1024]{1,0:T(8,128)(2,1)S(1)} %constant_dynamic-update-slice_fusion.pruned_ref, bf16[1024,256]{1,0:T(8,128)(2,1)S(1)} %solve_rows.1.rest_0_, ...), custom_call_target="tpu_custom_call" | custom-call | flops 3221225472 | bytes 9437184 | tf_op jit(solution)/shard_map/update/pallas_call | solution.py:365
  155.9 2.2 %update.3 = bf16[2048,1024]{1,0:T(8,128)(2,1)} custom-call(s32[1]{0:T(128)} %bitcast.index_ref, bf16[2048,1024]{1,0:T(8,128)(2,1)S(1)} %copy-done.2, bf16[2048,1024]{1,0:T(8,128)(2,1)S(1)} %narrowed.1.mask_ref, bf16[2048,1024]{1,0:T(8,128)(2,1)S(1)} %constant_dynamic-update-slice_fusion.pruned_ref, ...), custom_call_target="tpu_custom_call", output_to_operand_aliasing={{}: (6, {})} | custom-call | flops 1073741824 | bytes 3145728 | tf_op jit(solution)/shard_map/update/pallas_call | solution.py:365
  (110 shorter events, 41.5 us)
Async XLA Ops:
  1.1 17.9 %collective-permute-start.12 = (bf16[2048,128]{1,0:T(8,128)(2,1)S(1)}, bf16[2048,128]{1,0:T(8,128)(2,1)S(1)}, u32[]{:S(2)}, u32[]{:S(2)}) collective-permute-start(bf16[2048,128]{1,0:T(8,128)(2,1)S(1)} %slice.51.refs_0_), channel_id=1, source_target_pairs={{0,2},{1,3},{2,4},{3,5},{4,6},{5,7},{6,0},{7,1},{8,10},{9,11},{10,... | collective-permute-start | bytes 1572872 | tf_op jit(solution)/shard_map/ppermute | solution.py:18
  8.7 22.4 %collective-permute-start.9 = (bf16[2048,128]{1,0:T(8,128)(2,1)S(1)}, bf16[2048,128]{1,0:T(8,128)(2,1)S(1)}, u32[]{:S(2)}, u32[]{:S(2)}) collective-permute-start(bf16[2048,128]{1,0:T(8,128)(2,1)S(1)} %slice.51.refs_0_), channel_id=1, source_target_pairs={{0,1},{1,0},{2,3},{3,2},{4,5},{5,4},{6,7},{7,6},{8,9},{9,8},{10,11... | collective-permute-start | bytes 1572872 | tf_op jit(solution)/shard_map/ppermute | solution.py:22
  8.7 24.8 %collective-permute-start.18 = (bf16[2048,128]{1,0:T(8,128)(2,1)S(1)}, bf16[2048,128]{1,0:T(8,128)(2,1)S(1)}, u32[]{:S(2)}, u32[]{:S(2)}) collective-permute-start(bf16[2048,128]{1,0:T(8,128)(2,1)S(1)} %slice.51.refs_0_), channel_id=1, source_target_pairs={{0,6},{1,7},{2,0},{3,1},{4,2},{5,3},{6,4},{7,5},{8,14},{9,15},{10,... | collective-permute-start | bytes 1572872 | tf_op jit(solution)/shard_map/ppermute | solution.py:18
  14.7 21.1 %collective-permute-start = (bf16[2048,128]{1,0:T(8,128)(2,1)S(1)}, bf16[2048,128]{1,0:T(8,128)(2,1)S(1)}, u32[]{:S(2)}, u32[]{:S(2)}) collective-permute-start(bf16[2048,128]{1,0:T(8,128)(2,1)S(1)} %pruned_columns.1), channel_id=1, source_target_pairs={{0,1},{1,0},{2,3},{3,2},{4,5},{5,4},{6,7},{7,6},{8,9},{9,8},{10,11... | collective-permute-start | bytes 1572872 | tf_op jit(solution)/shard_map/ppermute | solution.py:22
  18.3 23.2 %collective-permute-start.1 = (bf16[2048,128]{1,0:T(8,128)(2,1)S(1)}, bf16[2048,128]{1,0:T(8,128)(2,1)S(1)}, u32[]{:S(2)}, u32[]{:S(2)}) collective-permute-start(bf16[2048,128]{1,0:T(8,128)(2,1)S(1)} %pruned_columns.1), channel_id=1, source_target_pairs={{0,2},{1,3},{2,4},{3,5},{4,6},{5,7},{6,0},{7,1},{8,10},{9,11},{10,... | collective-permute-start | bytes 1572872 | tf_op jit(solution)/shard_map/ppermute | solution.py:18
  19.0 33.6 %collective-permute-start.3 = (bf16[2048,128]{1,0:T(8,128)(2,1)S(1)}, bf16[2048,128]{1,0:T(8,128)(2,1)S(1)}, u32[]{:S(2)}, u32[]{:S(2)}) collective-permute-start(bf16[2048,128]{1,0:T(8,128)(2,1)S(1)} %pruned_columns.1), channel_id=1, source_target_pairs={{0,6},{1,7},{2,0},{3,1},{4,2},{5,3},{6,4},{7,5},{8,14},{9,15},{10,... | collective-permute-start | bytes 1572872 | tf_op jit(solution)/shard_map/ppermute | solution.py:18
  41.5 24.0 %collective-permute-start.24 = (bf16[2048,128]{1,0:T(8,128)(2,1)S(1)}, bf16[2048,128]{1,0:T(8,128)(2,1)S(1)}, u32[]{:S(2)}, u32[]{:S(2)}) collective-permute-start(bf16[2048,128]{1,0:T(8,128)(2,1)S(1)} %collective-permute-done.12.refs_0_.refs_2_), channel_id=1, source_target_pairs={{0,2},{1,3},{2,4},{3,5},{4,6},{5,7},{6,0},{7,1},{8,10},{9,11},{10,... | collective-permute-start | bytes 1572872 | tf_op jit(solution)/shard_map/ppermute | solution.py:18
  41.9 11.3 %collective-permute-start.2 = (bf16[2048,128]{1,0:T(8,128)(2,1)S(1)}, bf16[2048,128]{1,0:T(8,128)(2,1)S(1)}, u32[]{:S(2)}, u32[]{:S(2)}) collective-permute-start(bf16[2048,128]{1,0:T(8,128)(2,1)S(1)} %collective-permute-done.1), channel_id=1, source_target_pairs={{0,1},{1,0},{2,3},{3,2},{4,5},{5,4},{6,7},{7,6},{8,9},{9,8},{10,11... | collective-permute-start | bytes 1572872 | tf_op jit(solution)/shard_map/ppermute | solution.py:22
  43.2 23.8 %collective-permute-start.21 = (bf16[2048,128]{1,0:T(8,128)(2,1)S(1)}, bf16[2048,128]{1,0:T(8,128)(2,1)S(1)}, u32[]{:S(2)}, u32[]{:S(2)}) collective-permute-start(bf16[2048,128]{1,0:T(8,128)(2,1)S(1)} %collective-permute-done.18.refs_0_.refs_4_), channel_id=1, source_target_pairs={{0,1},{1,0},{2,3},{3,2},{4,5},{5,4},{6,7},{7,6},{8,9},{9,8},{10,11... | collective-permute-start | bytes 1572872 | tf_op jit(solution)/shard_map/ppermute | solution.py:22
  43.7 63.4 %collective-permute-start.8 = (f32[128,256]{1,0:T(8,128)S(1)}, f32[128,256]{1,0:T(8,128)S(1)}, u32[]{:S(2)}, u32[]{:S(2)}) collective-permute-start(f32[128,256]{1,0:T(8,128)S(1)} %slice_add_fusion.5), channel_id=1, source_target_pairs={{0,16},{8,24},{16,0},{24,8},{1,17},{9,25},{17,1},{25,9},{2,18},{10... | collective-permute-start | bytes 393224 | tf_op jit(solution)/shard_map/ppermute | solution.py:26
  52.6 62.6 %collective-permute-start.5 = (bf16[2048,128]{1,0:T(8,128)(2,1)S(1)}, bf16[2048,128]{1,0:T(8,128)(2,1)S(1)}, u32[]{:S(2)}, u32[]{:S(2)}) collective-permute-start(bf16[2048,128]{1,0:T(8,128)(2,1)S(1)} %collective-permute-done.1), channel_id=1, source_target_pairs={{0,2},{1,3},{2,4},{3,5},{4,6},{5,7},{6,0},{7,1},{8,10},{9,11},{10,... | collective-permute-start | bytes 1572872 | tf_op jit(solution)/shard_map/ppermute | solution.py:18
  53.2 14.8 %collective-permute-start.4 = (bf16[2048,128]{1,0:T(8,128)(2,1)S(1)}, bf16[2048,128]{1,0:T(8,128)(2,1)S(1)}, u32[]{:S(2)}, u32[]{:S(2)}) collective-permute-start(bf16[2048,128]{1,0:T(8,128)(2,1)S(1)} %collective-permute-done.3), channel_id=1, source_target_pairs={{0,1},{1,0},{2,3},{3,2},{4,5},{5,4},{6,7},{7,6},{8,9},{9,8},{10,11... | collective-permute-start | bytes 1572872 | tf_op jit(solution)/shard_map/ppermute | solution.py:22
  68.0 15.8 %collective-permute-start.16 = (f32[128,512]{1,0:T(8,128)S(1)}, f32[128,512]{1,0:T(8,128)S(1)}, u32[]{:S(2)}, u32[]{:S(2)}) collective-permute-start(f32[128,512]{1,0:T(8,128)S(1)} %get-tuple-element.32), channel_id=1, source_target_pairs={{0,16},{8,24},{16,0},{24,8},{1,17},{9,25},{17,1},{25,9},{2,18},{10... | collective-permute-start | bytes 786440 | tf_op jit(solution)/shard_map/ppermute | solution.py:26
  78.9 28.8 %collective-permute-start.14 = (f32[128,256]{1,0:T(8,128)S(1)}, f32[128,256]{1,0:T(8,128)S(1)}, u32[]{:S(2)}, u32[]{:S(2)}) collective-permute-start(f32[128,256]{1,0:T(8,128)S(1)} %slice_add_fusion.3), channel_id=1, source_target_pairs={{0,16},{8,24},{16,0},{24,8},{1,17},{9,25},{17,1},{25,9},{2,18},{10... | collective-permute-start | bytes 393224 | tf_op jit(solution)/shard_map/ppermute | solution.py:26
  82.1 27.1 %collective-permute-start.22 = (f32[128,512]{1,0:T(8,128)S(1)}, f32[128,512]{1,0:T(8,128)S(1)}, u32[]{:S(2)}, u32[]{:S(2)}) collective-permute-start(f32[128,512]{1,0:T(8,128)S(1)} %get-tuple-element.36), channel_id=1, source_target_pairs={{0,16},{8,24},{16,0},{24,8},{1,17},{9,25},{17,1},{25,9},{2,18},{10... | collective-permute-start | bytes 786440 | tf_op jit(solution)/shard_map/ppermute | solution.py:26
  113.1 15.4 %collective-permute-start.17 = (f32[128,256]{1,0:T(8,128)S(1)}, f32[128,256]{1,0:T(8,128)S(1)}, u32[]{:S(2)}, u32[]{:S(2)}) collective-permute-start(f32[128,256]{1,0:T(8,128)S(1)} %slice_add_fusion.2), channel_id=1, source_target_pairs={{0,8},{8,0},{16,24},{24,16},{1,9},{9,1},{17,25},{25,17},{2,10},{10... | collective-permute-start | bytes 393224 | tf_op jit(solution)/shard_map/ppermute | solution.py:26
  113.7 14.9 %collective-permute-start.23 = (f32[128,256]{1,0:T(8,128)S(1)}, f32[128,256]{1,0:T(8,128)S(1)}, u32[]{:S(2)}, u32[]{:S(2)}) collective-permute-start(f32[128,256]{1,0:T(8,128)S(1)} %slice_add_fusion), channel_id=1, source_target_pairs={{0,8},{8,0},{16,24},{24,16},{1,9},{9,1},{17,25},{25,17},{2,10},{10... | collective-permute-start | bytes 393224 | tf_op jit(solution)/shard_map/ppermute | solution.py:26
  115.2 13.4 %collective-permute-start.26 = (f32[256,256]{1,0:T(8,128)S(1)}, f32[256,256]{1,0:T(8,128)S(1)}, u32[]{:S(2)}, u32[]{:S(2)}) collective-permute-start(f32[256,256]{1,0:T(8,128)S(1)} %get-tuple-element.39), channel_id=1, source_target_pairs={{0,8},{8,0},{16,24},{24,16},{1,9},{9,1},{17,25},{25,17},{2,10},{10... | collective-permute-start | bytes 786440 | tf_op jit(solution)/shard_map/ppermute | solution.py:26
  115.7 12.9 %collective-permute-start.27 = (f32[256,256]{1,0:T(8,128)S(1)}, f32[256,256]{1,0:T(8,128)S(1)}, u32[]{:S(2)}, u32[]{:S(2)}) collective-permute-start(f32[256,256]{1,0:T(8,128)S(1)} %get-tuple-element.40), channel_id=1, source_target_pairs={{0,16},{8,24},{16,0},{24,8},{1,17},{9,25},{17,1},{25,9},{2,18},{10... | collective-permute-start | bytes 786440 | tf_op jit(solution)/shard_map/ppermute | solution.py:26
  117.2 15.9 %collective-permute-start.28 = (f32[256,256]{1,0:T(8,128)S(1)}, f32[256,256]{1,0:T(8,128)S(1)}, u32[]{:S(2)}, u32[]{:S(2)}) collective-permute-start(f32[256,256]{1,0:T(8,128)S(1)} %get-tuple-element.41), channel_id=1, source_target_pairs={{0,24},{8,16},{16,8},{24,0},{1,25},{9,17},{17,9},{25,1},{2,26},{10... | collective-permute-start | bytes 786440 | tf_op jit(solution)/shard_map/ppermute | solution.py:26
  135.1 14.4 %collective-permute-start.39 = (bf16[512,256]{1,0:T(8,128)(2,1)S(1)}, bf16[512,256]{1,0:T(8,128)(2,1)S(1)}, u32[]{:S(2)}, u32[]{:S(2)}) collective-permute-start(bf16[512,256]{1,0:T(8,128)(2,1)S(1)} %get-tuple-element.45), channel_id=1, source_target_pairs={{0,16},{8,24},{16,0},{24,8},{1,17},{9,25},{17,1},{25,9},{2,18},{10... | collective-permute-start | bytes 786440 | tf_op jit(solution)/shard_map/ppermute | solution.py:26
  135.7 14.4 %collective-permute-start.41 = (bf16[512,256]{1,0:T(8,128)(2,1)S(1)}, bf16[512,256]{1,0:T(8,128)(2,1)S(1)}, u32[]{:S(2)}, u32[]{:S(2)}) collective-permute-start(bf16[512,256]{1,0:T(8,128)(2,1)S(1)} %get-tuple-element.45), channel_id=1, source_target_pairs={{0,8},{8,0},{16,24},{24,16},{1,9},{9,1},{17,25},{25,17},{2,10},{10... | collective-permute-start | bytes 786440 | tf_op jit(solution)/shard_map/ppermute | solution.py:26
  136.2 11.8 %collective-permute-start.37 = (bf16[512,256]{1,0:T(8,128)(2,1)S(1)}, bf16[512,256]{1,0:T(8,128)(2,1)S(1)}, u32[]{:S(2)}, u32[]{:S(2)}) collective-permute-start(bf16[512,256]{1,0:T(8,128)(2,1)S(1)} %get-tuple-element.46), channel_id=1, source_target_pairs={{0,8},{8,0},{16,24},{24,16},{1,9},{9,1},{17,25},{25,17},{2,10},{10... | collective-permute-start | bytes 786440 | tf_op jit(solution)/shard_map/ppermute | solution.py:26
  137.7 12.4 %collective-permute-start.42 = (bf16[512,256]{1,0:T(8,128)(2,1)S(1)}, bf16[512,256]{1,0:T(8,128)(2,1)S(1)}, u32[]{:S(2)}, u32[]{:S(2)}) collective-permute-start(bf16[512,256]{1,0:T(8,128)(2,1)S(1)} %get-tuple-element.46), channel_id=1, source_target_pairs={{0,16},{8,24},{16,0},{24,8},{1,17},{9,25},{17,1},{25,9},{2,18},{10... | collective-permute-start | bytes 786440 | tf_op jit(solution)/shard_map/ppermute | solution.py:26
  (24 other events, 171.8 us)

commit v5 on v4

--- a/solution.py
+++ b/solution.py
@@ -27,10 +27,6 @@
 
 
 TRANSPOSED = (((0,), (0,)), ((), ()))
-
-
-def after(x, *others):
-    return lax.optimization_barrier((x, *others))[0]
 
 
 def joined(xs):
@@ -447,25 +443,31 @@
     part_2 = second_step(kept, over(sent, y), x)
 
     panels += [second, swapped(second)]
+    rows_2 = block_rows(panels, (2,))
+    middle = rows_2.shape[1] // 2
+    left, right = rows_2[:, :middle], rows_2[:, middle:]
+    left = added(left, over(left, x))
+    right = added(right, over(right, y))
+    left = added(left, over(left, y))
+    right = added(right, over(right, x))
+    sum_2 = jnp.concatenate([left, right], axis=1)
     sent, kept = panel_products(panels[4:5], activations, halving(bits))
     part_3 = second_step(kept, over(sent, x), y)
     sent, kept = panel_products(panels[5:], activations, halving(turned))
     part_4 = second_step(kept, over(sent, y), x)
 
     panels += [third, swapped(third)]
-    rows_3 = block_rows(panels, (2, 3))
-    middle = rows_3.shape[1] // 2
-    left, right = rows_3[:, :middle], rows_3[:, middle:]
-    left = added(left, over(left, x))
-    right = added(right, over(right, y))
-    sum_3 = [added(left, over(left, y)), added(right, over(right, x))]
+    width = 2 * own.shape[1]
+    behind = shift_chip(sum_2, n_col, -1)
+    before = shift_chip(sum_1[:, width : 2 * width], n_col, 1)
+    sum_3 = [behind[:, width : 2 * width], before, behind[:, :width], behind[:, 2 * width :]]
     sum_3 = jnp.concatenate(sum_3, axis=1)
-    products = panel_products(panels[6:], after(activations, rows_3), ((0,), (1,), (2,), (3,)))
+    products = panel_products(panels[6:], activations, ((0,), (1,), (2,), (3,)))
     part_5 = [products[0]] + [over(products[m], m) for m in (x, y, x | y)]
 
-    sums = [sum_1, sum_3]
+    sums = [sum_1, sum_2, sum_3]
     others = [swapped(v) for v in sums]
-    return sums, others, [part_0, part_0b, part_1, part_2, part_3, part_4, part_5], rows_3
+    return sums, others, [part_0, part_0b, part_1, part_2, part_3, part_4, part_5], sum_3
 
 
 def per_device(activations, weight, keep_mask):
@@ -482,12 +484,14 @@
     solved = solve_rows(parts, v_hi, v_lo, scale)
     pieces = gather_tok(solved, n_tok)
 
-    pruned = pruned_columns(weight, keep_mask, panel_width)
     mask = narrowed(keep_mask)
+    pruned = pruned_columns(weight, mask, panel_width)
     if chips == 4:
         second = shift_chip(pruned, n_col, 1)
         third = shift_chip(second, n_col, 1)
-        pruned = [pruned, second, shift_chip(pruned, n_col, -1), third]
+        half = pruned.shape[0] // 2
+        fourth = [shift_chip(pruned[:half], n_col, -1), shift_chip(pruned[half:], n_col, -1)]
+        pruned = [pruned, second, jnp.concatenate(fourth, axis=0), third]
     else:
         pruned = [pruned] + [shift_chip(pruned, n_col, k) for k in range(1, chips)]
     others = [swap_core(v, n_col) for v in pruned]

time: 159 us -> 155 us (0.975)
  waiting for transfers between devices: 70.3 us -> 65.3 us
  starting transfers between devices: 48.6 us -> 51.7 us
    ppermute x27, waiting for transfers between devices: 46.5 us -> 33.5 us  [swap_tok(): return lax.ppermute(x, 'tok', [(i, i ^ bit) for i in range(n_tok)])]
    ppermute x6 -> x9, waiting for transfers between devices: 23.3 us -> 30.7 us  [shift_chip(): lax.ppermute(x, 'col', [(i, (i + 2 * step) % n_col) for i in range(n_col)])]
    ppermute x27, starting transfers between devices: 30.3 us -> 36.5 us  [swap_tok(): return lax.ppermute(x, 'tok', [(i, i ^ bit) for i in range(n_tok)])]
    ppermute x6 -> x9, starting transfers between devices: 17.3 us -> 13.3 us  [shift_chip(): lax.ppermute(x, 'col', [(i, (i + 2 * step) % n_col) for i in range(n_col)])]
    unnamed x17 -> x22, local copies, waits for them, and re-layouts: 9.46 us -> 8.3 us
  transfers between devices with their start and end apart: 43 -> 47, of which waited for: 15 -> 17; matrix products, arithmetic and copies ran while one was open for 1% -> 1% of each run, Pallas kernels for 16% -> 16%
where the time goes in v5:
time: 155 us
  waiting for transfers between devices  65.3 us (42%)
  starting transfers between devices  51.7 us (33%)
  Pallas kernels  26.9 us (17%)
  local copies, waits for them, and re-layouts  9.66 us (6%)
    ppermute x27, starting transfers between devices, swap_tok(): return lax.ppermute(x, 'tok', [(i, i ^ bit) for i in range(n_tok)])  36.5 us
    ppermute x27, waiting for transfers between devices, swap_tok(): return lax.ppermute(x, 'tok', [(i, i ^ bit) for i in range(n_tok)])  33.5 us
    ppermute x9, waiting for transfers between devices, shift_chip(): lax.ppermute(x, 'col', [(i, (i + 2 * step) % n_col) for i in range(n_col)])  30.7 us
    ppermute x9, starting transfers between devices, shift_chip(): lax.ppermute(x, 'col', [(i, (i + 2 * step) % n_col) for i in range(n_col)])  13.3 us
    pallas_call x1, Pallas kernels, inverse(): pl.pallas_call(functools.partial(inverse_kernel, width, len(own)), out_sh...  9.59 us
    unnamed x22, local copies, waits for them, and re-layouts  8.3 us
    pallas_call x2, Pallas kernels, update(): pl.pallas_call(functools.partial(update_kernel, runs, counts), out_shape=...  7.15 us
    pallas_call x7, Pallas kernels, panel_products(): pl.pallas_call(functools.partial(panel_kernel, runs), out_shape=[jax.Shap...  5.84 us
  transfers between devices with their start and end apart: 47, of which 17 were waited for; matrix products, arithmetic and copies ran while one was open for 1% of the time, Pallas kernels for 16%

profile of v5, /device:TPU:0, one launch (start us, length us, event | category | flops | bytes accessed | tf_op | source)
XLA Modules:
  0.0 154.7 jit_solution(14535000654875297711)
XLA Ops:
  1.1 3.1 %collective-permute-start.13 = (bf16[2048,128]{1,0:T(8,128)(2,1)S(1)}, bf16[2048,128]{1,0:T(8,128)(2,1)S(1)}, u32[]{:S(2)}, u32[]{:S(2)}) collective-permute-start(bf16[2048,128]{1,0:T(8,128)(2,1)S(1)} %slice.71.refs_0_), channel_id=1, source_target_pairs={{0,2},{1,3},{2,4},{3,5},{4,6},{5,7},{6,0},{7,1},{8,10},{9,11},{10,... | collective-permute-start | bytes 1572872 | tf_op jit(solution)/shard_map/ppermute | solution.py:18
  4.2 3.4 %copy-done.6 = s32[2048,1024]{1,0:T(8,128)S(1)} copy-done((s32[2048,1024]{1,0:T(8,128)S(1)}, s32[2048,1024]{1,0:T(8,128)}, u32[]{:S(2)}) %copy-start.6) | copy-done | bytes 8388632
  10.1 2.7 %collective-permute-start.3 = (bf16[1024,128]{1,0:T(8,128)(2,1)S(1)}, bf16[1024,128]{1,0:T(8,128)(2,1)S(1)}, u32[]{:S(2)}, u32[]{:S(2)}) collective-permute-start(bf16[1024,128]{1,0:T(8,128)(2,1)S(1)} %get-tuple-element.46), channel_id=1, source_target_pairs={{0,6},{1,7},{2,0},{3,1},{4,2},{5,3},{6,4},{7,5},{8,14},{9,15},{10,... | collective-permute-start | bytes 786440 | tf_op jit(solution)/shard_map/ppermute | solution.py:18
  14.2 2.2 %copy-done = bf16[2048,1024]{1,0:T(8,128)(2,1)S(1)} copy-done((bf16[2048,1024]{1,0:T(8,128)(2,1)S(1)}, bf16[2048,1024]{1,0:T(8,128)(2,1)}, u32[]{:S(2)}) %copy-start) | copy-done | bytes 4194328
  18.9 4.9 %collective-permute-done.3 = bf16[1024,128]{1,0:T(8,128)(2,1)S(1)} collective-permute-done((bf16[1024,128]{1,0:T(8,128)(2,1)S(1)}, bf16[1024,128]{1,0:T(8,128)(2,1)S(1)}, u32[]{:S(2)}, u32[]{:S(2)}) %collective-permute-start.3) | collective-permute-done | bytes 262176 | tf_op jit(solution)/shard_map/ppermute | solution.py:18
  23.8 2.7 %collective-permute-start.19 = (bf16[2048,128]{1,0:T(8,128)(2,1)S(1)}, bf16[2048,128]{1,0:T(8,128)(2,1)S(1)}, u32[]{:S(2)}, u32[]{:S(2)}) collective-permute-start(bf16[2048,128]{1,0:T(8,128)(2,1)S(1)} %slice.71.refs_0_), channel_id=1, source_target_pairs={{0,6},{1,7},{2,0},{3,1},{4,2},{5,3},{6,4},{7,5},{8,14},{9,15},{10,... | collective-permute-start | bytes 1572872 | tf_op jit(solution)/shard_map/ppermute | solution.py:18
  26.5 2.9 %collective-permute-done.4 = bf16[1024,128]{1,0:T(8,128)(2,1)S(1)} collective-permute-done((bf16[1024,128]{1,0:T(8,128)(2,1)S(1)}, bf16[1024,128]{1,0:T(8,128)(2,1)S(1)}, u32[]{:S(2)}, u32[]{:S(2)}) %collective-permute-start.4) | collective-permute-done | bytes 262176 | tf_op jit(solution)/shard_map/ppermute | solution.py:18
  34.8 6.6 %collective-permute-done.19.refs_0_.refs_4_ = bf16[2048,128]{1,0:T(8,128)(2,1)S(1)} collective-permute-done((bf16[2048,128]{1,0:T(8,128)(2,1)S(1)}, bf16[2048,128]{1,0:T(8,128)(2,1)S(1)}, u32[]{:S(2)}, u32[]{:S(2)}) %collective-permute-start.19) | collective-permute-done | bytes 524320 | tf_op jit(solution)/shard_map/ppermute | solution.py:18
  45.7 6.2 %collective-permute-done.1 = bf16[2048,128]{1,0:T(8,128)(2,1)S(1)} collective-permute-done((bf16[2048,128]{1,0:T(8,128)(2,1)S(1)}, bf16[2048,128]{1,0:T(8,128)(2,1)S(1)}, u32[]{:S(2)}, u32[]{:S(2)}) %collective-permute-start.1) | collective-permute-done | bytes 524320 | tf_op jit(solution)/shard_map/ppermute | solution.py:18
  61.7 8.7 %collective-permute-done.25.refs_0_ = bf16[2048,128]{1,0:T(8,128)(2,1)S(1)} collective-permute-done((bf16[2048,128]{1,0:T(8,128)(2,1)S(1)}, bf16[2048,128]{1,0:T(8,128)(2,1)S(1)}, u32[]{:S(2)}, u32[]{:S(2)}) %collective-permute-start.25) | collective-permute-done | bytes 524320 | tf_op jit(solution)/shard_map/ppermute | solution.py:18
  73.5 2.6 %collective-permute-done.30 = bf16[128,768]{1,0:T(8,128)(2,1)S(1)} collective-permute-done((bf16[128,768]{1,0:T(8,128)(2,1)S(1)}, bf16[128,768]{1,0:T(8,128)(2,1)S(1)}, u32[]{:S(2)}, u32[]{:S(2)}) %collective-permute-start.30) | collective-permute-done | bytes 196640 | tf_op jit(solution)/shard_map/ppermute | solution.py:26
  77.6 3.1 %collective-permute-done.35 = bf16[128,384]{1,0:T(8,128)(2,1)S(1)} collective-permute-done((bf16[128,384]{1,0:T(8,128)(2,1)S(1)}, bf16[128,384]{1,0:T(8,128)(2,1)S(1)}, u32[]{:S(2)}, u32[]{:S(2)}) %collective-permute-start.35) | collective-permute-done | bytes 98336 | tf_op jit(solution)/shard_map/ppermute | solution.py:26
  82.2 4.1 %collective-permute-done.33 = bf16[128,384]{1,0:T(8,128)(2,1)S(1)} collective-permute-done((bf16[128,384]{1,0:T(8,128)(2,1)S(1)}, bf16[128,384]{1,0:T(8,128)(2,1)S(1)}, u32[]{:S(2)}, u32[]{:S(2)}) %collective-permute-start.33) | collective-permute-done | bytes 98336 | tf_op jit(solution)/shard_map/ppermute | solution.py:26
  87.9 4.8 %collective-permute-done.31 = bf16[128,768]{1,0:T(8,128)(2,1)S(1)} collective-permute-done((bf16[128,768]{1,0:T(8,128)(2,1)S(1)}, bf16[128,768]{1,0:T(8,128)(2,1)S(1)}, u32[]{:S(2)}, u32[]{:S(2)}) %collective-permute-start.31) | collective-permute-done | bytes 196640 | tf_op jit(solution)/shard_map/ppermute | solution.py:26
  92.8 2.3 %collective-permute-start.37 = (bf16[128,256]{1,0:T(8,128)(2,1)S(1)}, bf16[128,256]{1,0:T(8,128)(2,1)S(1)}, u32[]{:S(2)}, u32[]{:S(2)}) collective-permute-start(bf16[128,256]{1,0:T(8,128)(2,1)S(1)} %slice.103), channel_id=1, source_target_pairs={{0,2},{1,3},{2,4},{3,5},{4,6},{5,7},{6,0},{7,1},{8,10},{9,11},{10,... | collective-permute-start | bytes 196616 | tf_op jit(solution)/shard_map/ppermute | solution.py:18
  95.1 2.0 %collective-permute-start.15 = (f32[128,256]{1,0:T(8,128)S(1)}, f32[128,256]{1,0:T(8,128)S(1)}, u32[]{:S(2)}, u32[]{:S(2)}) collective-permute-start(f32[128,256]{1,0:T(8,128)S(1)} %slice_add_fusion.3), channel_id=1, source_target_pairs={{0,16},{8,24},{16,0},{24,8},{1,17},{9,25},{17,1},{25,9},{2,18},{10... | collective-permute-start | bytes 393224 | tf_op jit(solution)/shard_map/ppermute | solution.py:26
  98.4 1.9 %collective-permute-start.12 = (f32[128,256]{1,0:T(8,128)S(1)}, f32[128,256]{1,0:T(8,128)S(1)}, u32[]{:S(2)}, u32[]{:S(2)}) collective-permute-start(f32[128,256]{1,0:T(8,128)S(1)} %slice_add_fusion.4), channel_id=1, source_target_pairs={{0,8},{8,0},{16,24},{24,16},{1,9},{9,1},{17,25},{25,17},{2,10},{10... | collective-permute-start | bytes 393224 | tf_op jit(solution)/shard_map/ppermute | solution.py:26
  103.4 3.3 %collective-permute-done.23.refs_16_ = f32[128,512]{1,0:T(8,128)S(1)} collective-permute-done((f32[128,512]{1,0:T(8,128)S(1)}, f32[128,512]{1,0:T(8,128)S(1)}, u32[]{:S(2)}, u32[]{:S(2)}) %collective-permute-start.23) | collective-permute-done | bytes 262176 | tf_op jit(solution)/shard_map/ppermute | solution.py:26
  114.1 9.6 %inverse.1 = (bf16[1024,1024]{1,0:T(8,128)(2,1)S(1)}, bf16[1024,1024]{1,0:T(8,128)(2,1)S(1)}, f32[8,128]{1,0:T(8,128)S(1)}) custom-call(bf16[128,768]{1,0:T(8,128)(2,1)S(1)} %add_convert_fusion.refs_0_, bf16[128,768]{1,0:T(8,128)(2,1)S(1)} %pad_maximum_fusion.2.refs_1_, bf16[128,1024]{1,0:T(8,128)(2,1)S(1)} %pad_maximum_fusion.1.refs_2_, ...), custom_call_target="tpu_custom_call" | custom-call | flops 12884901888 | bytes 8388608 | tf_op jit(solution)/shard_map/inverse/pallas_call | solution.py:232
  123.8 5.2 %collective-permute-done.29.refs_21_ = f32[256,256]{1,0:T(8,128)S(1)} collective-permute-done((f32[256,256]{1,0:T(8,128)S(1)}, f32[256,256]{1,0:T(8,128)S(1)}, u32[]{:S(2)}, u32[]{:S(2)}) %collective-permute-start.29) | collective-permute-done | bytes 262176 | tf_op jit(solution)/shard_map/ppermute | solution.py:26
  129.0 2.1 %solve_rows.1.rest_0_ = bf16[1024,256]{1,0:T(8,128)(2,1)S(1)} custom-call(f32[128,512]{1,0:T(8,128)S(1)} %get-tuple-element.24.refs_0_, f32[128,512]{1,0:T(8,128)S(1)} %collective-permute-done.8.refs_1_, f32[128,256]{1,0:T(8,128)S(1)} %collective-permute-done.9.refs_2_, f32[128,512]{1,0:T(8,128)S(1)} %get-tuple-element.26.refs_3_, ...), custom_call_target="tpu_custom_call" | custom-call | flops 1610612736 | bytes 4194304 | tf_op jit(solution)/shard_map/solve_rows/pallas_call | solution.py:275
  135.6 8.8 %collective-permute-done.41.rest_1_ = bf16[512,256]{1,0:T(8,128)(2,1)S(1)} collective-permute-done((bf16[512,256]{1,0:T(8,128)(2,1)S(1)}, bf16[512,256]{1,0:T(8,128)(2,1)S(1)}, u32[]{:S(2)}, u32[]{:S(2)}) %collective-permute-start.41) | collective-permute-done | bytes 262176 | tf_op jit(solution)/shard_map/ppermute | solution.py:26
  146.6 4.9 %update.2.rest_2_ = bf16[2048,1024]{1,0:T(8,128)(2,1)} custom-call(s32[1]{0:T(128)} %bitcast.index_ref, bf16[2048,1024]{1,0:T(8,128)(2,1)S(1)} %copy-done.5, bf16[2048,1024]{1,0:T(8,128)(2,1)S(1)} %copy-done.3, bf16[2048,1024]{1,0:T(8,128)(2,1)S(1)} %constant_dynamic-update-slice_fusion.pruned_ref, bf16[1024,256]{1,0:T(8,128)(2,1)S(1)} %solve_rows.1.rest_0_, ...), custom_call_target="tpu_custom_call" | custom-call | flops 3221225472 | bytes 9437184 | tf_op jit(solution)/shard_map/update/pallas_call | solution.py:361
  152.3 2.2 %update.3 = bf16[2048,1024]{1,0:T(8,128)(2,1)} custom-call(s32[1]{0:T(128)} %bitcast.index_ref, bf16[2048,1024]{1,0:T(8,128)(2,1)S(1)} %copy-done.5, bf16[2048,1024]{1,0:T(8,128)(2,1)S(1)} %copy-done.3, bf16[2048,1024]{1,0:T(8,128)(2,1)S(1)} %constant_dynamic-update-slice_fusion.pruned_ref, ...), custom_call_target="tpu_custom_call", output_to_operand_aliasing={{}: (6, {})} | custom-call | flops 1073741824 | bytes 3145728 | tf_op jit(solution)/shard_map/update/pallas_call | solution.py:361
  (128 shorter events, 53.9 us)
Async XLA Ops:
  1.1 29.1 %collective-permute-start.13 = (bf16[2048,128]{1,0:T(8,128)(2,1)S(1)}, bf16[2048,128]{1,0:T(8,128)(2,1)S(1)}, u32[]{:S(2)}, u32[]{:S(2)}) collective-permute-start(bf16[2048,128]{1,0:T(8,128)(2,1)S(1)} %slice.71.refs_0_), channel_id=1, source_target_pairs={{0,2},{1,3},{2,4},{3,5},{4,6},{5,7},{6,0},{7,1},{8,10},{9,11},{10,... | collective-permute-start | bytes 1572872 | tf_op jit(solution)/shard_map/ppermute | solution.py:18
  4.2 28.3 %collective-permute-start.10 = (bf16[2048,128]{1,0:T(8,128)(2,1)S(1)}, bf16[2048,128]{1,0:T(8,128)(2,1)S(1)}, u32[]{:S(2)}, u32[]{:S(2)}) collective-permute-start(bf16[2048,128]{1,0:T(8,128)(2,1)S(1)} %slice.71.refs_0_), channel_id=1, source_target_pairs={{0,1},{1,0},{2,3},{3,2},{4,5},{5,4},{6,7},{7,6},{8,9},{9,8},{10,11... | collective-permute-start | bytes 1572872 | tf_op jit(solution)/shard_map/ppermute | solution.py:22
  10.1 13.7 %collective-permute-start.3 = (bf16[1024,128]{1,0:T(8,128)(2,1)S(1)}, bf16[1024,128]{1,0:T(8,128)(2,1)S(1)}, u32[]{:S(2)}, u32[]{:S(2)}) collective-permute-start(bf16[1024,128]{1,0:T(8,128)(2,1)S(1)} %get-tuple-element.46), channel_id=1, source_target_pairs={{0,6},{1,7},{2,0},{3,1},{4,2},{5,3},{6,4},{7,5},{8,14},{9,15},{10,... | collective-permute-start | bytes 786440 | tf_op jit(solution)/shard_map/ppermute | solution.py:18
  12.8 16.6 %collective-permute-start.4 = (bf16[1024,128]{1,0:T(8,128)(2,1)S(1)}, bf16[1024,128]{1,0:T(8,128)(2,1)S(1)}, u32[]{:S(2)}, u32[]{:S(2)}) collective-permute-start(bf16[1024,128]{1,0:T(8,128)(2,1)S(1)} %get-tuple-element.45), channel_id=1, source_target_pairs={{0,6},{1,7},{2,0},{3,1},{4,2},{5,3},{6,4},{7,5},{8,14},{9,15},{10,... | collective-permute-start | bytes 786440 | tf_op jit(solution)/shard_map/ppermute | solution.py:18
  17.2 12.3 %collective-permute-start.8 = (f32[128,512]{1,0:T(8,128)S(1)}, f32[128,512]{1,0:T(8,128)S(1)}, u32[]{:S(2)}, u32[]{:S(2)}) collective-permute-start(f32[128,512]{1,0:T(8,128)S(1)} %get-tuple-element.25), channel_id=1, source_target_pairs={{0,8},{8,0},{16,24},{24,16},{1,9},{9,1},{17,25},{25,17},{2,10},{10... | collective-permute-start | bytes 786440 | tf_op jit(solution)/shard_map/ppermute | solution.py:26
  23.8 17.6 %collective-permute-start.19 = (bf16[2048,128]{1,0:T(8,128)(2,1)S(1)}, bf16[2048,128]{1,0:T(8,128)(2,1)S(1)}, u32[]{:S(2)}, u32[]{:S(2)}) collective-permute-start(bf16[2048,128]{1,0:T(8,128)(2,1)S(1)} %slice.71.refs_0_), channel_id=1, source_target_pairs={{0,6},{1,7},{2,0},{3,1},{4,2},{5,3},{6,4},{7,5},{8,14},{9,15},{10,... | collective-permute-start | bytes 1572872 | tf_op jit(solution)/shard_map/ppermute | solution.py:18
  29.4 14.5 %collective-permute-start = (bf16[2048,128]{1,0:T(8,128)(2,1)S(1)}, bf16[2048,128]{1,0:T(8,128)(2,1)S(1)}, u32[]{:S(2)}, u32[]{:S(2)}) collective-permute-start(bf16[2048,128]{1,0:T(8,128)(2,1)S(1)} %pruned_columns.1), channel_id=1, source_target_pairs={{0,1},{1,0},{2,3},{3,2},{4,5},{5,4},{6,7},{7,6},{8,9},{9,8},{10,11... | collective-permute-start | bytes 1572872 | tf_op jit(solution)/shard_map/ppermute | solution.py:22
  29.5 22.4 %collective-permute-start.1 = (bf16[2048,128]{1,0:T(8,128)(2,1)S(1)}, bf16[2048,128]{1,0:T(8,128)(2,1)S(1)}, u32[]{:S(2)}, u32[]{:S(2)}) collective-permute-start(bf16[2048,128]{1,0:T(8,128)(2,1)S(1)} %pruned_columns.1), channel_id=1, source_target_pairs={{0,2},{1,3},{2,4},{3,5},{4,6},{5,7},{6,0},{7,1},{8,10},{9,11},{10,... | collective-permute-start | bytes 1572872 | tf_op jit(solution)/shard_map/ppermute | solution.py:18
  30.1 64.9 %collective-permute-start.9 = (f32[128,256]{1,0:T(8,128)S(1)}, f32[128,256]{1,0:T(8,128)S(1)}, u32[]{:S(2)}, u32[]{:S(2)}) collective-permute-start(f32[128,256]{1,0:T(8,128)S(1)} %slice_add_fusion.5), channel_id=1, source_target_pairs={{0,16},{8,24},{16,0},{24,8},{1,17},{9,25},{17,1},{25,9},{2,18},{10... | collective-permute-start | bytes 393224 | tf_op jit(solution)/shard_map/ppermute | solution.py:26
  32.5 19.6 %collective-permute-start.14 = (f32[128,512]{1,0:T(8,128)S(1)}, f32[128,512]{1,0:T(8,128)S(1)}, u32[]{:S(2)}, u32[]{:S(2)}) collective-permute-start(f32[128,512]{1,0:T(8,128)S(1)} %get-tuple-element.29), channel_id=1, source_target_pairs={{0,8},{8,0},{16,24},{24,16},{1,9},{9,1},{17,25},{25,17},{2,10},{10... | collective-permute-start | bytes 786440 | tf_op jit(solution)/shard_map/ppermute | solution.py:26
  53.8 16.6 %collective-permute-start.25 = (bf16[2048,128]{1,0:T(8,128)(2,1)S(1)}, bf16[2048,128]{1,0:T(8,128)(2,1)S(1)}, u32[]{:S(2)}, u32[]{:S(2)}) collective-permute-start(bf16[2048,128]{1,0:T(8,128)(2,1)S(1)} %collective-permute-done.13.refs_0_.refs_2_), channel_id=1, source_target_pairs={{0,2},{1,3},{2,4},{3,5},{4,6},{5,7},{6,0},{7,1},{8,10},{9,11},{10,... | collective-permute-start | bytes 1572872 | tf_op jit(solution)/shard_map/ppermute | solution.py:18
  54.6 54.7 %collective-permute-start.6 = (bf16[2048,128]{1,0:T(8,128)(2,1)S(1)}, bf16[2048,128]{1,0:T(8,128)(2,1)S(1)}, u32[]{:S(2)}, u32[]{:S(2)}) collective-permute-start(bf16[2048,128]{1,0:T(8,128)(2,1)S(1)} %collective-permute-done.1), channel_id=1, source_target_pairs={{0,2},{1,3},{2,4},{3,5},{4,6},{5,7},{6,0},{7,1},{8,10},{9,11},{10,... | collective-permute-start | bytes 1572872 | tf_op jit(solution)/shard_map/ppermute | solution.py:18
  55.8 16.1 %collective-permute-start.32 = (bf16[128,384]{1,0:T(8,128)(2,1)S(1)}, bf16[128,384]{1,0:T(8,128)(2,1)S(1)}, u32[]{:S(2)}, u32[]{:S(2)}) collective-permute-start(bf16[128,384]{1,0:T(8,128)(2,1)S(1)} %get-tuple-element.52), channel_id=1, source_target_pairs={{0,8},{8,0},{16,24},{24,16},{1,9},{9,1},{17,25},{25,17},{2,10},{10... | collective-permute-start | bytes 294920 | tf_op jit(solution)/shard_map/ppermute | solution.py:26
  58.3 15.1 %collective-permute-start.34 = (bf16[128,384]{1,0:T(8,128)(2,1)S(1)}, bf16[128,384]{1,0:T(8,128)(2,1)S(1)}, u32[]{:S(2)}, u32[]{:S(2)}) collective-permute-start(bf16[128,384]{1,0:T(8,128)(2,1)S(1)} %get-tuple-element.53), channel_id=1, source_target_pairs={{0,16},{8,24},{16,0},{24,8},{1,17},{9,25},{17,1},{25,9},{2,18},{10... | collective-permute-start | bytes 294920 | tf_op jit(solution)/shard_map/ppermute | solution.py:26
  71.9 20.9 %collective-permute-start.17 = (f32[128,512]{1,0:T(8,128)S(1)}, f32[128,512]{1,0:T(8,128)S(1)}, u32[]{:S(2)}, u32[]{:S(2)}) collective-permute-start(f32[128,512]{1,0:T(8,128)S(1)} %get-tuple-element.31), channel_id=1, source_target_pairs={{0,16},{8,24},{16,0},{24,8},{1,17},{9,25},{17,1},{25,9},{2,18},{10... | collective-permute-start | bytes 786440 | tf_op jit(solution)/shard_map/ppermute | solution.py:26
  73.4 33.2 %collective-permute-start.26 = (bf16[2048,128]{1,0:T(8,128)(2,1)S(1)}, bf16[2048,128]{1,0:T(8,128)(2,1)S(1)}, u32[]{:S(2)}, u32[]{:S(2)}) collective-permute-start(bf16[2048,128]{1,0:T(8,128)(2,1)S(1)} %collective-permute-done.25.refs_0_), channel_id=1, source_target_pairs={{0,1},{1,0},{2,3},{3,2},{4,5},{5,4},{6,7},{7,6},{8,9},{9,8},{10,11... | collective-permute-start | bytes 1572872 | tf_op jit(solution)/shard_map/ppermute | solution.py:22
  108.5 15.2 %collective-permute-start.18 = (f32[128,256]{1,0:T(8,128)S(1)}, f32[128,256]{1,0:T(8,128)S(1)}, u32[]{:S(2)}, u32[]{:S(2)}) collective-permute-start(f32[128,256]{1,0:T(8,128)S(1)} %slice_add_fusion.2), channel_id=1, source_target_pairs={{0,8},{8,0},{16,24},{24,16},{1,9},{9,1},{17,25},{25,17},{2,10},{10... | collective-permute-start | bytes 393224 | tf_op jit(solution)/shard_map/ppermute | solution.py:26
  109.2 14.5 %collective-permute-start.24 = (f32[128,256]{1,0:T(8,128)S(1)}, f32[128,256]{1,0:T(8,128)S(1)}, u32[]{:S(2)}, u32[]{:S(2)}) collective-permute-start(f32[128,256]{1,0:T(8,128)S(1)} %slice_add_fusion), channel_id=1, source_target_pairs={{0,8},{8,0},{16,24},{24,16},{1,9},{9,1},{17,25},{25,17},{2,10},{10... | collective-permute-start | bytes 393224 | tf_op jit(solution)/shard_map/ppermute | solution.py:26
  110.6 13.2 %collective-permute-start.27 = (f32[256,256]{1,0:T(8,128)S(1)}, f32[256,256]{1,0:T(8,128)S(1)}, u32[]{:S(2)}, u32[]{:S(2)}) collective-permute-start(f32[256,256]{1,0:T(8,128)S(1)} %get-tuple-element.37), channel_id=1, source_target_pairs={{0,8},{8,0},{16,24},{24,16},{1,9},{9,1},{17,25},{25,17},{2,10},{10... | collective-permute-start | bytes 786440 | tf_op jit(solution)/shard_map/ppermute | solution.py:26
  111.3 12.5 %collective-permute-start.28 = (f32[256,256]{1,0:T(8,128)S(1)}, f32[256,256]{1,0:T(8,128)S(1)}, u32[]{:S(2)}, u32[]{:S(2)}) collective-permute-start(f32[256,256]{1,0:T(8,128)S(1)} %get-tuple-element.38), channel_id=1, source_target_pairs={{0,16},{8,24},{16,0},{24,8},{1,17},{9,25},{17,1},{25,9},{2,18},{10... | collective-permute-start | bytes 786440 | tf_op jit(solution)/shard_map/ppermute | solution.py:26
  112.8 16.2 %collective-permute-start.29 = (f32[256,256]{1,0:T(8,128)S(1)}, f32[256,256]{1,0:T(8,128)S(1)}, u32[]{:S(2)}, u32[]{:S(2)}) collective-permute-start(f32[256,256]{1,0:T(8,128)S(1)} %get-tuple-element.39), channel_id=1, source_target_pairs={{0,24},{8,16},{16,8},{24,0},{1,25},{9,17},{17,9},{25,1},{2,26},{10... | collective-permute-start | bytes 786440 | tf_op jit(solution)/shard_map/ppermute | solution.py:26
  131.1 14.8 %collective-permute-start.43 = (bf16[512,256]{1,0:T(8,128)(2,1)S(1)}, bf16[512,256]{1,0:T(8,128)(2,1)S(1)}, u32[]{:S(2)}, u32[]{:S(2)}) collective-permute-start(bf16[512,256]{1,0:T(8,128)(2,1)S(1)} %get-tuple-element.43), channel_id=1, source_target_pairs={{0,16},{8,24},{16,0},{24,8},{1,17},{9,25},{17,1},{25,9},{2,18},{10... | collective-permute-start | bytes 786440 | tf_op jit(solution)/shard_map/ppermute | solution.py:26
  131.7 14.9 %collective-permute-start.45 = (bf16[512,256]{1,0:T(8,128)(2,1)S(1)}, bf16[512,256]{1,0:T(8,128)(2,1)S(1)}, u32[]{:S(2)}, u32[]{:S(2)}) collective-permute-start(bf16[512,256]{1,0:T(8,128)(2,1)S(1)} %get-tuple-element.43), channel_id=1, source_target_pairs={{0,8},{8,0},{16,24},{24,16},{1,9},{9,1},{17,25},{25,17},{2,10},{10... | collective-permute-start | bytes 786440 | tf_op jit(solution)/shard_map/ppermute | solution.py:26
  133.7 12.9 %collective-permute-start.46 = (bf16[512,256]{1,0:T(8,128)(2,1)S(1)}, bf16[512,256]{1,0:T(8,128)(2,1)S(1)}, u32[]{:S(2)}, u32[]{:S(2)}) collective-permute-start(bf16[512,256]{1,0:T(8,128)(2,1)S(1)} %get-tuple-element.44), channel_id=1, source_target_pairs={{0,16},{8,24},{16,0},{24,8},{1,17},{9,25},{17,1},{25,9},{2,18},{10... | collective-permute-start | bytes 786440 | tf_op jit(solution)/shard_map/ppermute | solution.py:26
  (30 other events, 213.8 us)
